TPU v7x, 256 devices: a whole 4x4x8 slice. The times are simulated.
256 devices in a mesh: cfg: 2 (over core), tm: 128 (over y, z, x).
Axes of the slice: x: 4, y: 4, z: 8, core: 2. Of those that a mesh axis runs over, the one named last changes fastest.
Arguments:
- queries: bfloat16 [2, 98304, 1152], P('cfg', 'tm'), may hold values from -6 to 6
- key_vectors: bfloat16 [2, 98304, 1152], P('cfg', 'tm'), may hold values from -12 to 12
- value_vectors: bfloat16 [2, 98304, 1152], P('cfg', 'tm'), may hold values from -4 to 4
- out_weight: bfloat16 [1152, 2240], replicated, may hold values from -0.1875 to 0.1875
- first_frame: int32 [256], P('tm'), may hold values from 0 to 255, as said below
Outputs:
- guided: bfloat16 [98304, 2240], P('tm', 'cfg')
Inputs may be any that keep to these rules, and one draw needn't show every extreme that they name: first_frame[f] is 0 or lies between f - 4 and f; some frame f has first_frame[f] = f - 4.
All inputs are finite; a program needn't handle non-finite values.
Results may differ from a plain program's by a relative error of at most 0.014.
Values may be sent and summed in bfloat16 or wider, within the bound.
No kernel may reach another device: no remote copies, remote signals or barrier semaphores. Data moves between devices by JAX's collectives and lax.ppermute only.
A program may use at most 192 MiB of HBM per device.

v0:
```python
import jax
import jax.numpy as jnp
from jax import lax
from jax.sharding import Mesh
from jax.sharding import PartitionSpec as P

H = 36
DH = 32
FR = 2
NEAR = 2
FT = 384
TM = ("tm_0", "tm_1", "tm_2")


guide_scale = 4.5
epsilon = 1e-06


def shifted(value, axis, steps):
    count = lax.axis_size(axis)
    initial, last = (max(0, -steps), min(count, count - steps))
    return lax.ppermute(value, axis, [(source, source + steps) for source in range(initial, last)])


def filled_with(x, identity):
    return jax.tree.map(
        lambda a, e: jnp.broadcast_to(jnp.asarray(e, a.dtype), a.shape), x, identity
    )


def carried_in(x, axes, combine, identity):
    before = start = filled_with(x, identity)
    running = x
    for axis in reversed(axes):
        devices, index = (lax.axis_size(axis), lax.axis_index(axis))
        pieces = jax.tree.map(
            lambda part, kind: lax.all_gather(part.astype(kind), axis),
            running,
            (jnp.bfloat16, jnp.bfloat16),
        )
        inside, running = (start, start)
        for k in range(devices):
            passed = k < index
            running = combine(
                running, jax.tree.map(lambda part, own: part[k].astype(own.dtype), pieces, x)
            )
            inside = jax.tree.map(lambda new, old: jnp.where(passed, new, old), running, inside)
        before = combine(inside, before)
    return before


def from_partner(value, axis, bit):
    mask = 2**bit
    pairs = [(source, source ^ mask) for source in range(lax.axis_size(axis))]
    return lax.ppermute(value, axis, pairs)


def add_pair(earlier, later):
    return (earlier[0] + later[0], earlier[1] + later[1])


def split_parts(values):
    upper = values.astype(jnp.bfloat16)
    lower = (values - upper.astype(jnp.float32)).astype(jnp.bfloat16)
    return jnp.concatenate([upper, lower], axis=-1)


def on_device(queries, key_vectors, value_vectors, out_weight, first_frame):
    rows_here = queries.shape[1]
    feature_width = queries.shape[2]
    query_frames = queries.reshape(FR, FT, H, DH)
    key_frames = jnp.maximum(key_vectors.reshape(FR, FT, H, DH), 0)
    value_frames = value_vectors.reshape(FR, FT, H, DH)
    frame_states = jnp.einsum(
        "fthd,fthe->fhde", key_frames, value_frames, preferred_element_type=jnp.float32
    )
    frame_sums = jnp.sum(key_frames, axis=1, dtype=jnp.float32)
    device_index = lax.axis_index(TM)
    local_ids = jnp.arange(FR, dtype=jnp.int32)
    own_frames = device_index * FR + local_ids
    source_states = [frame_states]
    source_sums = [frame_sums]
    source_frames = [own_frames]
    for offset in range(1, NEAR + 1):
        moved_states, moved_sums = (
            shifted(frame_states.astype(jnp.bfloat16), TM, offset).astype(frame_states.dtype),
            shifted(frame_sums.astype(jnp.bfloat16), TM, offset).astype(frame_sums.dtype),
        )
        source_states.append(moved_states)
        source_sums.append(moved_sums)
        source_frames.append((device_index - offset) * FR + local_ids)
    empty_states = jnp.zeros((H, DH, DH), jnp.float32)
    empty_sums = jnp.zeros((H, DH), jnp.float32)
    prefix_states, prefix_sums = carried_in(
        (jnp.sum(frame_states, axis=0), jnp.sum(frame_sums, axis=0)),
        TM,
        add_pair,
        (empty_states, empty_sums),
    )
    neighbour_states = jnp.sum(jnp.concatenate(source_states[1:], axis=0), axis=0)
    neighbour_sums = jnp.sum(jnp.concatenate(source_sums[1:], axis=0), axis=0)
    earlier_states = prefix_states - neighbour_states
    earlier_sums = prefix_sums - neighbour_sums
    all_states = jnp.concatenate(source_states + [earlier_states[None]], axis=0)
    all_sums = jnp.concatenate(source_sums + [earlier_sums[None]], axis=0)
    all_frames = jnp.concatenate(source_frames, axis=0)
    inside = (first_frame[:, None] <= all_frames[None, :]) & (
        all_frames[None, :] <= own_frames[:, None]
    )
    whole_prefix = (first_frame == 0)[:, None]
    mixing = jnp.concatenate([inside, whole_prefix], axis=1).astype(jnp.float32)
    attended_states = jnp.einsum("is,shde->ihde", mixing, all_states)
    attended_sums = jnp.einsum("is,shd->ihd", mixing, all_sums)
    query_feats = jnp.maximum(query_frames, 0)
    state_parts = split_parts(attended_states)
    sum_parts = split_parts(attended_sums[..., None])
    numerator_parts = jnp.einsum(
        "ithd,ihde->ithe", query_feats, state_parts, preferred_element_type=jnp.float32
    )
    numerator = numerator_parts[..., :DH] + numerator_parts[..., DH:]
    denominator_parts = jnp.einsum(
        "ithd,ihde->ithe", query_feats, sum_parts, preferred_element_type=jnp.float32
    )
    denominator = denominator_parts[..., 0] + denominator_parts[..., 1] + epsilon
    attended = (
        (numerator / denominator[..., None]).astype(jnp.bfloat16).reshape(rows_here, feature_width)
    )
    half_width = out_weight.shape[1] // 2
    partner = from_partner(attended, "cfg", 0)
    branch_index = lax.axis_index("cfg")
    is_cond = branch_index == 0
    cond_rows = jnp.where(is_cond, attended, partner)
    uncond_rows = jnp.where(is_cond, partner, attended)
    columns = lax.dynamic_slice_in_dim(out_weight, branch_index * half_width, half_width, 1)
    cond_part = jnp.dot(cond_rows, columns, preferred_element_type=jnp.float32)
    uncond_part = jnp.dot(uncond_rows, columns, preferred_element_type=jnp.float32)
    return (uncond_part + guide_scale * (cond_part - uncond_part)).astype(jnp.bfloat16)


def solution(mesh):
    torus = Mesh(mesh.devices.reshape(mesh.shape["cfg"], 4, 8, 4), ("cfg", "tm_0", "tm_1", "tm_2"))
    in_specs = (P("cfg", TM, None), P("cfg", TM, None), P("cfg", TM, None), P(), P(TM))
    out_specs = P(TM, "cfg")
    return jax.shard_map(
        on_device, mesh=torus, in_specs=in_specs, out_specs=out_specs, check_vma=False
    )
```

profile of v0, /device:TPU:1, one launch (start us, length us, event | category | flops | bytes accessed | tf_op | source)
XLA Modules:
  0.0 241.4 jit_solution(4729521157047469691)
XLA Ops:
  6.1 6.1 %collective-permute-start.3 = (bf16[2,36,32]{1,0,2:T(2,128)(2,1)}, bf16[2,36,32]{1,0,2:T(2,128)(2,1)}, u32[]{:S(2)}, u32[]{:S(2)}) collective-permute-start(bf16[2,36,32]{1,0,2:T(2,128)(2,1)} %copy.128), channel_id=1, source_target_pairs={{0,2},{1,3},{2,4},{3,5},{4,6},{5,7},{6,8},{7,9},{8,10},{9,11},{10,... | collective-permute-start | bytes 13832 | tf_op jit(solution)/shard_map/ppermute | solution.py:22
  12.1 2.8 %collective-permute-start.2 = (bf16[2,36,32]{1,0,2:T(2,128)(2,1)}, bf16[2,36,32]{1,0,2:T(2,128)(2,1)}, u32[]{:S(2)}, u32[]{:S(2)}) collective-permute-start(bf16[2,36,32]{1,0,2:T(2,128)(2,1)} %copy.128), channel_id=1, source_target_pairs={{0,1},{1,2},{2,3},{3,4},{4,5},{5,6},{6,7},{7,8},{8,9},{9,10},{10,1... | collective-permute-start | bytes 13832 | tf_op jit(solution)/shard_map/ppermute | solution.py:22
  14.9 2.6 %copy.84 = bf16[1,768,1152]{1,2,0:T(8,128)(2,1)S(1)} copy(bf16[1,768,1152]{2,1,0:T(8,128)(2,1)} %param.7) | data formatting | bytes 3538944 | tf_op args[2]
  23.3 4.6 %collective-permute-start.1 = (bf16[2,36,32,32]{1,3,2,0:T(8,128)(2,1)}, bf16[2,36,32,32]{1,3,2,0:T(8,128)(2,1)}, u32[]{:S(2)}, u32[]{:S(2)}) collective-permute-start(bf16[2,36,32,32]{1,3,2,0:T(8,128)(2,1)} %copy.87), channel_id=1, source_target_pairs={{0,2},{1,3},{2,4},{3,5},{4,6},{5,7},{6,8},{7,9},{8,10},{9,11},{10,... | collective-permute-start | bytes 442376 | tf_op jit(solution)/shard_map/ppermute | solution.py:22
  27.9 3.9 %collective-permute-start = (bf16[2,36,32,32]{1,3,2,0:T(8,128)(2,1)}, bf16[2,36,32,32]{1,3,2,0:T(8,128)(2,1)}, u32[]{:S(2)}, u32[]{:S(2)}) collective-permute-start(bf16[2,36,32,32]{1,3,2,0:T(8,128)(2,1)} %copy.87), channel_id=1, source_target_pairs={{0,1},{1,2},{2,3},{3,4},{4,5},{5,6},{6,7},{7,8},{8,9},{9,10},{10,1... | collective-permute-start | bytes 442376 | tf_op jit(solution)/shard_map/ppermute | solution.py:22
  32.0 24.3 %all_gather.30 = bf16[4,36,32]{1,2,0:T(8,128)(2,1)S(1)} all-gather(bf16[1,36,32]{1,2,0:T(8,128)(2,1)S(1)} %copy.109), channel_id=1, replica_groups=mesh['cfg'=2,'tm_0'=4,'tm_1'=8,'tm_2'=4] {'tm_2'}, dimensions={0}, use_global_device_ids=true | all-gather | bytes 11520 | tf_op jit(solution)/shard_map/all_gather | solution.py:37
  57.0 21.2 %all_gather.31 = bf16[8,36,32]{1,2,0:T(8,128)(2,1)S(1)} all-gather(bf16[1,36,32]{1,2,0:T(8,128)(2,1)S(1)} %copy.114), channel_id=1, replica_groups=mesh['cfg'=2,'tm_0'=4,'tm_1'=8,'tm_2'=4] {'tm_1'}, dimensions={0}, use_global_device_ids=true | all-gather | bytes 20736 | tf_op jit(solution)/shard_map/all_gather | solution.py:37
  78.9 9.5 %all_gather.32 = bf16[4,36,32]{1,2,0:T(8,128)(2,1)S(1)} all-gather(bf16[1,36,32]{1,2,0:T(8,128)(2,1)S(1)} %copy.123), channel_id=1, replica_groups=mesh['cfg'=2,'tm_0'=4,'tm_1'=8,'tm_2'=4] {'tm_0'}, dimensions={0}, use_global_device_ids=true | all-gather | bytes 11520 | tf_op jit(solution)/shard_map/all_gather | solution.py:37
  91.3 11.4 %all-gather = bf16[144,32,32]{2,1,0:T(8,128)(2,1)S(1)} all-gather(bf16[36,32,32]{2,1,0:T(8,128)(2,1)S(1)} %get-tuple-element.41), channel_id=2, replica_groups=mesh['cfg'=2,'tm_0'=4,'tm_1'=8,'tm_2'=4] {'tm_2'}, dimensions={0}, use_global_device_ids=true | all-gather | bytes 368640 | tf_op jit(solution)/shard_map/all_gather | solution.py:37
  103.3 23.9 %all_gather.27 = bf16[8,36,32,32]{1,3,2,0:T(8,128)(2,1)S(1)} all-gather(bf16[1,36,32,32]{1,3,2,0:T(8,128)(2,1)S(1)} %copy.90), channel_id=1, replica_groups=mesh['cfg'=2,'tm_0'=4,'tm_1'=8,'tm_2'=4] {'tm_1'}, dimensions={0}, use_global_device_ids=true | all-gather | bytes 663552 | tf_op jit(solution)/shard_map/all_gather | solution.py:37
  130.7 2.3 copy.137
  139.8 2.3 copy.141
  144.3 2.4 %fusion.39 = bf16[1,36,32,32]{3,2,1,0:T(8,128)(2,1)} fusion(bf16[1,36,32,32]{3,2,1,0:T(8,128)(2,1)} %copy.142, bf16[1,36,32,32]{3,2,1,0:T(8,128)(2,1)} %copy.141, bf16[1,36,32,32]{3,2,1,0:T(8,128)(2,1)} %copy.140, bf16[1,36,32,32]{3,2,1,0:T(8,128)(2,1)} %copy.139, bf16[1,36,32,32]{3,2,1,0:T(8,128)(2,1)} %copy.138, bf16[1,36,32,32]{3,2,1,0:T(8,128)(2,1)} %copy.137, ...), kind=kLoop, calls=%fused_computation.55 | loop fusion | flops 589824 | bytes 663552 | tf_op jit(solution)/shard_map/convert_element_type | solution.py:37
  148.1 11.1 %all_gather.28 = bf16[4,36,32,32]{1,3,2,0:T(8,128)(2,1)S(1)} all-gather(bf16[1,36,32,32]{1,3,2,0:T(8,128)(2,1)S(1)} %copy.99), channel_id=1, replica_groups=mesh['cfg'=2,'tm_0'=4,'tm_1'=8,'tm_2'=4] {'tm_0'}, dimensions={0}, use_global_device_ids=true | all-gather | bytes 368640 | tf_op jit(solution)/shard_map/all_gather | solution.py:37
  163.7 3.7 %max.20 = bf16[2,384,36,32]{1,0,3,2:T(2,128)(2,1)S(1)} reshape(bf16[1,768,1152]{1,2,0:T(8,128)(2,1)} %copy.105) | data formatting | bytes 3538944 | tf_op jit(solution)/shard_map/max | solution.py:114
  167.5 2.3 copy.143
  182.8 2.9 %copy.88 = bf16[2,36,32,32]{3,2,1,0:T(8,128)(2,1)} copy(bf16[2,36,32,32]{1,3,2,0:T(8,128)(2,1)} %collective-permute-done) | data formatting | bytes 294912 | tf_op jit(solution)/shard_map/ppermute | solution.py:22
  187.0 3.2 %fusion.30 = bf16[1,36,32,32]{3,2,1,0:T(8,128)(2,1)S(1)} fusion(bf16[1,36,32,32]{3,2,1,0:T(8,128)(2,1)} %copy-done.1, bf16[1,36,32,32]{3,2,1,0:T(8,128)(2,1)} %copy.143, f32[36,32,32]{2,1,0:T(8,128)S(1)} %convert_reduce_fusion.2, f32[36,32,32]{2,1,0:T(8,128)} %convert_reduce_fusion.1, bf16[1,36,32,32]{3,2,1,0:T(8,128)(2,1)} %copy.146, ...), kind=kLoop, calls=%fused_computation.43 | loop fusion | flops 1843200 | bytes 1548304 | tf_op jit(solution)/shard_map/sub | solution.py:102
  192.1 4.8 %copy.104 = bf16[7,36,32,32]{1,0,3,2:T(8,128)(2,1)} copy(bf16[7,36,32,32]{3,2,1,0:T(8,128)(2,1)} %pad_maximum_fusion) | data formatting | bytes 1032192 | tf_op jit(solution)/shard_map/concatenate | solution.py:104
  196.9 2.5 %subtract_convert_fusion = (bf16[2,36,32,32]{1,0,3,2:T(2,128)(2,1)S(1)}, bf16[2,36,32,32]{1,0,3,2:T(2,128)(2,1)S(1)}) fusion(bf16[7,36,32,32]{1,0,3,2:T(8,128)(2,1)} %copy.104, pred[2,1]{1,0:T(4,128)(4,1)S(1)} %copy-done.25, pred[2,6]{1,0:T(4,128)(4,1)S(1)} %copy-done.23), kind=kOutput, calls=%fused_computation.25 | convolution fusion | flops 1327118 | bytes 811022 | tf_op jit(solution)/shard_map/is,shde->ihde/dot_general | solution.py:112
  206.6 22.0 %collective-permute-start.4 = (bf16[768,1152]{0,1:T(8,128)(2,1)S(1)}, bf16[768,1152]{0,1:T(8,128)(2,1)S(1)}, u32[]{:S(2)}, u32[]{:S(2)}) collective-permute-start(bf16[768,1152]{0,1:T(8,128)(2,1)S(1)} %bitcast.49), channel_id=1, source_target_pairs={{0,128},{128,0},{1,129},{129,1},{2,130},{130,2},{3,131},{131,3},{4... | collective-permute-start | bytes 5308424 | tf_op jit(solution)/shard_map/ppermute | solution.py:55
  228.5 3.3 %collective-permute-done.4 = bf16[768,1152]{0,1:T(8,128)(2,1)S(1)} collective-permute-done((bf16[768,1152]{0,1:T(8,128)(2,1)S(1)}, bf16[768,1152]{0,1:T(8,128)(2,1)S(1)}, u32[]{:S(2)}, u32[]{:S(2)}) %collective-permute-start.4) | collective-permute-done | bytes 1769504 | tf_op jit(solution)/shard_map/ppermute | solution.py:55
  231.8 4.1 %fusion.5 = f32[768,1120]{0,1:T(8,128)S(1)} fusion(bf16[1152,2240]{0,1:T(8,128)(2,1)} %param.8, s32[]{:T(128)S(6)} %select_n.309, bf16[768,1152]{0,1:T(8,128)(2,1)S(1)} %collective-permute-done.4, bf16[768,1152]{0,1:T(8,128)(2,1)S(1)} %bitcast.50, pred[]{:T(512)S(6)} %eq.6), kind=kOutput, calls=%fused_computation.10 | convolution fusion | flops 1982693376 | bytes 9560069 | tf_op jit(solution)/shard_map/dot_general | solution.py:136
  236.0 5.4 %fusion.4 = bf16[768,1120]{0,1:T(8,128)(2,1)} fusion(f32[768,1120]{0,1:T(8,128)S(1)} %fusion.5, bf16[1152,2240]{0,1:T(8,128)(2,1)} %param.8, s32[]{:T(128)S(6)} %select_n.309, bf16[768,1152]{0,1:T(8,128)(2,1)S(1)} %bitcast.51, bf16[768,1152]{0,1:T(8,128)(2,1)S(1)} %collective-permute-done.4, pred[]{:T(512)S(6)} %eq.6), kind=kOutput, calls=%fused_computation.8 | convolution fusion | flops 1986134016 | bytes 11280389 | tf_op jit(solution)/shard_map/dot_general | solution.py:135
  (118 shorter events, 58.2 us)
Async XLA Ops:
  6.1 168.5 %collective-permute-start.3 = (bf16[2,36,32]{1,0,2:T(2,128)(2,1)}, bf16[2,36,32]{1,0,2:T(2,128)(2,1)}, u32[]{:S(2)}, u32[]{:S(2)}) collective-permute-start(bf16[2,36,32]{1,0,2:T(2,128)(2,1)} %copy.128), channel_id=1, source_target_pairs={{0,2},{1,3},{2,4},{3,5},{4,6},{5,7},{6,8},{7,9},{8,10},{9,11},{10,... | collective-permute-start | bytes 13832 | tf_op jit(solution)/shard_map/ppermute | solution.py:22
  12.1 163.2 %collective-permute-start.2 = (bf16[2,36,32]{1,0,2:T(2,128)(2,1)}, bf16[2,36,32]{1,0,2:T(2,128)(2,1)}, u32[]{:S(2)}, u32[]{:S(2)}) collective-permute-start(bf16[2,36,32]{1,0,2:T(2,128)(2,1)} %copy.128), channel_id=1, source_target_pairs={{0,1},{1,2},{2,3},{3,4},{4,5},{5,6},{6,7},{7,8},{8,9},{9,10},{10,1... | collective-permute-start | bytes 13832 | tf_op jit(solution)/shard_map/ppermute | solution.py:22
  21.7 67.3 %copy-start.3 = (bf16[2,36,32,32]{3,2,1,0:T(8,128)(2,1)}, bf16[2,36,32,32]{3,2,1,0:T(8,128)(2,1)S(1)}, u32[]{:S(2)}) copy-start(bf16[2,36,32,32]{3,2,1,0:T(8,128)(2,1)S(1)} %get-tuple-element.42) | copy-start | bytes 442372
  23.3 156.4 %collective-permute-start.1 = (bf16[2,36,32,32]{1,3,2,0:T(8,128)(2,1)}, bf16[2,36,32,32]{1,3,2,0:T(8,128)(2,1)}, u32[]{:S(2)}, u32[]{:S(2)}) collective-permute-start(bf16[2,36,32,32]{1,3,2,0:T(8,128)(2,1)} %copy.87), channel_id=1, source_target_pairs={{0,2},{1,3},{2,4},{3,5},{4,6},{5,7},{6,8},{7,9},{8,10},{9,11},{10,... | collective-permute-start | bytes 442376 | tf_op jit(solution)/shard_map/ppermute | solution.py:22
  27.9 154.9 %collective-permute-start = (bf16[2,36,32,32]{1,3,2,0:T(8,128)(2,1)}, bf16[2,36,32,32]{1,3,2,0:T(8,128)(2,1)}, u32[]{:S(2)}, u32[]{:S(2)}) collective-permute-start(bf16[2,36,32,32]{1,3,2,0:T(8,128)(2,1)} %copy.87), channel_id=1, source_target_pairs={{0,1},{1,2},{2,3},{3,4},{4,5},{5,6},{6,7},{7,8},{8,9},{9,10},{10,1... | collective-permute-start | bytes 442376 | tf_op jit(solution)/shard_map/ppermute | solution.py:22
  78.2 13.1 %copy-start.6 = (bf16[1,36,32]{1,2,0:T(8,128)(2,1)}, bf16[1,36,32]{1,2,0:T(8,128)(2,1)S(1)}, u32[]{:S(2)}) copy-start(bf16[1,36,32]{1,2,0:T(8,128)(2,1)S(1)} %get-tuple-element.25) | copy-start | bytes 6916
  78.2 13.1 %copy-start.8 = (bf16[1,36,32]{1,2,0:T(8,128)(2,1)}, bf16[1,36,32]{1,2,0:T(8,128)(2,1)S(1)}, u32[]{:S(2)}) copy-start(bf16[1,36,32]{1,2,0:T(8,128)(2,1)S(1)} %get-tuple-element.26) | copy-start | bytes 6916
  78.2 13.1 %copy-start.10 = (bf16[1,36,32]{1,2,0:T(8,128)(2,1)}, bf16[1,36,32]{1,2,0:T(8,128)(2,1)S(1)}, u32[]{:S(2)}) copy-start(bf16[1,36,32]{1,2,0:T(8,128)(2,1)S(1)} %get-tuple-element.27) | copy-start | bytes 6916
  78.2 13.1 %copy-start.12 = (bf16[1,36,32]{1,2,0:T(8,128)(2,1)}, bf16[1,36,32]{1,2,0:T(8,128)(2,1)S(1)}, u32[]{:S(2)}) copy-start(bf16[1,36,32]{1,2,0:T(8,128)(2,1)S(1)} %get-tuple-element.28) | copy-start | bytes 6916
  78.2 13.1 %copy-start.14 = (bf16[1,36,32]{1,2,0:T(8,128)(2,1)}, bf16[1,36,32]{1,2,0:T(8,128)(2,1)S(1)}, u32[]{:S(2)}) copy-start(bf16[1,36,32]{1,2,0:T(8,128)(2,1)S(1)} %get-tuple-element.29) | copy-start | bytes 6916
  129.1 15.2 %copy-start.1 = (bf16[1,36,32,32]{3,2,1,0:T(8,128)(2,1)}, bf16[1,36,32,32]{3,2,1,0:T(8,128)(2,1)S(1)}, u32[]{:S(2)}) copy-start(bf16[1,36,32,32]{3,2,1,0:T(8,128)(2,1)S(1)} %copy.135) | copy-start | bytes 221188
  130.7 16.0 %copy-start.2 = (bf16[1,36,32,32]{3,2,1,0:T(8,128)(2,1)}, bf16[1,36,32,32]{3,2,1,0:T(8,128)(2,1)S(1)}, u32[]{:S(2)}) copy-start(bf16[1,36,32,32]{3,2,1,0:T(8,128)(2,1)S(1)} %copy.136) | copy-start | bytes 221188
  148.1 12.1 %copy-start.24 = (s32[2]{0:T(128)S(1)}, s32[2]{0:T(128)}, u32[]{:S(2)}) copy-start(s32[2]{0:T(128)} %iota_add_fusion.2) | copy-start | bytes 28
  148.1 12.1 %copy-start.26 = (s32[2]{0:T(128)S(1)}, s32[2]{0:T(128)}, u32[]{:S(2)}) copy-start(s32[2]{0:T(128)} %param.9) | copy-start | bytes 28
  167.4 8.8 %copy-start.7 = (bf16[1,36,32]{1,2,0:T(8,128)(2,1)S(1)}, bf16[1,36,32]{1,2,0:T(8,128)(2,1)}, u32[]{:S(2)}) copy-start(bf16[1,36,32]{1,2,0:T(8,128)(2,1)} %copy-done.6) | copy-start | bytes 6916
  167.4 8.8 %copy-start.9 = (bf16[1,36,32]{1,2,0:T(8,128)(2,1)S(1)}, bf16[1,36,32]{1,2,0:T(8,128)(2,1)}, u32[]{:S(2)}) copy-start(bf16[1,36,32]{1,2,0:T(8,128)(2,1)} %copy-done.8) | copy-start | bytes 6916
  167.4 8.8 %copy-start.11 = (bf16[1,36,32]{1,2,0:T(8,128)(2,1)S(1)}, bf16[1,36,32]{1,2,0:T(8,128)(2,1)}, u32[]{:S(2)}) copy-start(bf16[1,36,32]{1,2,0:T(8,128)(2,1)} %copy-done.10) | copy-start | bytes 6916
  167.4 8.8 %copy-start.13 = (bf16[1,36,32]{1,2,0:T(8,128)(2,1)S(1)}, bf16[1,36,32]{1,2,0:T(8,128)(2,1)}, u32[]{:S(2)}) copy-start(bf16[1,36,32]{1,2,0:T(8,128)(2,1)} %copy-done.12) | copy-start | bytes 6916
  167.4 8.8 %copy-start.15 = (bf16[1,36,32]{1,2,0:T(8,128)(2,1)S(1)}, bf16[1,36,32]{1,2,0:T(8,128)(2,1)}, u32[]{:S(2)}) copy-start(bf16[1,36,32]{1,2,0:T(8,128)(2,1)} %copy-done.14) | copy-start | bytes 6916
  167.5 8.8 %copy-start.17 = (bf16[1,36,32]{1,2,0:T(8,128)(2,1)S(1)}, bf16[1,36,32]{1,2,0:T(8,128)(2,1)}, u32[]{:S(2)}) copy-start(bf16[1,36,32]{1,2,0:T(8,128)(2,1)} %copy-done.16) | copy-start | bytes 6916
  167.5 8.8 %copy-start.19 = (bf16[1,36,32]{1,2,0:T(8,128)(2,1)S(1)}, bf16[1,36,32]{1,2,0:T(8,128)(2,1)}, u32[]{:S(2)}) copy-start(bf16[1,36,32]{1,2,0:T(8,128)(2,1)} %copy-done.18) | copy-start | bytes 6916
  167.5 8.8 %copy-start.21 = (bf16[1,36,32]{1,2,0:T(8,128)(2,1)S(1)}, bf16[1,36,32]{1,2,0:T(8,128)(2,1)}, u32[]{:S(2)}) copy-start(bf16[1,36,32]{1,2,0:T(8,128)(2,1)} %copy-done.20) | copy-start | bytes 6916
  192.1 4.8 %copy-start.25 = (pred[2,1]{1,0:T(4,128)(4,1)S(1)}, pred[2,1]{1,0:T(4,128)(4,1)}, u32[]{:S(2)}) copy-start(pred[2,1]{1,0:T(4,128)(4,1)} %copy.82) | copy-start | bytes 10
  206.6 25.3 %collective-permute-start.4 = (bf16[768,1152]{0,1:T(8,128)(2,1)S(1)}, bf16[768,1152]{0,1:T(8,128)(2,1)S(1)}, u32[]{:S(2)}, u32[]{:S(2)}) collective-permute-start(bf16[768,1152]{0,1:T(8,128)(2,1)S(1)} %bitcast.49), channel_id=1, source_target_pairs={{0,128},{128,0},{1,129},{129,1},{2,130},{130,2},{3,131},{131,3},{4... | collective-permute-start | bytes 5308424 | tf_op jit(solution)/shard_map/ppermute | solution.py:55
  (8 other events, 14.8 us)
where the time goes:
time: 243 us; the launch traced here: 241 us
  blocking collectives  101 us (42%)
  local copies, waits for them, and re-layouts  57.5 us (24%)
  starting transfers between devices  39.4 us (16%)
  other arithmetic  22.4 us (9%)
  matrix products  16.8 us (7%)
  waiting for transfers between devices  3.33 us (1%)
    all_gather x6, blocking collectives, carried_in(): lax.all_gather(part.astype(kind), axis)  101 us
    unnamed x68, local copies, waits for them, and re-layouts  26.6 us
    ppermute x1, starting transfers between devices, from_partner(): return lax.ppermute(value, axis, pairs)  22 us
    ppermute x4, starting transfers between devices, shifted(): lax.ppermute(value, axis, [(source, source + steps) for source in range(i...  17.4 us
    max x2, local copies, waits for them, and re-layouts, on_device(): query_feats = jnp.maximum(query_frames, 0)  5.92 us
    dot_general x1, matrix products, on_device(): cond_part = jnp.dot(cond_rows, columns, preferred_element_type=jnp.float32)  5.4 us
    ppermute x2, local copies, waits for them, and re-layouts, shifted(): lax.ppermute(value, axis, [(source, source + steps) for source in range(i...  5.06 us
  transfers between devices with their start and end apart: 5, of which 1 were waited for; matrix products, arithmetic and copies ran while one was open for 24% of the time, Pallas kernels for 0%

commit v1 on v0

v1 whole, which is shorter than its diff:
```python
import jax
import jax.numpy as jnp
from jax import lax
from jax.experimental import pallas as pl
from jax.experimental.pallas import tpu as pltpu
from jax.sharding import Mesh
from jax.sharding import PartitionSpec as P

H = 36
DH = 32
FR = 2
FT = 384
HD = H * DH
LANES = 128
BLOCKS = HD // LANES
HEADS_PER_BLOCK = LANES // DH
PACKED = HD + LANES
ROWS = FR * FT
NEAR = 2
TM = ("tm_0", "tm_1", "tm_2")
Y, Z, X = TM
EARLY = ((X, 1), (X, 2), (X, 3), (Z, 1), (Z, 2), (Z, 3), (Z, 4))
LATE = ((Y, 1), (Y, 2), (Y, 3))
VMEM_LIMIT = 16 << 20

guide_scale = 4.5
epsilon = 1e-06


def state_kernel(k_hbm, v_hbm, frames_ref, message_ref, total_ref, k_buf, v_buf, sems):
    chunks = BLOCKS // 3
    width = 3 * LANES

    def copies(c):
        columns = pl.ds(c * width, width)
        return (
            pltpu.make_async_copy(k_hbm.at[:, columns], k_buf.at[:, columns], sems.at[0, c]),
            pltpu.make_async_copy(v_hbm.at[:, columns], v_buf.at[:, columns], sems.at[1, c]),
        )

    for c in range(chunks):
        for copy in copies(c):
            copy.start()
    lane = lax.broadcasted_iota(jnp.int32, (DH, LANES), 1)
    ones = jnp.ones((FT, LANES), jnp.bfloat16)
    sums = [jnp.zeros((DH, LANES), jnp.float32) for _ in range(FR)]
    for c in range(chunks):
        for copy in copies(c):
            copy.wait()
        for b in range(3 * c, 3 * c + 3):
            columns = slice(b * LANES, (b + 1) * LANES)
            states = []
            for f in range(FR):
                rows = slice(f * FT, (f + 1) * FT)
                keys = jnp.maximum(k_buf[rows, columns], 0)
                both = jnp.concatenate([v_buf[rows, columns], ones], axis=1)
                outer = lax.dot_general(
                    keys, both, (((0,), (0,)), ((), ())), preferred_element_type=jnp.float32
                )
                state = jnp.zeros((DH, LANES), jnp.float32)
                for h in range(HEADS_PER_BLOCK):
                    piece = outer[h * DH : (h + 1) * DH]
                    state = jnp.where(lane // DH == h, piece[:, :LANES], state)
                    sums[f] = jnp.where(
                        lane == b * HEADS_PER_BLOCK + h, piece[:, LANES:], sums[f]
                    )
                frames_ref[f, :, columns] = state
                message_ref[f, :, columns] = state.astype(jnp.bfloat16)
                states.append(state)
            total_ref[:, columns] = (states[0] + states[1]).astype(jnp.bfloat16)
    for f in range(FR):
        frames_ref[f, :, HD:] = sums[f]
        message_ref[f, :, HD:] = sums[f].astype(jnp.bfloat16)
    total_ref[:, HD:] = (sums[0] + sums[1]).astype(jnp.bfloat16)


def in_hbm(value):
    return pltpu.with_memory_space_constraint(value, pltpu.HBM)


def frame_states(keys, values):
    return pl.pallas_call(
        state_kernel,
        out_shape=(
            jax.ShapeDtypeStruct((FR, DH, PACKED), jnp.float32),
            jax.ShapeDtypeStruct((FR, DH, PACKED), jnp.bfloat16),
            jax.ShapeDtypeStruct((DH, PACKED), jnp.bfloat16),
        ),
        in_specs=[pl.BlockSpec(memory_space=pltpu.HBM)] * 2,
        out_specs=(pl.BlockSpec(memory_space=pltpu.VMEM),) * 3,
        scratch_shapes=[
            pltpu.VMEM((ROWS, HD), jnp.bfloat16),
            pltpu.VMEM((ROWS, HD), jnp.bfloat16),
            pltpu.SemaphoreType.DMA((2, 3)),
        ],
        compiler_params=pltpu.CompilerParams(vmem_limit_bytes=VMEM_LIMIT),
        cost_estimate=pl.CostEstimate(
            flops=2 * ROWS * HD * 2 * LANES, bytes_accessed=4 * ROWS * HD, transcendentals=0
        ),
        name="frame_states",
    )(in_hbm(keys), in_hbm(values))


def output_kernel(
    q0_hbm, q1_ref, s0_ref, s1_ref, w_hbm, out_hbm,
    q_buf, w_buf, x_buf, out_buf, q_sems, w_sem, out_sems,
):
    width = out_hbm.shape[0]
    part = width // 2

    def q_copy(f):
        rows = pl.ds(f * FT, FT)
        return pltpu.make_async_copy(q0_hbm.at[rows], q_buf.at[rows], q_sems.at[f])

    def out_copy(c):
        rows = pl.ds(c * part, part)
        return pltpu.make_async_copy(out_buf.at[rows], out_hbm.at[rows], out_sems.at[c])

    for f in range(FR):
        q_copy(f).start()
    branch = lax.axis_index("cfg")
    start = pl.multiple_of(branch * width, 8)
    own_scale = jnp.where(branch == 0, guide_scale, 1.0 - guide_scale)
    scales = (own_scale, 1.0 - own_scale)
    w_copy = pltpu.make_async_copy(w_hbm.at[pl.ds(start, width)], w_buf, w_sem)
    w_copy.start()

    head = lax.broadcasted_iota(jnp.int32, (LANES, HD), 0)
    lane = lax.broadcasted_iota(jnp.int32, (LANES, HD), 1)
    spread = (head == lane // DH).astype(jnp.bfloat16)
    row_of = lax.broadcasted_iota(jnp.int32, (LANES, LANES), 0) // DH
    lane_of = lax.broadcasted_iota(jnp.int32, (LANES, LANES), 1) // DH
    own_head = (row_of == lane_of).astype(jnp.bfloat16)
    for f in range(FR):
        rows = slice(f * FT, (f + 1) * FT)
        sums = [
            jnp.dot(s_ref[f, :, HD:], spread, preferred_element_type=jnp.float32).astype(
                jnp.bfloat16
            )
            for s_ref in (s0_ref, s1_ref)
        ]
        q_copy(f).wait()
        for b in range(BLOCKS):
            columns = slice(b * LANES, (b + 1) * LANES)
            mixed = None
            for i, (q_ref, s_ref) in enumerate(((q_buf, s0_ref), (q1_ref, s1_ref))):
                state = jnp.concatenate([s_ref[f, :, columns]] * HEADS_PER_BLOCK, axis=0)
                total = jnp.concatenate([sums[i][:, columns]] * HEADS_PER_BLOCK, axis=0)
                both = jnp.concatenate([state * own_head, total * own_head], axis=1)
                feats = jnp.maximum(q_ref[rows, columns], 0)
                parts = jnp.dot(feats, both, preferred_element_type=jnp.float32)
                attended = parts[:, :LANES] * scales[i] / (parts[:, LANES:] + epsilon)
                mixed = attended if mixed is None else mixed + attended
            x_buf[rows, columns] = mixed.astype(jnp.bfloat16)
    w_copy.wait()
    for c in range(2):
        rows = slice(c * part, (c + 1) * part)
        out_buf[rows, :] = lax.dot_general(
            w_buf[rows, :], x_buf[...], (((1,), (1,)), ((), ())), preferred_element_type=jnp.float32
        ).astype(jnp.bfloat16)
        out_copy(c).start()
    for c in range(2):
        out_copy(c).wait()


def guided_columns(own_queries, other_queries, own_states, other_states, weight):
    width = weight.shape[0] // 2
    hbm = pl.BlockSpec(memory_space=pltpu.HBM)
    vmem = pl.BlockSpec(memory_space=pltpu.VMEM)
    return pl.pallas_call(
        output_kernel,
        out_shape=jax.ShapeDtypeStruct((width, ROWS), jnp.bfloat16),
        in_specs=[hbm, vmem, vmem, vmem, hbm],
        out_specs=hbm,
        scratch_shapes=[
            pltpu.VMEM((ROWS, HD), jnp.bfloat16),
            pltpu.VMEM((width, HD), jnp.bfloat16),
            pltpu.VMEM((ROWS, HD), jnp.bfloat16),
            pltpu.VMEM((width, ROWS), jnp.bfloat16),
            pltpu.SemaphoreType.DMA((FR,)),
            pltpu.SemaphoreType.DMA,
            pltpu.SemaphoreType.DMA((2,)),
        ],
        compiler_params=pltpu.CompilerParams(vmem_limit_bytes=40 << 20),
        cost_estimate=pl.CostEstimate(
            flops=2 * ROWS * HD * (width + 4 * LANES),
            bytes_accessed=2 * (2 * ROWS * HD + HD * width + ROWS * width),
            transcendentals=0,
        ),
        name="guided_columns",
    )(in_hbm(own_queries), other_queries, own_states, other_states, in_hbm(weight))


def comes_before(axis, mask):
    index = lax.axis_index(axis)
    return ((index ^ mask) < index).astype(jnp.float32)


def early_kernel(first_ref, *refs):
    parts, (near1, near2, frames, out_ref) = refs[:-4], refs[-4:]
    device = lax.axis_index(TM)
    before = [comes_before(axis, mask) for axis, mask in EARLY]
    prefix = None
    for part, weight in zip(parts, before, strict=True):
        term = part[...].astype(jnp.float32) * weight
        prefix = term if prefix is None else prefix + term
    for i in range(FR):
        first = first_ref[i]
        value = prefix * (first == 0).astype(jnp.float32)
        for offset, pair in ((1, near1), (2, near2)):
            for j in range(FR):
                source = (device - offset) * FR + j
                reached = ((first != 0) & (first <= source)).astype(jnp.float32)
                value = value + pair[j].astype(jnp.float32) * reached
        for j in range(i + 1):
            reached = (first <= device * FR + j).astype(jnp.float32)
            value = value + frames[j] * reached
        out_ref[i] = value


def late_kernel(first_ref, base_ref, *refs):
    *parts, out_ref = refs
    prefix = None
    for part, (axis, mask) in zip(parts, LATE, strict=True):
        term = part[...].astype(jnp.float32) * comes_before(axis, mask)
        prefix = term if prefix is None else prefix + term
    for i in range(FR):
        whole = (first_ref[i] == 0).astype(jnp.float32)
        out_ref[i] = (base_ref[i] + prefix * whole).astype(jnp.bfloat16)


def small_call(kernel, dtype, name, first_frame, *arrays):
    return pl.pallas_call(
        kernel,
        out_shape=jax.ShapeDtypeStruct((FR, DH, PACKED), dtype),
        in_specs=[pl.BlockSpec(memory_space=pltpu.SMEM)]
        + [pl.BlockSpec(memory_space=pltpu.VMEM)] * len(arrays),
        out_specs=pl.BlockSpec(memory_space=pltpu.VMEM),
        compiler_params=pltpu.CompilerParams(vmem_limit_bytes=4 << 20),
        cost_estimate=pl.CostEstimate(
            flops=4 * DH * PACKED * len(arrays),
            bytes_accessed=4 * DH * PACKED * len(arrays),
            transcendentals=0,
        ),
        name=name,
    )(first_frame, *arrays)


def exchanged(value, axis, mask):
    pairs = [(i, i ^ mask) for i in range(lax.axis_size(axis))]
    return lax.ppermute(value, axis, pairs)


def shifted(value, axis, steps):
    count = lax.axis_size(axis)
    return lax.ppermute(value, axis, [(i, (i + steps) % count) for i in range(count)])


def summed(total, arrived):
    return sum((a.astype(jnp.float32) for a in arrived), total.astype(jnp.float32)).astype(
        jnp.bfloat16
    )


def on_device(queries, key_vectors, value_vectors, out_weight, first_frame):
    own_queries = queries[0]
    other_queries = exchanged(own_queries, "cfg", 1)
    frames, message, total = frame_states(key_vectors[0], value_vectors[0])
    total, other_queries = lax.optimization_barrier((total, other_queries))

    parts_x = [exchanged(total, X, m) for m in (1, 2, 3)]
    total = summed(total, parts_x)
    parts_z = [exchanged(total, Z, m) for m in (1, 2, 3)]
    near = [shifted(message, TM, offset) for offset in range(1, NEAR + 1)]
    total = summed(total, parts_z)
    parts_w = [exchanged(total, Z, 4)]
    total = summed(total, parts_w)
    parts_y = [exchanged(total, Y, m) for m in (1, 2, 3)]

    early = (*parts_x, *parts_z, *parts_w, *near, frames)
    base = small_call(early_kernel, jnp.float32, "early_mix", first_frame, *early)
    own_states = small_call(late_kernel, jnp.bfloat16, "late_mix", first_frame, base, *parts_y)
    other_states = exchanged(own_states, "cfg", 1)
    return guided_columns(
        own_queries, other_queries, own_states, other_states, out_weight.T
    ).T


def solution(mesh):
    torus = Mesh(mesh.devices.reshape(mesh.shape["cfg"], 4, 8, 4), ("cfg", "tm_0", "tm_1", "tm_2"))
    in_specs = (P("cfg", TM, None), P("cfg", TM, None), P("cfg", TM, None), P(), P(TM))
    return jax.shard_map(
        on_device, mesh=torus, in_specs=in_specs, out_specs=P(TM, "cfg"), check_vma=False
    )
```

time: 243 us -> 57.5 us (0.24)
  blocking collectives: 101 us -> 0 us
  local copies, waits for them, and re-layouts: 57.5 us -> 0.01 us
  other arithmetic: 22.4 us -> 0.12 us
  waiting for transfers between devices: 3.33 us -> 22.5 us
  matrix products: 16.8 us -> 0 us
  starting transfers between devices: 39.4 us -> 23.8 us
  Pallas kernels: 0 us -> 10.8 us
    all_gather x6 -> x0, blocking collectives: 101 us -> none  [carried_in(): lax.all_gather(part.astype(kind), axis)]
    unnamed x68 -> x2, local copies, waits for them, and re-layouts: 26.6 us -> 0.01 us
    ppermute x5 -> x14, waiting for transfers between devices: 3.33 us -> 22.5 us  [the longest x12 14.2 us: exchanged(): return lax.ppermute(value, axis, pairs)]
    dot_general x7 -> x0, matrix products: 16.8 us -> none  [the longest x1 5.4 us: on_device(): cond_part = jnp.dot(cond_rows, columns, preferred_element_type=jnp.float32)]
    ppermute x5 -> x14, starting transfers between devices: 39.4 us -> 23.8 us  [the longest x12 20.9 us: exchanged(): return lax.ppermute(value, axis, pairs)]
    pallas_call x0 -> x4, Pallas kernels: none -> 10.8 us  [the longest x1 6.76 us: guided_columns(): pl.pallas_call(output_kernel, out_shape=jax.ShapeDtypeStruct((width, ROWS...]
    reduce_sum x7 -> x0, other arithmetic: 7.33 us -> none  [the longest x2 2.21 us: on_device(): jnp.sum(jnp.concatenate(source_states[1:], axis=0), axis=0)]
    max x4 -> x0, local copies, waits for them, and re-layouts: 7.3 us -> none  [the longest x2 5.92 us: on_device(): query_feats = jnp.maximum(query_frames, 0)]
  transfers between devices with their start and end apart: 5 -> 14, of which waited for: 1 -> 10; matrix products, arithmetic and copies ran while one was open for 24% -> 0% of each run, Pallas kernels for 0% -> 6%
where the time goes in v1:
time: 57.5 us; the launch traced here: 57.4 us
  starting transfers between devices  23.8 us (41%)
  waiting for transfers between devices  22.5 us (39%)
  Pallas kernels  10.8 us (19%)
    ppermute x12, starting transfers between devices, exchanged(): return lax.ppermute(value, axis, pairs)  20.9 us
    ppermute x12, waiting for transfers between devices, exchanged(): return lax.ppermute(value, axis, pairs)  14.2 us
    ppermute x2, waiting for transfers between devices, shifted(): lax.ppermute(value, axis, [(i, (i + steps) % count) for i in range(count)])  8.3 us
    pallas_call x1, Pallas kernels, guided_columns(): pl.pallas_call(output_kernel, out_shape=jax.ShapeDtypeStruct((width, ROWS...  6.76 us
    ppermute x2, starting transfers between devices, shifted(): lax.ppermute(value, axis, [(i, (i + steps) % count) for i in range(count)])  2.84 us
    pallas_call x1, Pallas kernels, frame_states(): pl.pallas_call(state_kernel, out_shape=(jax.ShapeDtypeStruct((FR, DH, PAC...  2.58 us
    pallas_call x2, Pallas kernels, small_call(): pl.pallas_call(kernel, out_shape=jax.ShapeDtypeStruct((FR, DH, PACKED), d...  1.47 us
  transfers between devices with their start and end apart: 14, of which 10 were waited for; matrix products, arithmetic and copies ran while one was open for 0% of the time, Pallas kernels for 6%

profile of v1, /device:TPU:1, one launch (start us, length us, event | category | flops | bytes accessed | tf_op | source)
XLA Modules:
  0.0 57.4 jit_solution(13378304414381939160)
XLA Ops:
  0.0 3.2 %collective-permute-start = (bf16[768,1152]{1,0:T(8,128)(2,1)}, bf16[768,1152]{1,0:T(8,128)(2,1)S(1)}, u32[]{:S(2)}, u32[]{:S(2)}) collective-permute-start(bf16[768,1152]{1,0:T(8,128)(2,1)} %bitcast.8), channel_id=1, source_target_pairs={{0,128},{128,0},{1,129},{129,1},{2,130},{130,2},{3,131},{131,3},{4... | collective-permute-start | bytes 5308424 | tf_op jit(solution)/shard_map/ppermute | solution.py:251
  3.2 2.6 %frame_states.1 = (f32[2,32,1280]{2,1,0:T(8,128)S(1)}, bf16[2,32,1280]{2,1,0:T(8,128)(2,1)S(1)}, bf16[32,1280]{1,0:T(8,128)(2,1)S(1)}) custom-call(bf16[768,1152]{1,0:T(8,128)(2,1)} %bitcast.6, bf16[768,1152]{1,0:T(8,128)(2,1)} %bitcast.7), custom_call_target="tpu_custom_call" | custom-call | flops 452984832 | bytes 3538944 | tf_op jit(solution)/shard_map/frame_states/pallas_call | solution.py:82
  5.8 0.9 %collective-permute-done.q1_ref = bf16[768,1152]{1,0:T(8,128)(2,1)S(1)} collective-permute-done((bf16[768,1152]{1,0:T(8,128)(2,1)}, bf16[768,1152]{1,0:T(8,128)(2,1)S(1)}, u32[]{:S(2)}, u32[]{:S(2)}) %collective-permute-start) | collective-permute-done | bytes 1769504 | tf_op jit(solution)/shard_map/ppermute | solution.py:251
  6.8 0.7 %collective-permute-start.3 = (bf16[32,1280]{1,0:T(8,128)(2,1)S(1)}, bf16[32,1280]{1,0:T(8,128)(2,1)S(1)}, u32[]{:S(2)}, u32[]{:S(2)}) collective-permute-start(bf16[32,1280]{1,0:T(8,128)(2,1)S(1)} %get-tuple-element.12), channel_id=1, source_target_pairs={{0,3},{1,2},{2,1},{3,0},{4,7},{5,6},{6,5},{7,4},{8,11},{9,10},{10,... | collective-permute-start | bytes 245768 | tf_op jit(solution)/shard_map/ppermute | solution.py:251
  7.5 0.5 collective-permute-start.2
  8.0 2.0 %collective-permute-start.1 = (bf16[32,1280]{1,0:T(8,128)(2,1)S(1)}, bf16[32,1280]{1,0:T(8,128)(2,1)S(1)}, u32[]{:S(2)}, u32[]{:S(2)}) collective-permute-start(bf16[32,1280]{1,0:T(8,128)(2,1)S(1)} %get-tuple-element.12), channel_id=1, source_target_pairs={{0,1},{1,0},{2,3},{3,2},{4,5},{5,4},{6,7},{7,6},{8,9},{9,8},{10,11... | collective-permute-start | bytes 245768 | tf_op jit(solution)/shard_map/ppermute | solution.py:251
  10.0 1.6 %collective-permute-done.3.refs_2_ = bf16[32,1280]{1,0:T(8,128)(2,1)S(1)} collective-permute-done((bf16[32,1280]{1,0:T(8,128)(2,1)S(1)}, bf16[32,1280]{1,0:T(8,128)(2,1)S(1)}, u32[]{:S(2)}, u32[]{:S(2)}) %collective-permute-start.3) | collective-permute-done | bytes 81952 | tf_op jit(solution)/shard_map/ppermute | solution.py:251
  11.6 0.8 %collective-permute-done.2.refs_1_ = bf16[32,1280]{1,0:T(8,128)(2,1)S(1)} collective-permute-done((bf16[32,1280]{1,0:T(8,128)(2,1)S(1)}, bf16[32,1280]{1,0:T(8,128)(2,1)S(1)}, u32[]{:S(2)}, u32[]{:S(2)}) %collective-permute-start.2) | collective-permute-done | bytes 81952 | tf_op jit(solution)/shard_map/ppermute | solution.py:251
  12.4 1.2 %collective-permute-done.1.refs_0_ = bf16[32,1280]{1,0:T(8,128)(2,1)S(1)} collective-permute-done((bf16[32,1280]{1,0:T(8,128)(2,1)S(1)}, bf16[32,1280]{1,0:T(8,128)(2,1)S(1)}, u32[]{:S(2)}, u32[]{:S(2)}) %collective-permute-start.1) | collective-permute-done | bytes 81952 | tf_op jit(solution)/shard_map/ppermute | solution.py:251
  13.7 3.3 %collective-permute-start.6 = (bf16[32,1280]{1,0:T(8,128)(2,1)S(1)}, bf16[32,1280]{1,0:T(8,128)(2,1)S(1)}, u32[]{:S(2)}, u32[]{:S(2)}) collective-permute-start(bf16[32,1280]{1,0:T(8,128)(2,1)S(1)} %add_convert_fusion.2), channel_id=1, source_target_pairs={{0,12},{4,8},{8,4},{12,0},{16,28},{20,24},{24,20},{28,16},{1,13},{... | collective-permute-start | bytes 245768 | tf_op jit(solution)/shard_map/ppermute | solution.py:251
  17.0 0.4 collective-permute-start.4
  17.4 1.5 %collective-permute-done.6.refs_5_ = bf16[32,1280]{1,0:T(8,128)(2,1)S(1)} collective-permute-done((bf16[32,1280]{1,0:T(8,128)(2,1)S(1)}, bf16[32,1280]{1,0:T(8,128)(2,1)S(1)}, u32[]{:S(2)}, u32[]{:S(2)}) %collective-permute-start.6) | collective-permute-done | bytes 81952 | tf_op jit(solution)/shard_map/ppermute | solution.py:251
  18.9 4.5 %collective-permute-done.5.refs_4_ = bf16[32,1280]{1,0:T(8,128)(2,1)S(1)} collective-permute-done((bf16[32,1280]{1,0:T(8,128)(2,1)S(1)}, bf16[32,1280]{1,0:T(8,128)(2,1)S(1)}, u32[]{:S(2)}, u32[]{:S(2)}) %collective-permute-start.5) | collective-permute-done | bytes 81952 | tf_op jit(solution)/shard_map/ppermute | solution.py:251
  23.5 5.6 %collective-permute-start.7 = (bf16[32,1280]{1,0:T(8,128)(2,1)S(1)}, bf16[32,1280]{1,0:T(8,128)(2,1)S(1)}, u32[]{:S(2)}, u32[]{:S(2)}) collective-permute-start(bf16[32,1280]{1,0:T(8,128)(2,1)S(1)} %add_convert_fusion.1), channel_id=1, source_target_pairs={{0,16},{4,20},{8,24},{12,28},{16,0},{20,4},{24,8},{28,12},{1,17},{... | collective-permute-start | bytes 245768 | tf_op jit(solution)/shard_map/ppermute | solution.py:251
  29.1 2.6 %collective-permute-start.9 = (bf16[2,32,1280]{2,1,0:T(8,128)(2,1)S(1)}, bf16[2,32,1280]{2,1,0:T(8,128)(2,1)S(1)}, u32[]{:S(2)}, u32[]{:S(2)}) collective-permute-start(bf16[2,32,1280]{2,1,0:T(8,128)(2,1)S(1)} %get-tuple-element.13), channel_id=1, source_target_pairs={{0,2},{1,3},{2,4},{3,5},{4,6},{5,7},{6,8},{7,9},{8,10},{9,11},{10,... | collective-permute-start | bytes 491528 | tf_op jit(solution)/shard_map/ppermute | solution.py:256
  32.0 2.8 %collective-permute-start.12 = (bf16[32,1280]{1,0:T(8,128)(2,1)S(1)}, bf16[32,1280]{1,0:T(8,128)(2,1)S(1)}, u32[]{:S(2)}, u32[]{:S(2)}) collective-permute-start(bf16[32,1280]{1,0:T(8,128)(2,1)S(1)} %add_convert_fusion), channel_id=1, source_target_pairs={{0,96},{32,64},{64,32},{96,0},{1,97},{33,65},{65,33},{97,1},{2,98}... | collective-permute-start | bytes 245768 | tf_op jit(solution)/shard_map/ppermute | solution.py:251
  35.5 5.0 %collective-permute-done.9.refs_8_ = bf16[2,32,1280]{2,1,0:T(8,128)(2,1)S(1)} collective-permute-done((bf16[2,32,1280]{2,1,0:T(8,128)(2,1)S(1)}, bf16[2,32,1280]{2,1,0:T(8,128)(2,1)S(1)}, u32[]{:S(2)}, u32[]{:S(2)}) %collective-permute-start.9) | collective-permute-done | bytes 163872 | tf_op jit(solution)/shard_map/ppermute | solution.py:256
  40.5 3.3 %collective-permute-done.8.refs_7_ = bf16[2,32,1280]{2,1,0:T(8,128)(2,1)S(1)} collective-permute-done((bf16[2,32,1280]{2,1,0:T(8,128)(2,1)S(1)}, bf16[2,32,1280]{2,1,0:T(8,128)(2,1)S(1)}, u32[]{:S(2)}, u32[]{:S(2)}) %collective-permute-start.8) | collective-permute-done | bytes 163872 | tf_op jit(solution)/shard_map/ppermute | solution.py:256
  43.8 0.8 %early_mix.1.base_ref = f32[2,32,1280]{2,1,0:T(8,128)S(1)} custom-call(s32[2]{0:T(128)S(1)} %copy-done, bf16[32,1280]{1,0:T(8,128)(2,1)S(1)} %collective-permute-done.1.refs_0_, bf16[32,1280]{1,0:T(8,128)(2,1)S(1)} %collective-permute-done.2.refs_1_, bf16[32,1280]{1,0:T(8,128)(2,1)S(1)} %collective-permute-done.3.refs_2_, ...), custom_call_target="tpu_custom_call" | custom-call | flops 1638400 | bytes 1638400 | tf_op jit(solution)/shard_map/early_mix/pallas_call | solution.py:233
  44.6 2.6 %collective-permute-done.11.refs_1_ = bf16[32,1280]{1,0:T(8,128)(2,1)S(1)} collective-permute-done((bf16[32,1280]{1,0:T(8,128)(2,1)S(1)}, bf16[32,1280]{1,0:T(8,128)(2,1)S(1)}, u32[]{:S(2)}, u32[]{:S(2)}) %collective-permute-start.11) | collective-permute-done | bytes 81952 | tf_op jit(solution)/shard_map/ppermute | solution.py:251
  47.2 0.6 %late_mix.1.s0_ref = bf16[2,32,1280]{2,1,0:T(8,128)(2,1)S(1)} custom-call(s32[2]{0:T(128)S(1)} %copy-done, f32[2,32,1280]{2,1,0:T(8,128)S(1)} %early_mix.1.base_ref, bf16[32,1280]{1,0:T(8,128)(2,1)S(1)} %collective-permute-done.10.refs_0_, bf16[32,1280]{1,0:T(8,128)(2,1)S(1)} %collective-permute-done.11.refs_1_, ...), custom_call_target="tpu_custom_call" | custom-call | flops 655360 | bytes 655360 | tf_op jit(solution)/shard_map/late_mix/pallas_call | solution.py:233
  47.8 1.6 %collective-permute-start.13 = (bf16[2,32,1280]{2,1,0:T(8,128)(2,1)S(1)}, bf16[2,32,1280]{2,1,0:T(8,128)(2,1)S(1)}, u32[]{:S(2)}, u32[]{:S(2)}) collective-permute-start(bf16[2,32,1280]{2,1,0:T(8,128)(2,1)S(1)} %late_mix.1.s0_ref), channel_id=1, source_target_pairs={{0,128},{128,0},{1,129},{129,1},{2,130},{130,2},{3,131},{131,3},{4... | collective-permute-start | bytes 491528 | tf_op jit(solution)/shard_map/ppermute | solution.py:251
  49.5 1.0 %collective-permute-done.13.s1_ref = bf16[2,32,1280]{2,1,0:T(8,128)(2,1)S(1)} collective-permute-done((bf16[2,32,1280]{2,1,0:T(8,128)(2,1)S(1)}, bf16[2,32,1280]{2,1,0:T(8,128)(2,1)S(1)}, u32[]{:S(2)}, u32[]{:S(2)}) %collective-permute-start.13) | collective-permute-done | bytes 163872 | tf_op jit(solution)/shard_map/ppermute | solution.py:251
  50.5 6.8 %guided_columns.1 = bf16[1120,768]{1,0:T(8,128)(2,1)} custom-call(bf16[768,1152]{1,0:T(8,128)(2,1)} %bitcast.9, bf16[768,1152]{1,0:T(8,128)(2,1)S(1)} %collective-permute-done.q1_ref, bf16[2,32,1280]{2,1,0:T(8,128)(2,1)S(1)} %late_mix.1.s0_ref, bf16[2,32,1280]{2,1,0:T(8,128)(2,1)S(1)} %collective-permute-done.13.s1_ref, bf16[2240,1152]{1,0:T(8,128)(2,1)} %bitcast.5), custom_call_target="tpu_custom_call" | custom-call | flops 2887778304 | bytes 7839744 | tf_op jit(solution)/shard_map/guided_columns/pallas_call | solution.py:170
  (13 shorter events, 1.0 us)
Async XLA Ops:
  0.0 6.8 %collective-permute-start = (bf16[768,1152]{1,0:T(8,128)(2,1)}, bf16[768,1152]{1,0:T(8,128)(2,1)S(1)}, u32[]{:S(2)}, u32[]{:S(2)}) collective-permute-start(bf16[768,1152]{1,0:T(8,128)(2,1)} %bitcast.8), channel_id=1, source_target_pairs={{0,128},{128,0},{1,129},{129,1},{2,130},{130,2},{3,131},{131,3},{4... | collective-permute-start | bytes 5308424 | tf_op jit(solution)/shard_map/ppermute | solution.py:251
  3.2 40.5 %copy-start = (s32[2]{0:T(128)S(1)}, s32[2]{0:T(128)}, u32[]{:S(2)}) copy-start(s32[2]{0:T(128)} %first_ref.3) | copy-start | bytes 28
  6.8 4.9 %collective-permute-start.3 = (bf16[32,1280]{1,0:T(8,128)(2,1)S(1)}, bf16[32,1280]{1,0:T(8,128)(2,1)S(1)}, u32[]{:S(2)}, u32[]{:S(2)}) collective-permute-start(bf16[32,1280]{1,0:T(8,128)(2,1)S(1)} %get-tuple-element.12), channel_id=1, source_target_pairs={{0,3},{1,2},{2,1},{3,0},{4,7},{5,6},{6,5},{7,4},{8,11},{9,10},{10,... | collective-permute-start | bytes 245768 | tf_op jit(solution)/shard_map/ppermute | solution.py:251
  7.5 4.9 %collective-permute-start.2 = (bf16[32,1280]{1,0:T(8,128)(2,1)S(1)}, bf16[32,1280]{1,0:T(8,128)(2,1)S(1)}, u32[]{:S(2)}, u32[]{:S(2)}) collective-permute-start(bf16[32,1280]{1,0:T(8,128)(2,1)S(1)} %get-tuple-element.12), channel_id=1, source_target_pairs={{0,2},{1,3},{2,0},{3,1},{4,6},{5,7},{6,4},{7,5},{8,10},{9,11},{10,... | collective-permute-start | bytes 245768 | tf_op jit(solution)/shard_map/ppermute | solution.py:251
  8.0 5.6 %collective-permute-start.1 = (bf16[32,1280]{1,0:T(8,128)(2,1)S(1)}, bf16[32,1280]{1,0:T(8,128)(2,1)S(1)}, u32[]{:S(2)}, u32[]{:S(2)}) collective-permute-start(bf16[32,1280]{1,0:T(8,128)(2,1)S(1)} %get-tuple-element.12), channel_id=1, source_target_pairs={{0,1},{1,0},{2,3},{3,2},{4,5},{5,4},{6,7},{7,6},{8,9},{9,8},{10,11... | collective-permute-start | bytes 245768 | tf_op jit(solution)/shard_map/ppermute | solution.py:251
  13.7 5.2 %collective-permute-start.6 = (bf16[32,1280]{1,0:T(8,128)(2,1)S(1)}, bf16[32,1280]{1,0:T(8,128)(2,1)S(1)}, u32[]{:S(2)}, u32[]{:S(2)}) collective-permute-start(bf16[32,1280]{1,0:T(8,128)(2,1)S(1)} %add_convert_fusion.2), channel_id=1, source_target_pairs={{0,12},{4,8},{8,4},{12,0},{16,28},{20,24},{24,20},{28,16},{1,13},{... | collective-permute-start | bytes 245768 | tf_op jit(solution)/shard_map/ppermute | solution.py:251
  17.0 6.4 %collective-permute-start.5 = (bf16[32,1280]{1,0:T(8,128)(2,1)S(1)}, bf16[32,1280]{1,0:T(8,128)(2,1)S(1)}, u32[]{:S(2)}, u32[]{:S(2)}) collective-permute-start(bf16[32,1280]{1,0:T(8,128)(2,1)S(1)} %add_convert_fusion.2), channel_id=1, source_target_pairs={{0,8},{4,12},{8,0},{12,4},{16,24},{20,28},{24,16},{28,20},{1,9},{5... | collective-permute-start | bytes 245768 | tf_op jit(solution)/shard_map/ppermute | solution.py:251
  17.0 6.4 %collective-permute-start.4 = (bf16[32,1280]{1,0:T(8,128)(2,1)S(1)}, bf16[32,1280]{1,0:T(8,128)(2,1)S(1)}, u32[]{:S(2)}, u32[]{:S(2)}) collective-permute-start(bf16[32,1280]{1,0:T(8,128)(2,1)S(1)} %add_convert_fusion.2), channel_id=1, source_target_pairs={{0,4},{4,0},{8,12},{12,8},{16,20},{20,16},{24,28},{28,24},{1,5},{5... | collective-permute-start | bytes 245768 | tf_op jit(solution)/shard_map/ppermute | solution.py:251
  23.5 8.5 %collective-permute-start.7 = (bf16[32,1280]{1,0:T(8,128)(2,1)S(1)}, bf16[32,1280]{1,0:T(8,128)(2,1)S(1)}, u32[]{:S(2)}, u32[]{:S(2)}) collective-permute-start(bf16[32,1280]{1,0:T(8,128)(2,1)S(1)} %add_convert_fusion.1), channel_id=1, source_target_pairs={{0,16},{4,20},{8,24},{12,28},{16,0},{20,4},{24,8},{28,12},{1,17},{... | collective-permute-start | bytes 245768 | tf_op jit(solution)/shard_map/ppermute | solution.py:251
  29.1 11.4 %collective-permute-start.9 = (bf16[2,32,1280]{2,1,0:T(8,128)(2,1)S(1)}, bf16[2,32,1280]{2,1,0:T(8,128)(2,1)S(1)}, u32[]{:S(2)}, u32[]{:S(2)}) collective-permute-start(bf16[2,32,1280]{2,1,0:T(8,128)(2,1)S(1)} %get-tuple-element.13), channel_id=1, source_target_pairs={{0,2},{1,3},{2,4},{3,5},{4,6},{5,7},{6,8},{7,9},{8,10},{9,11},{10,... | collective-permute-start | bytes 491528 | tf_op jit(solution)/shard_map/ppermute | solution.py:256
  31.7 12.0 %collective-permute-start.8 = (bf16[2,32,1280]{2,1,0:T(8,128)(2,1)S(1)}, bf16[2,32,1280]{2,1,0:T(8,128)(2,1)S(1)}, u32[]{:S(2)}, u32[]{:S(2)}) collective-permute-start(bf16[2,32,1280]{2,1,0:T(8,128)(2,1)S(1)} %get-tuple-element.13), channel_id=1, source_target_pairs={{0,1},{1,2},{2,3},{3,4},{4,5},{5,6},{6,7},{7,8},{8,9},{9,10},{10,1... | collective-permute-start | bytes 491528 | tf_op jit(solution)/shard_map/ppermute | solution.py:256
  32.0 12.6 %collective-permute-start.12 = (bf16[32,1280]{1,0:T(8,128)(2,1)S(1)}, bf16[32,1280]{1,0:T(8,128)(2,1)S(1)}, u32[]{:S(2)}, u32[]{:S(2)}) collective-permute-start(bf16[32,1280]{1,0:T(8,128)(2,1)S(1)} %add_convert_fusion), channel_id=1, source_target_pairs={{0,96},{32,64},{64,32},{96,0},{1,97},{33,65},{65,33},{97,1},{2,98}... | collective-permute-start | bytes 245768 | tf_op jit(solution)/shard_map/ppermute | solution.py:251
  34.8 12.4 %collective-permute-start.11 = (bf16[32,1280]{1,0:T(8,128)(2,1)S(1)}, bf16[32,1280]{1,0:T(8,128)(2,1)S(1)}, u32[]{:S(2)}, u32[]{:S(2)}) collective-permute-start(bf16[32,1280]{1,0:T(8,128)(2,1)S(1)} %add_convert_fusion), channel_id=1, source_target_pairs={{0,64},{32,96},{64,0},{96,32},{1,65},{33,97},{65,1},{97,33},{2,66}... | collective-permute-start | bytes 245768 | tf_op jit(solution)/shard_map/ppermute | solution.py:251
  35.1 12.1 %collective-permute-start.10 = (bf16[32,1280]{1,0:T(8,128)(2,1)S(1)}, bf16[32,1280]{1,0:T(8,128)(2,1)S(1)}, u32[]{:S(2)}, u32[]{:S(2)}) collective-permute-start(bf16[32,1280]{1,0:T(8,128)(2,1)S(1)} %add_convert_fusion), channel_id=1, source_target_pairs={{0,32},{32,0},{64,96},{96,64},{1,33},{33,1},{65,97},{97,65},{2,34}... | collective-permute-start | bytes 245768 | tf_op jit(solution)/shard_map/ppermute | solution.py:251
  47.8 2.7 %collective-permute-start.13 = (bf16[2,32,1280]{2,1,0:T(8,128)(2,1)S(1)}, bf16[2,32,1280]{2,1,0:T(8,128)(2,1)S(1)}, u32[]{:S(2)}, u32[]{:S(2)}) collective-permute-start(bf16[2,32,1280]{2,1,0:T(8,128)(2,1)S(1)} %late_mix.1.s0_ref), channel_id=1, source_target_pairs={{0,128},{128,0},{1,129},{129,1},{2,130},{130,2},{3,131},{131,3},{4... | collective-permute-start | bytes 491528 | tf_op jit(solution)/shard_map/ppermute | solution.py:251

commit v2 on v1

--- a/solution.py
+++ b/solution.py
@@ -19,7 +19,7 @@
 NEAR = 2
 TM = ("tm_0", "tm_1", "tm_2")
 Y, Z, X = TM
-EARLY = ((X, 1), (X, 2), (X, 3), (Z, 1), (Z, 2), (Z, 3), (Z, 4))
+EARLY = ((X, 1), (X, 2), (X, 3), (Z, 1), (Z, 2), (Z, 3), (Z, 7))
 LATE = ((Y, 1), (Y, 2), (Y, 3))
 VMEM_LIMIT = 16 << 20
 
@@ -102,28 +102,14 @@
 
 
 def output_kernel(
-    q0_hbm, q1_ref, s0_ref, s1_ref, w_hbm, out_hbm,
-    q_buf, w_buf, x_buf, out_buf, q_sems, w_sem, out_sems,
+    q0_ref, q1_ref, s0_ref, s1_ref, w_ref, out_hbm, x_buf, out_buf, out_sems
 ):
     width = out_hbm.shape[0]
     part = width // 2
 
-    def q_copy(f):
-        rows = pl.ds(f * FT, FT)
-        return pltpu.make_async_copy(q0_hbm.at[rows], q_buf.at[rows], q_sems.at[f])
-
     def out_copy(c):
         rows = pl.ds(c * part, part)
         return pltpu.make_async_copy(out_buf.at[rows], out_hbm.at[rows], out_sems.at[c])
-
-    for f in range(FR):
-        q_copy(f).start()
-    branch = lax.axis_index("cfg")
-    start = pl.multiple_of(branch * width, 8)
-    own_scale = jnp.where(branch == 0, guide_scale, 1.0 - guide_scale)
-    scales = (own_scale, 1.0 - own_scale)
-    w_copy = pltpu.make_async_copy(w_hbm.at[pl.ds(start, width)], w_buf, w_sem)
-    w_copy.start()
 
     head = lax.broadcasted_iota(jnp.int32, (LANES, HD), 0)
     lane = lax.broadcasted_iota(jnp.int32, (LANES, HD), 1)
@@ -139,46 +125,73 @@
             )
             for s_ref in (s0_ref, s1_ref)
         ]
-        q_copy(f).wait()
         for b in range(BLOCKS):
             columns = slice(b * LANES, (b + 1) * LANES)
-            mixed = None
-            for i, (q_ref, s_ref) in enumerate(((q_buf, s0_ref), (q1_ref, s1_ref))):
+            parts = []
+            for i, (q_ref, s_ref) in enumerate(((q0_ref, s0_ref), (q1_ref, s1_ref))):
                 state = jnp.concatenate([s_ref[f, :, columns]] * HEADS_PER_BLOCK, axis=0)
                 total = jnp.concatenate([sums[i][:, columns]] * HEADS_PER_BLOCK, axis=0)
                 both = jnp.concatenate([state * own_head, total * own_head], axis=1)
                 feats = jnp.maximum(q_ref[rows, columns], 0)
-                parts = jnp.dot(feats, both, preferred_element_type=jnp.float32)
-                attended = parts[:, :LANES] * scales[i] / (parts[:, LANES:] + epsilon)
-                mixed = attended if mixed is None else mixed + attended
+                parts.append(jnp.dot(feats, both, preferred_element_type=jnp.float32))
+            above = [part[:, :LANES] for part in parts]
+            below = [part[:, LANES:] + epsilon for part in parts]
+            mixed = (above[0] * below[1] + above[1] * below[0]) / (below[0] * below[1])
             x_buf[rows, columns] = mixed.astype(jnp.bfloat16)
-    w_copy.wait()
     for c in range(2):
         rows = slice(c * part, (c + 1) * part)
         out_buf[rows, :] = lax.dot_general(
-            w_buf[rows, :], x_buf[...], (((1,), (1,)), ((), ())), preferred_element_type=jnp.float32
+            w_ref[rows, :], x_buf[...], (((1,), (1,)), ((), ())), preferred_element_type=jnp.float32
         ).astype(jnp.bfloat16)
         out_copy(c).start()
     for c in range(2):
         out_copy(c).wait()
 
 
+def fetch_kernel(q_hbm, w_hbm, q_ref, w_ref, sems):
+    width = w_ref.shape[0]
+    start = pl.multiple_of(lax.axis_index("cfg") * width, 16)
+    copies = (
+        pltpu.make_async_copy(q_hbm, q_ref, sems.at[0]),
+        pltpu.make_async_copy(w_hbm.at[pl.ds(start, width)], w_ref, sems.at[1]),
+    )
+    for copy in copies:
+        copy.start()
+    for copy in copies:
+        copy.wait()
+
+
+def fetched(queries, weight):
+    width = weight.shape[0] // 2
+    return pl.pallas_call(
+        fetch_kernel,
+        out_shape=(
+            jax.ShapeDtypeStruct(queries.shape, queries.dtype),
+            jax.ShapeDtypeStruct((width, weight.shape[1]), weight.dtype),
+        ),
+        in_specs=[pl.BlockSpec(memory_space=pltpu.HBM)] * 2,
+        out_specs=(pl.BlockSpec(memory_space=pltpu.VMEM),) * 2,
+        scratch_shapes=[pltpu.SemaphoreType.DMA((2,))],
+        compiler_params=pltpu.CompilerParams(vmem_limit_bytes=2 << 20),
+        cost_estimate=pl.CostEstimate(
+            flops=0, bytes_accessed=4 * (queries.size + weight.size // 2), transcendentals=0
+        ),
+        name="fetch",
+    )(in_hbm(queries), in_hbm(weight))
+
+
 def guided_columns(own_queries, other_queries, own_states, other_states, weight):
-    width = weight.shape[0] // 2
+    width = weight.shape[0]
     hbm = pl.BlockSpec(memory_space=pltpu.HBM)
     vmem = pl.BlockSpec(memory_space=pltpu.VMEM)
     return pl.pallas_call(
         output_kernel,
         out_shape=jax.ShapeDtypeStruct((width, ROWS), jnp.bfloat16),
-        in_specs=[hbm, vmem, vmem, vmem, hbm],
+        in_specs=[vmem] * 5,
         out_specs=hbm,
         scratch_shapes=[
             pltpu.VMEM((ROWS, HD), jnp.bfloat16),
-            pltpu.VMEM((width, HD), jnp.bfloat16),
-            pltpu.VMEM((ROWS, HD), jnp.bfloat16),
             pltpu.VMEM((width, ROWS), jnp.bfloat16),
-            pltpu.SemaphoreType.DMA((FR,)),
-            pltpu.SemaphoreType.DMA,
             pltpu.SemaphoreType.DMA((2,)),
         ],
         compiler_params=pltpu.CompilerParams(vmem_limit_bytes=40 << 20),
@@ -188,7 +201,7 @@
             transcendentals=0,
         ),
         name="guided_columns",
-    )(in_hbm(own_queries), other_queries, own_states, other_states, in_hbm(weight))
+    )(own_queries, other_queries, own_states, other_states, weight)
 
 
 def comes_before(axis, mask):
@@ -224,9 +237,12 @@
     for part, (axis, mask) in zip(parts, LATE, strict=True):
         term = part[...].astype(jnp.float32) * comes_before(axis, mask)
         prefix = term if prefix is None else prefix + term
+    own_scale = jnp.where(lax.axis_index("cfg") == 0, guide_scale, 1.0 - guide_scale)
     for i in range(FR):
         whole = (first_ref[i] == 0).astype(jnp.float32)
-        out_ref[i] = (base_ref[i] + prefix * whole).astype(jnp.bfloat16)
+        value = base_ref[i] + prefix * whole
+        out_ref[i, :, :HD] = (value[:, :HD] * own_scale).astype(jnp.bfloat16)
+        out_ref[i, :, HD:] = value[:, HD:].astype(jnp.bfloat16)
 
 
 def small_call(kernel, dtype, name, first_frame, *arrays):
@@ -270,10 +286,13 @@
 
     parts_x = [exchanged(total, X, m) for m in (1, 2, 3)]
     total = summed(total, parts_x)
+    total, later_queries, later_weight = lax.optimization_barrier((total, own_queries, out_weight.T))
+    held_queries, half_weight = fetched(later_queries, later_weight)
     parts_z = [exchanged(total, Z, m) for m in (1, 2, 3)]
     near = [shifted(message, TM, offset) for offset in range(1, NEAR + 1)]
     total = summed(total, parts_z)
-    parts_w = [exchanged(total, Z, 4)]
+    total, held_queries, half_weight = lax.optimization_barrier((total, held_queries, half_weight))
+    parts_w = [exchanged(total, Z, 7)]
     total = summed(total, parts_w)
     parts_y = [exchanged(total, Y, m) for m in (1, 2, 3)]
 
@@ -282,7 +301,7 @@
     own_states = small_call(late_kernel, jnp.bfloat16, "late_mix", first_frame, base, *parts_y)
     other_states = exchanged(own_states, "cfg", 1)
     return guided_columns(
-        own_queries, other_queries, own_states, other_states, out_weight.T
+        held_queries, other_queries, own_states, other_states, half_weight
     ).T
 
 

time: 57.5 us -> 55 us (0.957)
  waiting for transfers between devices: 22.5 us -> 20.1 us
  starting transfers between devices: 23.8 us -> 22.7 us
  Pallas kernels: 10.8 us -> 11.8 us
    ppermute x12, waiting for transfers between devices: 14.2 us -> 11.4 us  [exchanged(): return lax.ppermute(value, axis, pairs)]
    pallas_call x0 -> x1, Pallas kernels: none -> 2.28 us  [fetched(): pl.pallas_call(fetch_kernel, out_shape=(jax.ShapeDtypeStruct(queries.shap...]
    pallas_call x1, Pallas kernels: 6.76 us -> 5.47 us  [guided_columns(): pl.pallas_call(output_kernel, out_shape=jax.ShapeDtypeStruct((width, ROWS...]
    ppermute x12, starting transfers between devices: 20.9 us -> 20.1 us  [exchanged(): return lax.ppermute(value, axis, pairs)]
  transfers between devices with their start and end apart: 14 -> 14, of which waited for: 10 -> 9; matrix products, arithmetic and copies ran while one was open for 0% -> 0% of each run, Pallas kernels for 6% -> 10%
where the time goes in v2:
time: 55 us; the launch traced here: 54.9 us
  starting transfers between devices  22.7 us (41%)
  waiting for transfers between devices  20.1 us (37%)
  Pallas kernels  11.8 us (21%)
    ppermute x12, starting transfers between devices, exchanged(): return lax.ppermute(value, axis, pairs)  20.1 us
    ppermute x12, waiting for transfers between devices, exchanged(): return lax.ppermute(value, axis, pairs)  11.4 us
    ppermute x2, waiting for transfers between devices, shifted(): lax.ppermute(value, axis, [(i, (i + steps) % count) for i in range(count)])  8.72 us
    pallas_call x1, Pallas kernels, guided_columns(): pl.pallas_call(output_kernel, out_shape=jax.ShapeDtypeStruct((width, ROWS...  5.47 us
    ppermute x2, starting transfers between devices, shifted(): lax.ppermute(value, axis, [(i, (i + steps) % count) for i in range(count)])  2.62 us
    pallas_call x1, Pallas kernels, frame_states(): pl.pallas_call(state_kernel, out_shape=(jax.ShapeDtypeStruct((FR, DH, PAC...  2.57 us
    pallas_call x1, Pallas kernels, fetched(): pl.pallas_call(fetch_kernel, out_shape=(jax.ShapeDtypeStruct(queries.shap...  2.28 us
    pallas_call x2, Pallas kernels, small_call(): pl.pallas_call(kernel, out_shape=jax.ShapeDtypeStruct((FR, DH, PACKED), d...  1.48 us
  transfers between devices with their start and end apart: 14, of which 9 were waited for; matrix products, arithmetic and copies ran while one was open for 0% of the time, Pallas kernels for 10%

profile of v2, /device:TPU:1, one launch (start us, length us, event | category | flops | bytes accessed | tf_op | source)
XLA Modules:
  0.0 54.9 jit_solution(4190020773345820912)
XLA Ops:
  0.0 3.2 %collective-permute-start = (bf16[768,1152]{1,0:T(8,128)(2,1)}, bf16[768,1152]{1,0:T(8,128)(2,1)S(1)}, u32[]{:S(2)}, u32[]{:S(2)}) collective-permute-start(bf16[768,1152]{1,0:T(8,128)(2,1)} %bitcast.8), channel_id=1, source_target_pairs={{0,128},{128,0},{1,129},{129,1},{2,130},{130,2},{3,131},{131,3},{4... | collective-permute-start | bytes 5308424 | tf_op jit(solution)/shard_map/ppermute | solution.py:267
  3.2 2.6 %frame_states.1 = (f32[2,32,1280]{2,1,0:T(8,128)S(1)}, bf16[2,32,1280]{2,1,0:T(8,128)(2,1)S(1)}, bf16[32,1280]{1,0:T(8,128)(2,1)S(1)}) custom-call(bf16[768,1152]{1,0:T(8,128)(2,1)} %bitcast.6, bf16[768,1152]{1,0:T(8,128)(2,1)} %bitcast.7), custom_call_target="tpu_custom_call" | custom-call | flops 452984832 | bytes 3538944 | tf_op jit(solution)/shard_map/frame_states/pallas_call | solution.py:82
  5.8 1.0 %collective-permute-done.q1_ref = bf16[768,1152]{1,0:T(8,128)(2,1)S(1)} collective-permute-done((bf16[768,1152]{1,0:T(8,128)(2,1)}, bf16[768,1152]{1,0:T(8,128)(2,1)S(1)}, u32[]{:S(2)}, u32[]{:S(2)}) %collective-permute-start) | collective-permute-done | bytes 1769504 | tf_op jit(solution)/shard_map/ppermute | solution.py:267
  6.8 0.7 %collective-permute-start.3 = (bf16[32,1280]{1,0:T(8,128)(2,1)S(1)}, bf16[32,1280]{1,0:T(8,128)(2,1)S(1)}, u32[]{:S(2)}, u32[]{:S(2)}) collective-permute-start(bf16[32,1280]{1,0:T(8,128)(2,1)S(1)} %get-tuple-element.19), channel_id=1, source_target_pairs={{0,3},{1,2},{2,1},{3,0},{4,7},{5,6},{6,5},{7,4},{8,11},{9,10},{10,... | collective-permute-start | bytes 245768 | tf_op jit(solution)/shard_map/ppermute | solution.py:267
  7.5 0.5 collective-permute-start.2
  8.0 2.0 %collective-permute-start.1 = (bf16[32,1280]{1,0:T(8,128)(2,1)S(1)}, bf16[32,1280]{1,0:T(8,128)(2,1)S(1)}, u32[]{:S(2)}, u32[]{:S(2)}) collective-permute-start(bf16[32,1280]{1,0:T(8,128)(2,1)S(1)} %get-tuple-element.19), channel_id=1, source_target_pairs={{0,1},{1,0},{2,3},{3,2},{4,5},{5,4},{6,7},{7,6},{8,9},{9,8},{10,11... | collective-permute-start | bytes 245768 | tf_op jit(solution)/shard_map/ppermute | solution.py:267
  10.0 1.6 %collective-permute-done.3.refs_2_ = bf16[32,1280]{1,0:T(8,128)(2,1)S(1)} collective-permute-done((bf16[32,1280]{1,0:T(8,128)(2,1)S(1)}, bf16[32,1280]{1,0:T(8,128)(2,1)S(1)}, u32[]{:S(2)}, u32[]{:S(2)}) %collective-permute-start.3) | collective-permute-done | bytes 81952 | tf_op jit(solution)/shard_map/ppermute | solution.py:267
  11.6 0.8 %collective-permute-done.2.refs_1_ = bf16[32,1280]{1,0:T(8,128)(2,1)S(1)} collective-permute-done((bf16[32,1280]{1,0:T(8,128)(2,1)S(1)}, bf16[32,1280]{1,0:T(8,128)(2,1)S(1)}, u32[]{:S(2)}, u32[]{:S(2)}) %collective-permute-start.2) | collective-permute-done | bytes 81952 | tf_op jit(solution)/shard_map/ppermute | solution.py:267
  12.4 1.2 %collective-permute-done.1.refs_0_ = bf16[32,1280]{1,0:T(8,128)(2,1)S(1)} collective-permute-done((bf16[32,1280]{1,0:T(8,128)(2,1)S(1)}, bf16[32,1280]{1,0:T(8,128)(2,1)S(1)}, u32[]{:S(2)}, u32[]{:S(2)}) %collective-permute-start.1) | collective-permute-done | bytes 81952 | tf_op jit(solution)/shard_map/ppermute | solution.py:267
  13.7 3.3 %collective-permute-start.6 = (bf16[32,1280]{1,0:T(8,128)(2,1)S(1)}, bf16[32,1280]{1,0:T(8,128)(2,1)S(1)}, u32[]{:S(2)}, u32[]{:S(2)}) collective-permute-start(bf16[32,1280]{1,0:T(8,128)(2,1)S(1)} %add_convert_fusion.2), channel_id=1, source_target_pairs={{0,12},{4,8},{8,4},{12,0},{16,28},{20,24},{24,20},{28,16},{1,13},{... | collective-permute-start | bytes 245768 | tf_op jit(solution)/shard_map/ppermute | solution.py:267
  17.0 0.4 collective-permute-start.4
  17.4 2.3 %fetch.1 = (bf16[768,1152]{1,0:T(8,128)(2,1)S(1)}, bf16[1120,1152]{1,0:T(8,128)(2,1)S(1)}) custom-call(bf16[768,1152]{1,0:T(8,128)(2,1)} %bitcast.9, bf16[2240,1152]{1,0:T(8,128)(2,1)} %bitcast.5), custom_call_target="tpu_custom_call" | custom-call | bytes 8699904 | tf_op jit(solution)/shard_map/fetch/pallas_call | solution.py:166
  19.7 3.8 %collective-permute-done.5.refs_4_ = bf16[32,1280]{1,0:T(8,128)(2,1)S(1)} collective-permute-done((bf16[32,1280]{1,0:T(8,128)(2,1)S(1)}, bf16[32,1280]{1,0:T(8,128)(2,1)S(1)}, u32[]{:S(2)}, u32[]{:S(2)}) %collective-permute-start.5) | collective-permute-done | bytes 81952 | tf_op jit(solution)/shard_map/ppermute | solution.py:267
  23.5 4.3 %collective-permute-start.7 = (bf16[32,1280]{1,0:T(8,128)(2,1)S(1)}, bf16[32,1280]{1,0:T(8,128)(2,1)S(1)}, u32[]{:S(2)}, u32[]{:S(2)}) collective-permute-start(bf16[32,1280]{1,0:T(8,128)(2,1)S(1)} %add_convert_fusion.1), channel_id=1, source_target_pairs={{0,28},{4,24},{8,20},{12,16},{16,12},{20,8},{24,4},{28,0},{1,29},{... | collective-permute-start | bytes 245768 | tf_op jit(solution)/shard_map/ppermute | solution.py:267
  27.8 2.6 %collective-permute-start.9 = (bf16[2,32,1280]{2,1,0:T(8,128)(2,1)S(1)}, bf16[2,32,1280]{2,1,0:T(8,128)(2,1)S(1)}, u32[]{:S(2)}, u32[]{:S(2)}) collective-permute-start(bf16[2,32,1280]{2,1,0:T(8,128)(2,1)S(1)} %get-tuple-element.28), channel_id=1, source_target_pairs={{0,2},{1,3},{2,4},{3,5},{4,6},{5,7},{6,8},{7,9},{8,10},{9,11},{10,... | collective-permute-start | bytes 491528 | tf_op jit(solution)/shard_map/ppermute | solution.py:272
  30.4 2.8 %collective-permute-start.12 = (bf16[32,1280]{1,0:T(8,128)(2,1)S(1)}, bf16[32,1280]{1,0:T(8,128)(2,1)S(1)}, u32[]{:S(2)}, u32[]{:S(2)}) collective-permute-start(bf16[32,1280]{1,0:T(8,128)(2,1)S(1)} %add_convert_fusion), channel_id=1, source_target_pairs={{0,96},{32,64},{64,32},{96,0},{1,97},{33,65},{65,33},{97,1},{2,98}... | collective-permute-start | bytes 245768 | tf_op jit(solution)/shard_map/ppermute | solution.py:267
  33.9 4.7 %collective-permute-done.9.refs_8_ = bf16[2,32,1280]{2,1,0:T(8,128)(2,1)S(1)} collective-permute-done((bf16[2,32,1280]{2,1,0:T(8,128)(2,1)S(1)}, bf16[2,32,1280]{2,1,0:T(8,128)(2,1)S(1)}, u32[]{:S(2)}, u32[]{:S(2)}) %collective-permute-start.9) | collective-permute-done | bytes 163872 | tf_op jit(solution)/shard_map/ppermute | solution.py:272
  38.6 4.0 %collective-permute-done.8.refs_7_ = bf16[2,32,1280]{2,1,0:T(8,128)(2,1)S(1)} collective-permute-done((bf16[2,32,1280]{2,1,0:T(8,128)(2,1)S(1)}, bf16[2,32,1280]{2,1,0:T(8,128)(2,1)S(1)}, u32[]{:S(2)}, u32[]{:S(2)}) %collective-permute-start.8) | collective-permute-done | bytes 163872 | tf_op jit(solution)/shard_map/ppermute | solution.py:272
  42.7 0.8 %early_mix.1.base_ref = f32[2,32,1280]{2,1,0:T(8,128)S(1)} custom-call(s32[2]{0:T(128)S(1)} %copy-done, bf16[32,1280]{1,0:T(8,128)(2,1)S(1)} %collective-permute-done.1.refs_0_, bf16[32,1280]{1,0:T(8,128)(2,1)S(1)} %collective-permute-done.2.refs_1_, bf16[32,1280]{1,0:T(8,128)(2,1)S(1)} %collective-permute-done.3.refs_2_, ...), custom_call_target="tpu_custom_call" | custom-call | flops 1638400 | bytes 1638400 | tf_op jit(solution)/shard_map/early_mix/pallas_call | solution.py:249
  43.5 2.0 %collective-permute-done.11.refs_1_ = bf16[32,1280]{1,0:T(8,128)(2,1)S(1)} collective-permute-done((bf16[32,1280]{1,0:T(8,128)(2,1)S(1)}, bf16[32,1280]{1,0:T(8,128)(2,1)S(1)}, u32[]{:S(2)}, u32[]{:S(2)}) %collective-permute-start.11) | collective-permute-done | bytes 81952 | tf_op jit(solution)/shard_map/ppermute | solution.py:267
  45.5 0.6 %late_mix.1.s0_ref = bf16[2,32,1280]{2,1,0:T(8,128)(2,1)S(1)} custom-call(s32[2]{0:T(128)S(1)} %copy-done, f32[2,32,1280]{2,1,0:T(8,128)S(1)} %early_mix.1.base_ref, bf16[32,1280]{1,0:T(8,128)(2,1)S(1)} %collective-permute-done.10.refs_0_, bf16[32,1280]{1,0:T(8,128)(2,1)S(1)} %collective-permute-done.11.refs_1_, ...), custom_call_target="tpu_custom_call" | custom-call | flops 655360 | bytes 655360 | tf_op jit(solution)/shard_map/late_mix/pallas_call | solution.py:249
  46.1 2.1 %collective-permute-start.13 = (bf16[2,32,1280]{2,1,0:T(8,128)(2,1)S(1)}, bf16[2,32,1280]{2,1,0:T(8,128)(2,1)S(1)}, u32[]{:S(2)}, u32[]{:S(2)}) collective-permute-start(bf16[2,32,1280]{2,1,0:T(8,128)(2,1)S(1)} %late_mix.1.s0_ref), channel_id=1, source_target_pairs={{0,128},{128,0},{1,129},{129,1},{2,130},{130,2},{3,131},{131,3},{4... | collective-permute-start | bytes 491528 | tf_op jit(solution)/shard_map/ppermute | solution.py:267
  48.3 1.0 %collective-permute-done.13.s1_ref = bf16[2,32,1280]{2,1,0:T(8,128)(2,1)S(1)} collective-permute-done((bf16[2,32,1280]{2,1,0:T(8,128)(2,1)S(1)}, bf16[2,32,1280]{2,1,0:T(8,128)(2,1)S(1)}, u32[]{:S(2)}, u32[]{:S(2)}) %collective-permute-start.13) | collective-permute-done | bytes 163872 | tf_op jit(solution)/shard_map/ppermute | solution.py:267
  49.3 5.5 %guided_columns.1 = bf16[1120,768]{1,0:T(8,128)(2,1)} custom-call(bf16[768,1152]{1,0:T(8,128)(2,1)S(1)} %get-tuple-element.25.q0_ref, bf16[768,1152]{1,0:T(8,128)(2,1)S(1)} %collective-permute-done.q1_ref, bf16[2,32,1280]{2,1,0:T(8,128)(2,1)S(1)} %late_mix.1.s0_ref, bf16[2,32,1280]{2,1,0:T(8,128)(2,1)S(1)} %collective-permute-done.13.s1_ref, ...), custom_call_target="tpu_custom_call" | custom-call | flops 2887778304 | bytes 7839744 | tf_op jit(solution)/shard_map/guided_columns/pallas_call | solution.py:187
  (14 shorter events, 0.8 us)
Async XLA Ops:
  0.0 6.8 %collective-permute-start = (bf16[768,1152]{1,0:T(8,128)(2,1)}, bf16[768,1152]{1,0:T(8,128)(2,1)S(1)}, u32[]{:S(2)}, u32[]{:S(2)}) collective-permute-start(bf16[768,1152]{1,0:T(8,128)(2,1)} %bitcast.8), channel_id=1, source_target_pairs={{0,128},{128,0},{1,129},{129,1},{2,130},{130,2},{3,131},{131,3},{4... | collective-permute-start | bytes 5308424 | tf_op jit(solution)/shard_map/ppermute | solution.py:267
  6.8 4.9 %collective-permute-start.3 = (bf16[32,1280]{1,0:T(8,128)(2,1)S(1)}, bf16[32,1280]{1,0:T(8,128)(2,1)S(1)}, u32[]{:S(2)}, u32[]{:S(2)}) collective-permute-start(bf16[32,1280]{1,0:T(8,128)(2,1)S(1)} %get-tuple-element.19), channel_id=1, source_target_pairs={{0,3},{1,2},{2,1},{3,0},{4,7},{5,6},{6,5},{7,4},{8,11},{9,10},{10,... | collective-permute-start | bytes 245768 | tf_op jit(solution)/shard_map/ppermute | solution.py:267
  7.5 4.9 %collective-permute-start.2 = (bf16[32,1280]{1,0:T(8,128)(2,1)S(1)}, bf16[32,1280]{1,0:T(8,128)(2,1)S(1)}, u32[]{:S(2)}, u32[]{:S(2)}) collective-permute-start(bf16[32,1280]{1,0:T(8,128)(2,1)S(1)} %get-tuple-element.19), channel_id=1, source_target_pairs={{0,2},{1,3},{2,0},{3,1},{4,6},{5,7},{6,4},{7,5},{8,10},{9,11},{10,... | collective-permute-start | bytes 245768 | tf_op jit(solution)/shard_map/ppermute | solution.py:267
  8.0 5.6 %collective-permute-start.1 = (bf16[32,1280]{1,0:T(8,128)(2,1)S(1)}, bf16[32,1280]{1,0:T(8,128)(2,1)S(1)}, u32[]{:S(2)}, u32[]{:S(2)}) collective-permute-start(bf16[32,1280]{1,0:T(8,128)(2,1)S(1)} %get-tuple-element.19), channel_id=1, source_target_pairs={{0,1},{1,0},{2,3},{3,2},{4,5},{5,4},{6,7},{7,6},{8,9},{9,8},{10,11... | collective-permute-start | bytes 245768 | tf_op jit(solution)/shard_map/ppermute | solution.py:267
  13.7 28.9 %copy-start = (s32[2]{0:T(128)S(1)}, s32[2]{0:T(128)}, u32[]{:S(2)}) copy-start(s32[2]{0:T(128)} %first_ref.3) | copy-start | bytes 28
  13.7 5.9 %collective-permute-start.6 = (bf16[32,1280]{1,0:T(8,128)(2,1)S(1)}, bf16[32,1280]{1,0:T(8,128)(2,1)S(1)}, u32[]{:S(2)}, u32[]{:S(2)}) collective-permute-start(bf16[32,1280]{1,0:T(8,128)(2,1)S(1)} %add_convert_fusion.2), channel_id=1, source_target_pairs={{0,12},{4,8},{8,4},{12,0},{16,28},{20,24},{24,20},{28,16},{1,13},{... | collective-permute-start | bytes 245768 | tf_op jit(solution)/shard_map/ppermute | solution.py:267
  17.0 6.4 %collective-permute-start.5 = (bf16[32,1280]{1,0:T(8,128)(2,1)S(1)}, bf16[32,1280]{1,0:T(8,128)(2,1)S(1)}, u32[]{:S(2)}, u32[]{:S(2)}) collective-permute-start(bf16[32,1280]{1,0:T(8,128)(2,1)S(1)} %add_convert_fusion.2), channel_id=1, source_target_pairs={{0,8},{4,12},{8,0},{12,4},{16,24},{20,28},{24,16},{28,20},{1,9},{5... | collective-permute-start | bytes 245768 | tf_op jit(solution)/shard_map/ppermute | solution.py:267
  17.0 6.4 %collective-permute-start.4 = (bf16[32,1280]{1,0:T(8,128)(2,1)S(1)}, bf16[32,1280]{1,0:T(8,128)(2,1)S(1)}, u32[]{:S(2)}, u32[]{:S(2)}) collective-permute-start(bf16[32,1280]{1,0:T(8,128)(2,1)S(1)} %add_convert_fusion.2), channel_id=1, source_target_pairs={{0,4},{4,0},{8,12},{12,8},{16,20},{20,16},{24,28},{28,24},{1,5},{5... | collective-permute-start | bytes 245768 | tf_op jit(solution)/shard_map/ppermute | solution.py:267
  23.5 6.9 %collective-permute-start.7 = (bf16[32,1280]{1,0:T(8,128)(2,1)S(1)}, bf16[32,1280]{1,0:T(8,128)(2,1)S(1)}, u32[]{:S(2)}, u32[]{:S(2)}) collective-permute-start(bf16[32,1280]{1,0:T(8,128)(2,1)S(1)} %add_convert_fusion.1), channel_id=1, source_target_pairs={{0,28},{4,24},{8,20},{12,16},{16,12},{20,8},{24,4},{28,0},{1,29},{... | collective-permute-start | bytes 245768 | tf_op jit(solution)/shard_map/ppermute | solution.py:267
  27.8 10.9 %collective-permute-start.9 = (bf16[2,32,1280]{2,1,0:T(8,128)(2,1)S(1)}, bf16[2,32,1280]{2,1,0:T(8,128)(2,1)S(1)}, u32[]{:S(2)}, u32[]{:S(2)}) collective-permute-start(bf16[2,32,1280]{2,1,0:T(8,128)(2,1)S(1)} %get-tuple-element.28), channel_id=1, source_target_pairs={{0,2},{1,3},{2,4},{3,5},{4,6},{5,7},{6,8},{7,9},{8,10},{9,11},{10,... | collective-permute-start | bytes 491528 | tf_op jit(solution)/shard_map/ppermute | solution.py:272
  30.4 12.3 %collective-permute-start.8 = (bf16[2,32,1280]{2,1,0:T(8,128)(2,1)S(1)}, bf16[2,32,1280]{2,1,0:T(8,128)(2,1)S(1)}, u32[]{:S(2)}, u32[]{:S(2)}) collective-permute-start(bf16[2,32,1280]{2,1,0:T(8,128)(2,1)S(1)} %get-tuple-element.28), channel_id=1, source_target_pairs={{0,1},{1,2},{2,3},{3,4},{4,5},{5,6},{6,7},{7,8},{8,9},{9,10},{10,1... | collective-permute-start | bytes 491528 | tf_op jit(solution)/shard_map/ppermute | solution.py:272
  30.4 13.1 %collective-permute-start.12 = (bf16[32,1280]{1,0:T(8,128)(2,1)S(1)}, bf16[32,1280]{1,0:T(8,128)(2,1)S(1)}, u32[]{:S(2)}, u32[]{:S(2)}) collective-permute-start(bf16[32,1280]{1,0:T(8,128)(2,1)S(1)} %add_convert_fusion), channel_id=1, source_target_pairs={{0,96},{32,64},{64,32},{96,0},{1,97},{33,65},{65,33},{97,1},{2,98}... | collective-permute-start | bytes 245768 | tf_op jit(solution)/shard_map/ppermute | solution.py:267
  33.2 12.2 %collective-permute-start.11 = (bf16[32,1280]{1,0:T(8,128)(2,1)S(1)}, bf16[32,1280]{1,0:T(8,128)(2,1)S(1)}, u32[]{:S(2)}, u32[]{:S(2)}) collective-permute-start(bf16[32,1280]{1,0:T(8,128)(2,1)S(1)} %add_convert_fusion), channel_id=1, source_target_pairs={{0,64},{32,96},{64,0},{96,32},{1,65},{33,97},{65,1},{97,33},{2,66}... | collective-permute-start | bytes 245768 | tf_op jit(solution)/shard_map/ppermute | solution.py:267
  33.6 11.9 %collective-permute-start.10 = (bf16[32,1280]{1,0:T(8,128)(2,1)S(1)}, bf16[32,1280]{1,0:T(8,128)(2,1)S(1)}, u32[]{:S(2)}, u32[]{:S(2)}) collective-permute-start(bf16[32,1280]{1,0:T(8,128)(2,1)S(1)} %add_convert_fusion), channel_id=1, source_target_pairs={{0,32},{32,0},{64,96},{96,64},{1,33},{33,1},{65,97},{97,65},{2,34}... | collective-permute-start | bytes 245768 | tf_op jit(solution)/shard_map/ppermute | solution.py:267
  46.1 3.2 %collective-permute-start.13 = (bf16[2,32,1280]{2,1,0:T(8,128)(2,1)S(1)}, bf16[2,32,1280]{2,1,0:T(8,128)(2,1)S(1)}, u32[]{:S(2)}, u32[]{:S(2)}) collective-permute-start(bf16[2,32,1280]{2,1,0:T(8,128)(2,1)S(1)} %late_mix.1.s0_ref), channel_id=1, source_target_pairs={{0,128},{128,0},{1,129},{129,1},{2,130},{130,2},{3,131},{131,3},{4... | collective-permute-start | bytes 491528 | tf_op jit(solution)/shard_map/ppermute | solution.py:267

commit v3 on v2

--- a/solution.py
+++ b/solution.py
@@ -16,10 +16,11 @@
 HEADS_PER_BLOCK = LANES // DH
 PACKED = HD + LANES
 ROWS = FR * FT
-NEAR = 2
 TM = ("tm_0", "tm_1", "tm_2")
 Y, Z, X = TM
-EARLY = ((X, 1), (X, 2), (X, 3), (Z, 1), (Z, 2), (Z, 3), (Z, 7))
+ROW = (Y, Z)
+MASKS = (1, 2, 3)
+EARLY = ((Z, 1), (Z, 2), (Z, 3), (Z, 7))
 LATE = ((Y, 1), (Y, 2), (Y, 3))
 VMEM_LIMIT = 16 << 20
 
@@ -27,7 +28,7 @@
 epsilon = 1e-06
 
 
-def state_kernel(k_hbm, v_hbm, frames_ref, message_ref, total_ref, k_buf, v_buf, sems):
+def state_kernel(k_hbm, v_hbm, frames_ref, total_ref, second_ref, k_buf, v_buf, sems):
     chunks = BLOCKS // 3
     width = 3 * LANES
 
@@ -65,13 +66,13 @@
                         lane == b * HEADS_PER_BLOCK + h, piece[:, LANES:], sums[f]
                     )
                 frames_ref[f, :, columns] = state
-                message_ref[f, :, columns] = state.astype(jnp.bfloat16)
                 states.append(state)
             total_ref[:, columns] = (states[0] + states[1]).astype(jnp.bfloat16)
+            second_ref[:, columns] = states[1].astype(jnp.bfloat16)
     for f in range(FR):
         frames_ref[f, :, HD:] = sums[f]
-        message_ref[f, :, HD:] = sums[f].astype(jnp.bfloat16)
     total_ref[:, HD:] = (sums[0] + sums[1]).astype(jnp.bfloat16)
+    second_ref[:, HD:] = sums[1].astype(jnp.bfloat16)
 
 
 def in_hbm(value):
@@ -83,7 +84,7 @@
         state_kernel,
         out_shape=(
             jax.ShapeDtypeStruct((FR, DH, PACKED), jnp.float32),
-            jax.ShapeDtypeStruct((FR, DH, PACKED), jnp.bfloat16),
+            jax.ShapeDtypeStruct((DH, PACKED), jnp.bfloat16),
             jax.ShapeDtypeStruct((DH, PACKED), jnp.bfloat16),
         ),
         in_specs=[pl.BlockSpec(memory_space=pltpu.HBM)] * 2,
@@ -209,25 +210,44 @@
     return ((index ^ mask) < index).astype(jnp.float32)
 
 
+def row_source(mask, j):
+    x = lax.axis_index(X)
+    return (lax.axis_index(TM) - x + (x ^ mask)) * FR + j
+
+
+def reached_part(first, mask, both, second):
+    one = (first <= row_source(mask, 1)).astype(jnp.float32)
+    two = (first <= row_source(mask, 0)).astype(jnp.float32)
+    return both.astype(jnp.float32) * two + second.astype(jnp.float32) * (one - two)
+
+
+def window_kernel(first_ref, total1, total2, total3, second1, second2, second3, frames, out_ref):
+    others = tuple(zip(MASKS, (total1, total2, total3), (second1, second2, second3), strict=True))
+    for i in range(FR):
+        first = first_ref[i]
+        value = reached_part(first, 0, frames[0] + frames[1], frames[1])
+        for mask, both, second in others:
+            value = value + reached_part(first, mask, both[...], second[...])
+        out_ref[i] = (value * (first != 0).astype(jnp.float32)).astype(jnp.bfloat16)
+
+
 def early_kernel(first_ref, *refs):
-    parts, (near1, near2, frames, out_ref) = refs[:-4], refs[-4:]
-    device = lax.axis_index(TM)
-    before = [comes_before(axis, mask) for axis, mask in EARLY]
+    parts, refs = refs[: len(EARLY)], refs[len(EARLY) :]
+    totals, seconds, (window, frames, out_ref) = refs[:3], refs[3:6], refs[6:]
     prefix = None
-    for part, weight in zip(parts, before, strict=True):
-        term = part[...].astype(jnp.float32) * weight
+    for part, (axis, mask) in zip(parts, EARLY, strict=True):
+        term = part[...].astype(jnp.float32) * comes_before(axis, mask)
         prefix = term if prefix is None else prefix + term
+    later_row = (lax.axis_index(ROW) > 0).astype(jnp.float32)
     for i in range(FR):
         first = first_ref[i]
         value = prefix * (first == 0).astype(jnp.float32)
-        for offset, pair in ((1, near1), (2, near2)):
-            for j in range(FR):
-                source = (device - offset) * FR + j
-                reached = ((first != 0) & (first <= source)).astype(jnp.float32)
-                value = value + pair[j].astype(jnp.float32) * reached
+        value = value + window[i].astype(jnp.float32) * later_row
+        for mask, both, second in zip(MASKS, totals, seconds, strict=True):
+            part = reached_part(first, mask, both[...], second[...])
+            value = value + part * comes_before(X, mask)
         for j in range(i + 1):
-            reached = (first <= device * FR + j).astype(jnp.float32)
-            value = value + frames[j] * reached
+            value = value + frames[j] * (first <= row_source(0, j)).astype(jnp.float32)
         out_ref[i] = value
 
 
@@ -281,22 +301,27 @@
 def on_device(queries, key_vectors, value_vectors, out_weight, first_frame):
     own_queries = queries[0]
     other_queries = exchanged(own_queries, "cfg", 1)
-    frames, message, total = frame_states(key_vectors[0], value_vectors[0])
-    total, other_queries = lax.optimization_barrier((total, other_queries))
-
-    parts_x = [exchanged(total, X, m) for m in (1, 2, 3)]
+    next_first = shifted(first_frame, ROW, -1)
+    frames, total, second = frame_states(key_vectors[0], value_vectors[0])
+
+    parts_x = [exchanged(total, X, m) for m in MASKS]
     total = summed(total, parts_x)
+    total, other_queries, next_first = lax.optimization_barrier((total, other_queries, next_first))
+    seconds = [exchanged(second, X, m) for m in MASKS]
     total, later_queries, later_weight = lax.optimization_barrier((total, own_queries, out_weight.T))
     held_queries, half_weight = fetched(later_queries, later_weight)
     parts_z = [exchanged(total, Z, m) for m in (1, 2, 3)]
-    near = [shifted(message, TM, offset) for offset in range(1, NEAR + 1)]
+    window = small_call(
+        window_kernel, jnp.bfloat16, "window_mix", next_first, *parts_x, *seconds, frames
+    )
+    window = shifted(window, ROW, 1)
     total = summed(total, parts_z)
     total, held_queries, half_weight = lax.optimization_barrier((total, held_queries, half_weight))
     parts_w = [exchanged(total, Z, 7)]
     total = summed(total, parts_w)
     parts_y = [exchanged(total, Y, m) for m in (1, 2, 3)]
 
-    early = (*parts_x, *parts_z, *parts_w, *near, frames)
+    early = (*parts_z, *parts_w, *parts_x, *seconds, window, frames)
     base = small_call(early_kernel, jnp.float32, "early_mix", first_frame, *early)
     own_states = small_call(late_kernel, jnp.bfloat16, "late_mix", first_frame, base, *parts_y)
     other_states = exchanged(own_states, "cfg", 1)

time: 55 us -> 51.9 us (0.944)
  waiting for transfers between devices: 20.1 us -> 8.81 us
  starting transfers between devices: 22.7 us -> 29.9 us
  Pallas kernels: 11.8 us -> 12.7 us
    ppermute x12 -> x15, waiting for transfers between devices: 11.4 us -> 3.84 us  [exchanged(): return lax.ppermute(value, axis, pairs)]
    ppermute x2, starting transfers between devices: 2.62 us -> 6.37 us  [shifted(): lax.ppermute(value, axis, [(i, (i + steps) % count) for i in range(count)])]
    ppermute x2, waiting for transfers between devices: 8.72 us -> 4.97 us  [shifted(): lax.ppermute(value, axis, [(i, (i + steps) % count) for i in range(count)])]
    ppermute x12 -> x15, starting transfers between devices: 20.1 us -> 23.6 us  [exchanged(): return lax.ppermute(value, axis, pairs)]
    pallas_call x2 -> x3, Pallas kernels: 1.48 us -> 2.38 us  [small_call(): pl.pallas_call(kernel, out_shape=jax.ShapeDtypeStruct((FR, DH, PACKED), d...]
  transfers between devices with their start and end apart: 14 -> 17, of which waited for: 9 -> 5; matrix products, arithmetic and copies ran while one was open for 0% -> 0% of each run, Pallas kernels for 10% -> 13%
where the time goes in v3:
time: 51.9 us; the launch traced here: 51.8 us
  starting transfers between devices  29.9 us (58%)
  Pallas kernels  12.7 us (24%)
  waiting for transfers between devices  8.81 us (17%)
    ppermute x15, starting transfers between devices, exchanged(): return lax.ppermute(value, axis, pairs)  23.6 us
    ppermute x2, starting transfers between devices, shifted(): lax.ppermute(value, axis, [(i, (i + steps) % count) for i in range(count)])  6.37 us
    pallas_call x1, Pallas kernels, guided_columns(): pl.pallas_call(output_kernel, out_shape=jax.ShapeDtypeStruct((width, ROWS...  5.47 us
    ppermute x2, waiting for transfers between devices, shifted(): lax.ppermute(value, axis, [(i, (i + steps) % count) for i in range(count)])  4.97 us
    ppermute x15, waiting for transfers between devices, exchanged(): return lax.ppermute(value, axis, pairs)  3.84 us
    pallas_call x1, Pallas kernels, frame_states(): pl.pallas_call(state_kernel, out_shape=(jax.ShapeDtypeStruct((FR, DH, PAC...  2.58 us
    pallas_call x3, Pallas kernels, small_call(): pl.pallas_call(kernel, out_shape=jax.ShapeDtypeStruct((FR, DH, PACKED), d...  2.38 us
    pallas_call x1, Pallas kernels, fetched(): pl.pallas_call(fetch_kernel, out_shape=(jax.ShapeDtypeStruct(queries.shap...  2.28 us
  transfers between devices with their start and end apart: 17, of which 5 were waited for; matrix products, arithmetic and copies ran while one was open for 0% of the time, Pallas kernels for 13%

profile of v3, /device:TPU:1, one launch (start us, length us, event | category | flops | bytes accessed | tf_op | source)
XLA Modules:
  0.0 51.8 jit_solution(8989801362626943340)
XLA Ops:
  0.0 3.2 %collective-permute-start.3 = (bf16[768,1152]{1,0:T(8,128)(2,1)}, bf16[768,1152]{1,0:T(8,128)(2,1)S(1)}, u32[]{:S(2)}, u32[]{:S(2)}) collective-permute-start(bf16[768,1152]{1,0:T(8,128)(2,1)} %bitcast.8), channel_id=1, source_target_pairs={{0,128},{128,0},{1,129},{129,1},{2,130},{130,2},{3,131},{131,3},{4... | collective-permute-start | bytes 5308424 | tf_op jit(solution)/shard_map/ppermute | solution.py:287
  3.2 2.6 %frame_states.1 = (f32[2,32,1280]{2,1,0:T(8,128)S(1)}, bf16[32,1280]{1,0:T(8,128)(2,1)S(1)}, bf16[32,1280]{1,0:T(8,128)(2,1)S(1)}) custom-call(bf16[768,1152]{1,0:T(8,128)(2,1)} %bitcast.6, bf16[768,1152]{1,0:T(8,128)(2,1)} %bitcast.7), custom_call_target="tpu_custom_call" | custom-call | flops 452984832 | bytes 3538944 | tf_op jit(solution)/shard_map/frame_states/pallas_call | solution.py:83
  5.8 0.8 %collective-permute-start.2 = (bf16[32,1280]{1,0:T(8,128)(2,1)S(1)}, bf16[32,1280]{1,0:T(8,128)(2,1)S(1)}, u32[]{:S(2)}, u32[]{:S(2)}) collective-permute-start(bf16[32,1280]{1,0:T(8,128)(2,1)S(1)} %get-tuple-element.19), channel_id=1, source_target_pairs={{0,3},{1,2},{2,1},{3,0},{4,7},{5,6},{6,5},{7,4},{8,11},{9,10},{10,... | collective-permute-start | bytes 245768 | tf_op jit(solution)/shard_map/ppermute | solution.py:287
  6.7 0.5 %collective-permute-start.1 = (bf16[32,1280]{1,0:T(8,128)(2,1)S(1)}, bf16[32,1280]{1,0:T(8,128)(2,1)S(1)}, u32[]{:S(2)}, u32[]{:S(2)}) collective-permute-start(bf16[32,1280]{1,0:T(8,128)(2,1)S(1)} %get-tuple-element.19), channel_id=1, source_target_pairs={{0,2},{1,3},{2,0},{3,1},{4,6},{5,7},{6,4},{7,5},{8,10},{9,11},{10,... | collective-permute-start | bytes 245768 | tf_op jit(solution)/shard_map/ppermute | solution.py:287
  7.2 2.0 %collective-permute-start = (bf16[32,1280]{1,0:T(8,128)(2,1)S(1)}, bf16[32,1280]{1,0:T(8,128)(2,1)S(1)}, u32[]{:S(2)}, u32[]{:S(2)}) collective-permute-start(bf16[32,1280]{1,0:T(8,128)(2,1)S(1)} %get-tuple-element.19), channel_id=1, source_target_pairs={{0,1},{1,0},{2,3},{3,2},{4,5},{5,4},{6,7},{7,6},{8,9},{9,8},{10,11... | collective-permute-start | bytes 245768 | tf_op jit(solution)/shard_map/ppermute | solution.py:287
  9.2 6.3 %collective-permute-start.4 = (s32[2]{0:T(128)S(1)}, s32[2]{0:T(128)S(1)}, u32[]{:S(2)}, u32[]{:S(2)}) collective-permute-start(s32[2]{0:T(128)S(1)} %copy-done), channel_id=1, source_target_pairs={{0,124},{4,0},{8,4},{12,8},{16,12},{20,16},{24,20},{28,24},{32,28}... | collective-permute-start | bytes 32 | tf_op jit(solution)/shard_map/ppermute | solution.py:292
  15.5 0.7 %collective-permute-done.4.first_ref = s32[2]{0:T(128)S(1)} collective-permute-done((s32[2]{0:T(128)S(1)}, s32[2]{0:T(128)S(1)}, u32[]{:S(2)}, u32[]{:S(2)}) %collective-permute-start.4) | collective-permute-done | bytes 40 | tf_op jit(solution)/shard_map/ppermute | solution.py:292
  16.4 3.3 %collective-permute-start.5 = (bf16[32,1280]{1,0:T(8,128)(2,1)S(1)}, bf16[32,1280]{1,0:T(8,128)(2,1)S(1)}, u32[]{:S(2)}, u32[]{:S(2)}) collective-permute-start(bf16[32,1280]{1,0:T(8,128)(2,1)S(1)} %add_convert_fusion.2), channel_id=1, source_target_pairs={{0,4},{4,0},{8,12},{12,8},{16,20},{20,16},{24,28},{28,24},{1,5},{5... | collective-permute-start | bytes 245768 | tf_op jit(solution)/shard_map/ppermute | solution.py:287
  19.7 2.5 %collective-permute-start.11 = (bf16[32,1280]{1,0:T(8,128)(2,1)S(1)}, bf16[32,1280]{1,0:T(8,128)(2,1)S(1)}, u32[]{:S(2)}, u32[]{:S(2)}) collective-permute-start(bf16[32,1280]{1,0:T(8,128)(2,1)S(1)} %get-tuple-element.29), channel_id=1, source_target_pairs={{0,3},{1,2},{2,1},{3,0},{4,7},{5,6},{6,5},{7,4},{8,11},{9,10},{10,... | collective-permute-start | bytes 245768 | tf_op jit(solution)/shard_map/ppermute | solution.py:287
  22.2 0.5 %collective-permute-start.10 = (bf16[32,1280]{1,0:T(8,128)(2,1)S(1)}, bf16[32,1280]{1,0:T(8,128)(2,1)S(1)}, u32[]{:S(2)}, u32[]{:S(2)}) collective-permute-start(bf16[32,1280]{1,0:T(8,128)(2,1)S(1)} %get-tuple-element.29), channel_id=1, source_target_pairs={{0,2},{1,3},{2,0},{3,1},{4,6},{5,7},{6,4},{7,5},{8,10},{9,11},{10,... | collective-permute-start | bytes 245768 | tf_op jit(solution)/shard_map/ppermute | solution.py:287
  22.7 2.3 %fetch.1 = (bf16[768,1152]{1,0:T(8,128)(2,1)S(1)}, bf16[1120,1152]{1,0:T(8,128)(2,1)S(1)}) custom-call(bf16[768,1152]{1,0:T(8,128)(2,1)} %bitcast.9, bf16[2240,1152]{1,0:T(8,128)(2,1)} %bitcast.5), custom_call_target="tpu_custom_call" | custom-call | bytes 8699904 | tf_op jit(solution)/shard_map/fetch/pallas_call | solution.py:167
  25.0 0.3 collective-permute-start.9
  25.4 2.0 %collective-permute-start.8 = (bf16[32,1280]{1,0:T(8,128)(2,1)S(1)}, bf16[32,1280]{1,0:T(8,128)(2,1)S(1)}, u32[]{:S(2)}, u32[]{:S(2)}) collective-permute-start(bf16[32,1280]{1,0:T(8,128)(2,1)S(1)} %add_convert_fusion.1), channel_id=1, source_target_pairs={{0,28},{4,24},{8,20},{12,16},{16,12},{20,8},{24,4},{28,0},{1,29},{... | collective-permute-start | bytes 245768 | tf_op jit(solution)/shard_map/ppermute | solution.py:287
  27.4 1.6 %collective-permute-done.9.second1.refs_7_ = bf16[32,1280]{1,0:T(8,128)(2,1)S(1)} collective-permute-done((bf16[32,1280]{1,0:T(8,128)(2,1)S(1)}, bf16[32,1280]{1,0:T(8,128)(2,1)S(1)}, u32[]{:S(2)}, u32[]{:S(2)}) %collective-permute-start.9) | collective-permute-done | bytes 81952 | tf_op jit(solution)/shard_map/ppermute | solution.py:287
  29.0 0.8 %window_mix.1 = bf16[2,32,1280]{2,1,0:T(8,128)(2,1)S(1)} custom-call(s32[2]{0:T(128)S(1)} %collective-permute-done.4.first_ref, bf16[32,1280]{1,0:T(8,128)(2,1)S(1)} %collective-permute-done.total1.refs_4_, bf16[32,1280]{1,0:T(8,128)(2,1)S(1)} %collective-permute-done.1.total2.refs_5_, bf16[32,1280]{1,0:T(8,128)(2,1)S(1)} %collective-permute-done.2.total3.refs_6_, ...), custom_call_target="tpu_custom_call" | custom-call | flops 1146880 | bytes 1146880 | tf_op jit(solution)/shard_map/window_mix/pallas_call | solution.py:269
  29.9 1.2 %collective-permute-done.8.refs_3_ = bf16[32,1280]{1,0:T(8,128)(2,1)S(1)} collective-permute-done((bf16[32,1280]{1,0:T(8,128)(2,1)S(1)}, bf16[32,1280]{1,0:T(8,128)(2,1)S(1)}, u32[]{:S(2)}, u32[]{:S(2)}) %collective-permute-start.8) | collective-permute-done | bytes 81952 | tf_op jit(solution)/shard_map/ppermute | solution.py:287
  31.1 2.2 %collective-permute-start.15 = (bf16[32,1280]{1,0:T(8,128)(2,1)S(1)}, bf16[32,1280]{1,0:T(8,128)(2,1)S(1)}, u32[]{:S(2)}, u32[]{:S(2)}) collective-permute-start(bf16[32,1280]{1,0:T(8,128)(2,1)S(1)} %add_convert_fusion), channel_id=1, source_target_pairs={{0,96},{32,64},{64,32},{96,0},{1,97},{33,65},{65,33},{97,1},{2,98}... | collective-permute-start | bytes 245768 | tf_op jit(solution)/shard_map/ppermute | solution.py:287
  33.3 1.1 %collective-permute-start.13 = (bf16[32,1280]{1,0:T(8,128)(2,1)S(1)}, bf16[32,1280]{1,0:T(8,128)(2,1)S(1)}, u32[]{:S(2)}, u32[]{:S(2)}) collective-permute-start(bf16[32,1280]{1,0:T(8,128)(2,1)S(1)} %add_convert_fusion), channel_id=1, source_target_pairs={{0,32},{32,0},{64,96},{96,64},{1,33},{33,1},{65,97},{97,65},{2,34}... | collective-permute-start | bytes 245768 | tf_op jit(solution)/shard_map/ppermute | solution.py:287
  34.5 4.3 %collective-permute-done.12.refs_10_ = bf16[2,32,1280]{2,1,0:T(8,128)(2,1)S(1)} collective-permute-done((bf16[2,32,1280]{2,1,0:T(8,128)(2,1)S(1)}, bf16[2,32,1280]{2,1,0:T(8,128)(2,1)S(1)}, u32[]{:S(2)}, u32[]{:S(2)}) %collective-permute-start.12) | collective-permute-done | bytes 163872 | tf_op jit(solution)/shard_map/ppermute | solution.py:292
  38.8 0.9 %early_mix.1.base_ref = f32[2,32,1280]{2,1,0:T(8,128)S(1)} custom-call(s32[2]{0:T(128)S(1)} %copy-done, bf16[32,1280]{1,0:T(8,128)(2,1)S(1)} %collective-permute-done.5.refs_0_, bf16[32,1280]{1,0:T(8,128)(2,1)S(1)} %collective-permute-done.6.refs_1_, bf16[32,1280]{1,0:T(8,128)(2,1)S(1)} %collective-permute-done.7.refs_2_, ...), custom_call_target="tpu_custom_call" | custom-call | flops 1966080 | bytes 1966080 | tf_op jit(solution)/shard_map/early_mix/pallas_call | solution.py:269
  39.8 0.6 %late_mix.1.s0_ref = bf16[2,32,1280]{2,1,0:T(8,128)(2,1)S(1)} custom-call(s32[2]{0:T(128)S(1)} %copy-done, f32[2,32,1280]{2,1,0:T(8,128)S(1)} %early_mix.1.base_ref, bf16[32,1280]{1,0:T(8,128)(2,1)S(1)} %collective-permute-done.13.refs_0_, bf16[32,1280]{1,0:T(8,128)(2,1)S(1)} %collective-permute-done.14.refs_1_, ...), custom_call_target="tpu_custom_call" | custom-call | flops 655360 | bytes 655360 | tf_op jit(solution)/shard_map/late_mix/pallas_call | solution.py:269
  40.4 4.8 %collective-permute-start.16 = (bf16[2,32,1280]{2,1,0:T(8,128)(2,1)S(1)}, bf16[2,32,1280]{2,1,0:T(8,128)(2,1)S(1)}, u32[]{:S(2)}, u32[]{:S(2)}) collective-permute-start(bf16[2,32,1280]{2,1,0:T(8,128)(2,1)S(1)} %late_mix.1.s0_ref), channel_id=1, source_target_pairs={{0,128},{128,0},{1,129},{129,1},{2,130},{130,2},{3,131},{131,3},{4... | collective-permute-start | bytes 491528 | tf_op jit(solution)/shard_map/ppermute | solution.py:287
  45.2 1.0 %collective-permute-done.16.s1_ref = bf16[2,32,1280]{2,1,0:T(8,128)(2,1)S(1)} collective-permute-done((bf16[2,32,1280]{2,1,0:T(8,128)(2,1)S(1)}, bf16[2,32,1280]{2,1,0:T(8,128)(2,1)S(1)}, u32[]{:S(2)}, u32[]{:S(2)}) %collective-permute-start.16) | collective-permute-done | bytes 163872 | tf_op jit(solution)/shard_map/ppermute | solution.py:287
  46.2 5.5 %guided_columns.1 = bf16[1120,768]{1,0:T(8,128)(2,1)} custom-call(bf16[768,1152]{1,0:T(8,128)(2,1)S(1)} %get-tuple-element.26.q0_ref, bf16[768,1152]{1,0:T(8,128)(2,1)S(1)} %collective-permute-done.3.q1_ref, bf16[2,32,1280]{2,1,0:T(8,128)(2,1)S(1)} %late_mix.1.s0_ref, bf16[2,32,1280]{2,1,0:T(8,128)(2,1)S(1)} %collective-permute-done.16.s1_ref, ...), custom_call_target="tpu_custom_call" | custom-call | flops 2887778304 | bytes 7839744 | tf_op jit(solution)/shard_map/guided_columns/pallas_call | solution.py:188
  (21 shorter events, 0.5 us)
Async XLA Ops:
  0.0 16.2 %collective-permute-start.3 = (bf16[768,1152]{1,0:T(8,128)(2,1)}, bf16[768,1152]{1,0:T(8,128)(2,1)S(1)}, u32[]{:S(2)}, u32[]{:S(2)}) collective-permute-start(bf16[768,1152]{1,0:T(8,128)(2,1)} %bitcast.8), channel_id=1, source_target_pairs={{0,128},{128,0},{1,129},{129,1},{2,130},{130,2},{3,131},{131,3},{4... | collective-permute-start | bytes 5308424 | tf_op jit(solution)/shard_map/ppermute | solution.py:287
  3.2 5.9 %copy-start = (s32[2]{0:T(128)S(1)}, s32[2]{0:T(128)}, u32[]{:S(2)}) copy-start(s32[2]{0:T(128)} %first_ref.3) | copy-start | bytes 28
  5.8 9.6 %collective-permute-start.2 = (bf16[32,1280]{1,0:T(8,128)(2,1)S(1)}, bf16[32,1280]{1,0:T(8,128)(2,1)S(1)}, u32[]{:S(2)}, u32[]{:S(2)}) collective-permute-start(bf16[32,1280]{1,0:T(8,128)(2,1)S(1)} %get-tuple-element.19), channel_id=1, source_target_pairs={{0,3},{1,2},{2,1},{3,0},{4,7},{5,6},{6,5},{7,4},{8,11},{9,10},{10,... | collective-permute-start | bytes 245768 | tf_op jit(solution)/shard_map/ppermute | solution.py:287
  6.7 8.8 %collective-permute-start.1 = (bf16[32,1280]{1,0:T(8,128)(2,1)S(1)}, bf16[32,1280]{1,0:T(8,128)(2,1)S(1)}, u32[]{:S(2)}, u32[]{:S(2)}) collective-permute-start(bf16[32,1280]{1,0:T(8,128)(2,1)S(1)} %get-tuple-element.19), channel_id=1, source_target_pairs={{0,2},{1,3},{2,0},{3,1},{4,6},{5,7},{6,4},{7,5},{8,10},{9,11},{10,... | collective-permute-start | bytes 245768 | tf_op jit(solution)/shard_map/ppermute | solution.py:287
  7.2 8.3 %collective-permute-start = (bf16[32,1280]{1,0:T(8,128)(2,1)S(1)}, bf16[32,1280]{1,0:T(8,128)(2,1)S(1)}, u32[]{:S(2)}, u32[]{:S(2)}) collective-permute-start(bf16[32,1280]{1,0:T(8,128)(2,1)S(1)} %get-tuple-element.19), channel_id=1, source_target_pairs={{0,1},{1,0},{2,3},{3,2},{4,5},{5,4},{6,7},{7,6},{8,9},{9,8},{10,11... | collective-permute-start | bytes 245768 | tf_op jit(solution)/shard_map/ppermute | solution.py:287
  9.2 7.0 %collective-permute-start.4 = (s32[2]{0:T(128)S(1)}, s32[2]{0:T(128)S(1)}, u32[]{:S(2)}, u32[]{:S(2)}) collective-permute-start(s32[2]{0:T(128)S(1)} %copy-done), channel_id=1, source_target_pairs={{0,124},{4,0},{8,4},{12,8},{16,12},{20,16},{24,20},{28,24},{32,28}... | collective-permute-start | bytes 32 | tf_op jit(solution)/shard_map/ppermute | solution.py:292
  16.2 8.8 %collective-permute-start.7 = (bf16[32,1280]{1,0:T(8,128)(2,1)S(1)}, bf16[32,1280]{1,0:T(8,128)(2,1)S(1)}, u32[]{:S(2)}, u32[]{:S(2)}) collective-permute-start(bf16[32,1280]{1,0:T(8,128)(2,1)S(1)} %add_convert_fusion.2), channel_id=1, source_target_pairs={{0,12},{4,8},{8,4},{12,0},{16,28},{20,24},{24,20},{28,16},{1,13},{... | collective-permute-start | bytes 245768 | tf_op jit(solution)/shard_map/ppermute | solution.py:287
  16.4 9.0 %collective-permute-start.6 = (bf16[32,1280]{1,0:T(8,128)(2,1)S(1)}, bf16[32,1280]{1,0:T(8,128)(2,1)S(1)}, u32[]{:S(2)}, u32[]{:S(2)}) collective-permute-start(bf16[32,1280]{1,0:T(8,128)(2,1)S(1)} %add_convert_fusion.2), channel_id=1, source_target_pairs={{0,8},{4,12},{8,0},{12,4},{16,24},{20,28},{24,16},{28,20},{1,9},{5... | collective-permute-start | bytes 245768 | tf_op jit(solution)/shard_map/ppermute | solution.py:287
  16.4 9.0 %collective-permute-start.5 = (bf16[32,1280]{1,0:T(8,128)(2,1)S(1)}, bf16[32,1280]{1,0:T(8,128)(2,1)S(1)}, u32[]{:S(2)}, u32[]{:S(2)}) collective-permute-start(bf16[32,1280]{1,0:T(8,128)(2,1)S(1)} %add_convert_fusion.2), channel_id=1, source_target_pairs={{0,4},{4,0},{8,12},{12,8},{16,20},{20,16},{24,28},{28,24},{1,5},{5... | collective-permute-start | bytes 245768 | tf_op jit(solution)/shard_map/ppermute | solution.py:287
  19.7 7.7 %collective-permute-start.11 = (bf16[32,1280]{1,0:T(8,128)(2,1)S(1)}, bf16[32,1280]{1,0:T(8,128)(2,1)S(1)}, u32[]{:S(2)}, u32[]{:S(2)}) collective-permute-start(bf16[32,1280]{1,0:T(8,128)(2,1)S(1)} %get-tuple-element.29), channel_id=1, source_target_pairs={{0,3},{1,2},{2,1},{3,0},{4,7},{5,6},{6,5},{7,4},{8,11},{9,10},{10,... | collective-permute-start | bytes 245768 | tf_op jit(solution)/shard_map/ppermute | solution.py:287
  22.2 5.2 %collective-permute-start.10 = (bf16[32,1280]{1,0:T(8,128)(2,1)S(1)}, bf16[32,1280]{1,0:T(8,128)(2,1)S(1)}, u32[]{:S(2)}, u32[]{:S(2)}) collective-permute-start(bf16[32,1280]{1,0:T(8,128)(2,1)S(1)} %get-tuple-element.29), channel_id=1, source_target_pairs={{0,2},{1,3},{2,0},{3,1},{4,6},{5,7},{6,4},{7,5},{8,10},{9,11},{10,... | collective-permute-start | bytes 245768 | tf_op jit(solution)/shard_map/ppermute | solution.py:287
  25.0 3.9 %collective-permute-start.9 = (bf16[32,1280]{1,0:T(8,128)(2,1)S(1)}, bf16[32,1280]{1,0:T(8,128)(2,1)S(1)}, u32[]{:S(2)}, u32[]{:S(2)}) collective-permute-start(bf16[32,1280]{1,0:T(8,128)(2,1)S(1)} %get-tuple-element.29), channel_id=1, source_target_pairs={{0,1},{1,0},{2,3},{3,2},{4,5},{5,4},{6,7},{7,6},{8,9},{9,8},{10,11... | collective-permute-start | bytes 245768 | tf_op jit(solution)/shard_map/ppermute | solution.py:287
  25.4 5.7 %collective-permute-start.8 = (bf16[32,1280]{1,0:T(8,128)(2,1)S(1)}, bf16[32,1280]{1,0:T(8,128)(2,1)S(1)}, u32[]{:S(2)}, u32[]{:S(2)}) collective-permute-start(bf16[32,1280]{1,0:T(8,128)(2,1)S(1)} %add_convert_fusion.1), channel_id=1, source_target_pairs={{0,28},{4,24},{8,20},{12,16},{16,12},{20,8},{24,4},{28,0},{1,29},{... | collective-permute-start | bytes 245768 | tf_op jit(solution)/shard_map/ppermute | solution.py:287
  29.8 9.0 %collective-permute-start.12 = (bf16[2,32,1280]{2,1,0:T(8,128)(2,1)S(1)}, bf16[2,32,1280]{2,1,0:T(8,128)(2,1)S(1)}, u32[]{:S(2)}, u32[]{:S(2)}) collective-permute-start(bf16[2,32,1280]{2,1,0:T(8,128)(2,1)S(1)} %window_mix.1), channel_id=1, source_target_pairs={{0,4},{4,8},{8,12},{12,16},{16,20},{20,24},{24,28},{28,32},{32,36}... | collective-permute-start | bytes 491528 | tf_op jit(solution)/shard_map/ppermute | solution.py:292
  31.1 8.6 %collective-permute-start.15 = (bf16[32,1280]{1,0:T(8,128)(2,1)S(1)}, bf16[32,1280]{1,0:T(8,128)(2,1)S(1)}, u32[]{:S(2)}, u32[]{:S(2)}) collective-permute-start(bf16[32,1280]{1,0:T(8,128)(2,1)S(1)} %add_convert_fusion), channel_id=1, source_target_pairs={{0,96},{32,64},{64,32},{96,0},{1,97},{33,65},{65,33},{97,1},{2,98}... | collective-permute-start | bytes 245768 | tf_op jit(solution)/shard_map/ppermute | solution.py:287
  33.3 6.4 %collective-permute-start.14 = (bf16[32,1280]{1,0:T(8,128)(2,1)S(1)}, bf16[32,1280]{1,0:T(8,128)(2,1)S(1)}, u32[]{:S(2)}, u32[]{:S(2)}) collective-permute-start(bf16[32,1280]{1,0:T(8,128)(2,1)S(1)} %add_convert_fusion), channel_id=1, source_target_pairs={{0,64},{32,96},{64,0},{96,32},{1,65},{33,97},{65,1},{97,33},{2,66}... | collective-permute-start | bytes 245768 | tf_op jit(solution)/shard_map/ppermute | solution.py:287
  33.3 6.4 %collective-permute-start.13 = (bf16[32,1280]{1,0:T(8,128)(2,1)S(1)}, bf16[32,1280]{1,0:T(8,128)(2,1)S(1)}, u32[]{:S(2)}, u32[]{:S(2)}) collective-permute-start(bf16[32,1280]{1,0:T(8,128)(2,1)S(1)} %add_convert_fusion), channel_id=1, source_target_pairs={{0,32},{32,0},{64,96},{96,64},{1,33},{33,1},{65,97},{97,65},{2,34}... | collective-permute-start | bytes 245768 | tf_op jit(solution)/shard_map/ppermute | solution.py:287
  40.4 5.8 %collective-permute-start.16 = (bf16[2,32,1280]{2,1,0:T(8,128)(2,1)S(1)}, bf16[2,32,1280]{2,1,0:T(8,128)(2,1)S(1)}, u32[]{:S(2)}, u32[]{:S(2)}) collective-permute-start(bf16[2,32,1280]{2,1,0:T(8,128)(2,1)S(1)} %late_mix.1.s0_ref), channel_id=1, source_target_pairs={{0,128},{128,0},{1,129},{129,1},{2,130},{130,2},{3,131},{131,3},{4... | collective-permute-start | bytes 491528 | tf_op jit(solution)/shard_map/ppermute | solution.py:287

commit v4 on v3

--- a/solution.py
+++ b/solution.py
@@ -29,50 +29,40 @@
 
 
 def state_kernel(k_hbm, v_hbm, frames_ref, total_ref, second_ref, k_buf, v_buf, sems):
-    chunks = BLOCKS // 3
-    width = 3 * LANES
-
-    def copies(c):
-        columns = pl.ds(c * width, width)
+    def copies(f):
+        rows = pl.ds(f * FT, FT)
         return (
-            pltpu.make_async_copy(k_hbm.at[:, columns], k_buf.at[:, columns], sems.at[0, c]),
-            pltpu.make_async_copy(v_hbm.at[:, columns], v_buf.at[:, columns], sems.at[1, c]),
+            pltpu.make_async_copy(k_hbm.at[rows], k_buf.at[rows], sems.at[0, f]),
+            pltpu.make_async_copy(v_hbm.at[rows], v_buf.at[rows], sems.at[1, f]),
         )
 
-    for c in range(chunks):
-        for copy in copies(c):
+    for f in range(FR):
+        for copy in copies(f):
             copy.start()
     lane = lax.broadcasted_iota(jnp.int32, (DH, LANES), 1)
     ones = jnp.ones((FT, LANES), jnp.bfloat16)
-    sums = [jnp.zeros((DH, LANES), jnp.float32) for _ in range(FR)]
-    for c in range(chunks):
-        for copy in copies(c):
+    for f in range(FR):
+        rows = slice(f * FT, (f + 1) * FT)
+        for copy in copies(f):
             copy.wait()
-        for b in range(3 * c, 3 * c + 3):
+        sums = jnp.zeros((DH, LANES), jnp.float32)
+        for b in range(BLOCKS):
             columns = slice(b * LANES, (b + 1) * LANES)
-            states = []
-            for f in range(FR):
-                rows = slice(f * FT, (f + 1) * FT)
-                keys = jnp.maximum(k_buf[rows, columns], 0)
-                both = jnp.concatenate([v_buf[rows, columns], ones], axis=1)
-                outer = lax.dot_general(
-                    keys, both, (((0,), (0,)), ((), ())), preferred_element_type=jnp.float32
-                )
-                state = jnp.zeros((DH, LANES), jnp.float32)
-                for h in range(HEADS_PER_BLOCK):
-                    piece = outer[h * DH : (h + 1) * DH]
-                    state = jnp.where(lane // DH == h, piece[:, :LANES], state)
-                    sums[f] = jnp.where(
-                        lane == b * HEADS_PER_BLOCK + h, piece[:, LANES:], sums[f]
-                    )
-                frames_ref[f, :, columns] = state
-                states.append(state)
-            total_ref[:, columns] = (states[0] + states[1]).astype(jnp.bfloat16)
-            second_ref[:, columns] = states[1].astype(jnp.bfloat16)
-    for f in range(FR):
-        frames_ref[f, :, HD:] = sums[f]
-    total_ref[:, HD:] = (sums[0] + sums[1]).astype(jnp.bfloat16)
-    second_ref[:, HD:] = sums[1].astype(jnp.bfloat16)
+            keys = jnp.maximum(k_buf[rows, columns], 0)
+            both = jnp.concatenate([v_buf[rows, columns], ones], axis=1)
+            outer = lax.dot_general(
+                keys, both, (((0,), (0,)), ((), ())), preferred_element_type=jnp.float32
+            )
+            state = jnp.zeros((DH, LANES), jnp.float32)
+            for h in range(HEADS_PER_BLOCK):
+                piece = outer[h * DH : (h + 1) * DH]
+                state = jnp.where(lane // DH == h, piece[:, :LANES], state)
+                sums = jnp.where(lane == b * HEADS_PER_BLOCK + h, piece[:, LANES:], sums)
+            frames_ref[f, :, columns] = state
+        frames_ref[f, :, HD:] = sums
+    second = frames_ref[FR - 1]
+    second_ref[...] = second.astype(jnp.bfloat16)
+    total_ref[...] = (frames_ref[0] + second).astype(jnp.bfloat16)
 
 
 def in_hbm(value):
@@ -92,7 +82,7 @@
         scratch_shapes=[
             pltpu.VMEM((ROWS, HD), jnp.bfloat16),
             pltpu.VMEM((ROWS, HD), jnp.bfloat16),
-            pltpu.SemaphoreType.DMA((2, 3)),
+            pltpu.SemaphoreType.DMA((2, FR)),
         ],
         compiler_params=pltpu.CompilerParams(vmem_limit_bytes=VMEM_LIMIT),
         cost_estimate=pl.CostEstimate(
@@ -149,36 +139,28 @@
         out_copy(c).wait()
 
 
-def fetch_kernel(q_hbm, w_hbm, q_ref, w_ref, sems):
+def fetch_kernel(w_hbm, w_ref, sem):
     width = w_ref.shape[0]
     start = pl.multiple_of(lax.axis_index("cfg") * width, 16)
-    copies = (
-        pltpu.make_async_copy(q_hbm, q_ref, sems.at[0]),
-        pltpu.make_async_copy(w_hbm.at[pl.ds(start, width)], w_ref, sems.at[1]),
-    )
-    for copy in copies:
-        copy.start()
-    for copy in copies:
-        copy.wait()
-
-
-def fetched(queries, weight):
+    copy = pltpu.make_async_copy(w_hbm.at[pl.ds(start, width)], w_ref, sem)
+    copy.start()
+    copy.wait()
+
+
+def fetched(weight):
     width = weight.shape[0] // 2
     return pl.pallas_call(
         fetch_kernel,
-        out_shape=(
-            jax.ShapeDtypeStruct(queries.shape, queries.dtype),
-            jax.ShapeDtypeStruct((width, weight.shape[1]), weight.dtype),
-        ),
-        in_specs=[pl.BlockSpec(memory_space=pltpu.HBM)] * 2,
-        out_specs=(pl.BlockSpec(memory_space=pltpu.VMEM),) * 2,
-        scratch_shapes=[pltpu.SemaphoreType.DMA((2,))],
+        out_shape=jax.ShapeDtypeStruct((width, weight.shape[1]), weight.dtype),
+        in_specs=[pl.BlockSpec(memory_space=pltpu.HBM)],
+        out_specs=pl.BlockSpec(memory_space=pltpu.VMEM),
+        scratch_shapes=[pltpu.SemaphoreType.DMA],
         compiler_params=pltpu.CompilerParams(vmem_limit_bytes=2 << 20),
         cost_estimate=pl.CostEstimate(
-            flops=0, bytes_accessed=4 * (queries.size + weight.size // 2), transcendentals=0
+            flops=0, bytes_accessed=2 * weight.size, transcendentals=0
         ),
         name="fetch",
-    )(in_hbm(queries), in_hbm(weight))
+    )(in_hbm(weight))
 
 
 def guided_columns(own_queries, other_queries, own_states, other_states, weight):
@@ -308,25 +290,25 @@
     total = summed(total, parts_x)
     total, other_queries, next_first = lax.optimization_barrier((total, other_queries, next_first))
     seconds = [exchanged(second, X, m) for m in MASKS]
-    total, later_queries, later_weight = lax.optimization_barrier((total, own_queries, out_weight.T))
-    held_queries, half_weight = fetched(later_queries, later_weight)
     parts_z = [exchanged(total, Z, m) for m in (1, 2, 3)]
     window = small_call(
         window_kernel, jnp.bfloat16, "window_mix", next_first, *parts_x, *seconds, frames
     )
     window = shifted(window, ROW, 1)
     total = summed(total, parts_z)
-    total, held_queries, half_weight = lax.optimization_barrier((total, held_queries, half_weight))
     parts_w = [exchanged(total, Z, 7)]
     total = summed(total, parts_w)
+    total, later_weight = lax.optimization_barrier((total, out_weight.T))
+    half_weight = fetched(later_weight)
     parts_y = [exchanged(total, Y, m) for m in (1, 2, 3)]
 
     early = (*parts_z, *parts_w, *parts_x, *seconds, window, frames)
     base = small_call(early_kernel, jnp.float32, "early_mix", first_frame, *early)
+    base, half_weight = lax.optimization_barrier((base, half_weight))
     own_states = small_call(late_kernel, jnp.bfloat16, "late_mix", first_frame, base, *parts_y)
     other_states = exchanged(own_states, "cfg", 1)
     return guided_columns(
-        held_queries, other_queries, own_states, other_states, half_weight
+        own_queries, other_queries, own_states, other_states, half_weight
     ).T
 
 

time: 51.9 us -> 50.2 us (0.967)
  waiting for transfers between devices: 8.81 us -> 5.91 us
  starting transfers between devices: 29.9 us -> 31.7 us
  Pallas kernels: 12.7 us -> 12.1 us
    ppermute x2, waiting for transfers between devices: 4.97 us -> 1.5 us  [shifted(): lax.ppermute(value, axis, [(i, (i + steps) % count) for i in range(count)])]
    ppermute x15, starting transfers between devices: 23.6 us -> 25.3 us  [exchanged(): return lax.ppermute(value, axis, pairs)]
    ppermute x15, waiting for transfers between devices: 3.84 us -> 4.4 us  [exchanged(): return lax.ppermute(value, axis, pairs)]
    pallas_call x1, Pallas kernels: 2.28 us -> 1.74 us  [fetched(): pl.pallas_call(fetch_kernel, out_shape=jax.ShapeDtypeStruct((width, weigh...]
  transfers between devices with their start and end apart: 17 -> 17, of which waited for: 5 -> 5; matrix products, arithmetic and copies ran while one was open for 0% -> 0% of each run, Pallas kernels for 13% -> 12%
where the time goes in v4:
time: 50.2 us; the launch traced here: 50.1 us
  starting transfers between devices  31.7 us (63%)
  Pallas kernels  12.1 us (24%)
  waiting for transfers between devices  5.91 us (12%)
    ppermute x15, starting transfers between devices, exchanged(): return lax.ppermute(value, axis, pairs)  25.3 us
    ppermute x2, starting transfers between devices, shifted(): lax.ppermute(value, axis, [(i, (i + steps) % count) for i in range(count)])  6.38 us
    pallas_call x1, Pallas kernels, guided_columns(): pl.pallas_call(output_kernel, out_shape=jax.ShapeDtypeStruct((width, ROWS...  5.47 us
    ppermute x15, waiting for transfers between devices, exchanged(): return lax.ppermute(value, axis, pairs)  4.4 us
    pallas_call x1, Pallas kernels, frame_states(): pl.pallas_call(state_kernel, out_shape=(jax.ShapeDtypeStruct((FR, DH, PAC...  2.54 us
    pallas_call x3, Pallas kernels, small_call(): pl.pallas_call(kernel, out_shape=jax.ShapeDtypeStruct((FR, DH, PACKED), d...  2.39 us
    pallas_call x1, Pallas kernels, fetched(): pl.pallas_call(fetch_kernel, out_shape=jax.ShapeDtypeStruct((width, weigh...  1.74 us
    ppermute x2, waiting for transfers between devices, shifted(): lax.ppermute(value, axis, [(i, (i + steps) % count) for i in range(count)])  1.5 us
  transfers between devices with their start and end apart: 17, of which 5 were waited for; matrix products, arithmetic and copies ran while one was open for 0% of the time, Pallas kernels for 12%

profile of v4, /device:TPU:1, one launch (start us, length us, event | category | flops | bytes accessed | tf_op | source)
XLA Modules:
  0.0 50.1 jit_solution(2459329996727042782)
XLA Ops:
  0.0 3.2 %collective-permute-start.3 = (bf16[768,1152]{1,0:T(8,128)(2,1)}, bf16[768,1152]{1,0:T(8,128)(2,1)S(1)}, u32[]{:S(2)}, u32[]{:S(2)}) collective-permute-start(bf16[768,1152]{1,0:T(8,128)(2,1)} %bitcast.5), channel_id=1, source_target_pairs={{0,128},{128,0},{1,129},{129,1},{2,130},{130,2},{3,131},{131,3},{4... | collective-permute-start | bytes 5308424 | tf_op jit(solution)/shard_map/ppermute | solution.py:269
  3.2 2.5 %frame_states.1 = (f32[2,32,1280]{2,1,0:T(8,128)S(1)}, bf16[32,1280]{1,0:T(8,128)(2,1)S(1)}, bf16[32,1280]{1,0:T(8,128)(2,1)S(1)}) custom-call(bf16[768,1152]{1,0:T(8,128)(2,1)} %bitcast.8, bf16[768,1152]{1,0:T(8,128)(2,1)} %bitcast.9), custom_call_target="tpu_custom_call" | custom-call | flops 452984832 | bytes 3538944 | tf_op jit(solution)/shard_map/frame_states/pallas_call | solution.py:73
  5.8 0.8 %collective-permute-start.2 = (bf16[32,1280]{1,0:T(8,128)(2,1)S(1)}, bf16[32,1280]{1,0:T(8,128)(2,1)S(1)}, u32[]{:S(2)}, u32[]{:S(2)}) collective-permute-start(bf16[32,1280]{1,0:T(8,128)(2,1)S(1)} %get-tuple-element.15), channel_id=1, source_target_pairs={{0,3},{1,2},{2,1},{3,0},{4,7},{5,6},{6,5},{7,4},{8,11},{9,10},{10,... | collective-permute-start | bytes 245768 | tf_op jit(solution)/shard_map/ppermute | solution.py:269
  6.6 0.5 %collective-permute-start.1 = (bf16[32,1280]{1,0:T(8,128)(2,1)S(1)}, bf16[32,1280]{1,0:T(8,128)(2,1)S(1)}, u32[]{:S(2)}, u32[]{:S(2)}) collective-permute-start(bf16[32,1280]{1,0:T(8,128)(2,1)S(1)} %get-tuple-element.15), channel_id=1, source_target_pairs={{0,2},{1,3},{2,0},{3,1},{4,6},{5,7},{6,4},{7,5},{8,10},{9,11},{10,... | collective-permute-start | bytes 245768 | tf_op jit(solution)/shard_map/ppermute | solution.py:269
  7.1 2.0 %collective-permute-start = (bf16[32,1280]{1,0:T(8,128)(2,1)S(1)}, bf16[32,1280]{1,0:T(8,128)(2,1)S(1)}, u32[]{:S(2)}, u32[]{:S(2)}) collective-permute-start(bf16[32,1280]{1,0:T(8,128)(2,1)S(1)} %get-tuple-element.15), channel_id=1, source_target_pairs={{0,1},{1,0},{2,3},{3,2},{4,5},{5,4},{6,7},{7,6},{8,9},{9,8},{10,11... | collective-permute-start | bytes 245768 | tf_op jit(solution)/shard_map/ppermute | solution.py:269
  9.1 6.3 %collective-permute-start.4 = (s32[2]{0:T(128)S(1)}, s32[2]{0:T(128)S(1)}, u32[]{:S(2)}, u32[]{:S(2)}) collective-permute-start(s32[2]{0:T(128)S(1)} %copy-done), channel_id=1, source_target_pairs={{0,124},{4,0},{8,4},{12,8},{16,12},{20,16},{24,20},{28,24},{32,28}... | collective-permute-start | bytes 32 | tf_op jit(solution)/shard_map/ppermute | solution.py:274
  15.5 0.7 %collective-permute-done.4.first_ref = s32[2]{0:T(128)S(1)} collective-permute-done((s32[2]{0:T(128)S(1)}, s32[2]{0:T(128)S(1)}, u32[]{:S(2)}, u32[]{:S(2)}) %collective-permute-start.4) | collective-permute-done | bytes 40 | tf_op jit(solution)/shard_map/ppermute | solution.py:274
  16.4 3.3 %collective-permute-start.5 = (bf16[32,1280]{1,0:T(8,128)(2,1)S(1)}, bf16[32,1280]{1,0:T(8,128)(2,1)S(1)}, u32[]{:S(2)}, u32[]{:S(2)}) collective-permute-start(bf16[32,1280]{1,0:T(8,128)(2,1)S(1)} %add_convert_fusion.2), channel_id=1, source_target_pairs={{0,4},{4,0},{8,12},{12,8},{16,20},{20,16},{24,28},{28,24},{1,5},{5... | collective-permute-start | bytes 245768 | tf_op jit(solution)/shard_map/ppermute | solution.py:269
  19.7 2.5 %collective-permute-start.11 = (bf16[32,1280]{1,0:T(8,128)(2,1)S(1)}, bf16[32,1280]{1,0:T(8,128)(2,1)S(1)}, u32[]{:S(2)}, u32[]{:S(2)}) collective-permute-start(bf16[32,1280]{1,0:T(8,128)(2,1)S(1)} %get-tuple-element.18), channel_id=1, source_target_pairs={{0,3},{1,2},{2,1},{3,0},{4,7},{5,6},{6,5},{7,4},{8,11},{9,10},{10,... | collective-permute-start | bytes 245768 | tf_op jit(solution)/shard_map/ppermute | solution.py:269
  22.2 0.5 %collective-permute-start.10 = (bf16[32,1280]{1,0:T(8,128)(2,1)S(1)}, bf16[32,1280]{1,0:T(8,128)(2,1)S(1)}, u32[]{:S(2)}, u32[]{:S(2)}) collective-permute-start(bf16[32,1280]{1,0:T(8,128)(2,1)S(1)} %get-tuple-element.18), channel_id=1, source_target_pairs={{0,2},{1,3},{2,0},{3,1},{4,6},{5,7},{6,4},{7,5},{8,10},{9,11},{10,... | collective-permute-start | bytes 245768 | tf_op jit(solution)/shard_map/ppermute | solution.py:269
  22.7 0.3 collective-permute-start.9
  23.0 4.4 %collective-permute-start.8 = (bf16[32,1280]{1,0:T(8,128)(2,1)S(1)}, bf16[32,1280]{1,0:T(8,128)(2,1)S(1)}, u32[]{:S(2)}, u32[]{:S(2)}) collective-permute-start(bf16[32,1280]{1,0:T(8,128)(2,1)S(1)} %add_convert_fusion.1), channel_id=1, source_target_pairs={{0,28},{4,24},{8,20},{12,16},{16,12},{20,8},{24,4},{28,0},{1,29},{... | collective-permute-start | bytes 245768 | tf_op jit(solution)/shard_map/ppermute | solution.py:269
  27.4 0.8 %window_mix.1 = bf16[2,32,1280]{2,1,0:T(8,128)(2,1)S(1)} custom-call(s32[2]{0:T(128)S(1)} %collective-permute-done.4.first_ref, bf16[32,1280]{1,0:T(8,128)(2,1)S(1)} %collective-permute-done.total1.refs_4_, bf16[32,1280]{1,0:T(8,128)(2,1)S(1)} %collective-permute-done.1.total2.refs_5_, bf16[32,1280]{1,0:T(8,128)(2,1)S(1)} %collective-permute-done.2.total3.refs_6_, ...), custom_call_target="tpu_custom_call" | custom-call | flops 1146880 | bytes 1146880 | tf_op jit(solution)/shard_map/window_mix/pallas_call | solution.py:251
  28.3 1.9 %collective-permute-done.8.refs_3_ = bf16[32,1280]{1,0:T(8,128)(2,1)S(1)} collective-permute-done((bf16[32,1280]{1,0:T(8,128)(2,1)S(1)}, bf16[32,1280]{1,0:T(8,128)(2,1)S(1)}, u32[]{:S(2)}, u32[]{:S(2)}) %collective-permute-start.8) | collective-permute-done | bytes 81952 | tf_op jit(solution)/shard_map/ppermute | solution.py:269
  30.2 2.7 %collective-permute-start.15 = (bf16[32,1280]{1,0:T(8,128)(2,1)S(1)}, bf16[32,1280]{1,0:T(8,128)(2,1)S(1)}, u32[]{:S(2)}, u32[]{:S(2)}) collective-permute-start(bf16[32,1280]{1,0:T(8,128)(2,1)S(1)} %add_convert_fusion), channel_id=1, source_target_pairs={{0,96},{32,64},{64,32},{96,0},{1,97},{33,65},{65,33},{97,1},{2,98}... | collective-permute-start | bytes 245768 | tf_op jit(solution)/shard_map/ppermute | solution.py:269
  33.0 0.7 %collective-permute-start.13 = (bf16[32,1280]{1,0:T(8,128)(2,1)S(1)}, bf16[32,1280]{1,0:T(8,128)(2,1)S(1)}, u32[]{:S(2)}, u32[]{:S(2)}) collective-permute-start(bf16[32,1280]{1,0:T(8,128)(2,1)S(1)} %add_convert_fusion), channel_id=1, source_target_pairs={{0,32},{32,0},{64,96},{96,64},{1,33},{33,1},{65,97},{97,65},{2,34}... | collective-permute-start | bytes 245768 | tf_op jit(solution)/shard_map/ppermute | solution.py:269
  33.6 1.7 %fetch.1.w_ref = bf16[1120,1152]{1,0:T(8,128)(2,1)S(1)} custom-call(bf16[2240,1152]{1,0:T(8,128)(2,1)} %bitcast.7), custom_call_target="tpu_custom_call" | custom-call | bytes 5160960 | tf_op jit(solution)/shard_map/fetch/pallas_call | solution.py:152
  35.4 0.8 %collective-permute-done.12.refs_10_ = bf16[2,32,1280]{2,1,0:T(8,128)(2,1)S(1)} collective-permute-done((bf16[2,32,1280]{2,1,0:T(8,128)(2,1)S(1)}, bf16[2,32,1280]{2,1,0:T(8,128)(2,1)S(1)}, u32[]{:S(2)}, u32[]{:S(2)}) %collective-permute-start.12) | collective-permute-done | bytes 163872 | tf_op jit(solution)/shard_map/ppermute | solution.py:274
  36.2 0.9 %early_mix.1.base_ref = f32[2,32,1280]{2,1,0:T(8,128)S(1)} custom-call(s32[2]{0:T(128)S(1)} %copy-done, bf16[32,1280]{1,0:T(8,128)(2,1)S(1)} %collective-permute-done.5.refs_0_, bf16[32,1280]{1,0:T(8,128)(2,1)S(1)} %collective-permute-done.6.refs_1_, bf16[32,1280]{1,0:T(8,128)(2,1)S(1)} %collective-permute-done.7.refs_2_, ...), custom_call_target="tpu_custom_call" | custom-call | flops 1966080 | bytes 1966080 | tf_op jit(solution)/shard_map/early_mix/pallas_call | solution.py:251
  37.2 1.4 %collective-permute-done.14.refs_1_ = bf16[32,1280]{1,0:T(8,128)(2,1)S(1)} collective-permute-done((bf16[32,1280]{1,0:T(8,128)(2,1)S(1)}, bf16[32,1280]{1,0:T(8,128)(2,1)S(1)}, u32[]{:S(2)}, u32[]{:S(2)}) %collective-permute-start.14) | collective-permute-done | bytes 81952 | tf_op jit(solution)/shard_map/ppermute | solution.py:269
  38.6 0.6 %late_mix.1.s0_ref = bf16[2,32,1280]{2,1,0:T(8,128)(2,1)S(1)} custom-call(s32[2]{0:T(128)S(1)} %copy-done, f32[2,32,1280]{2,1,0:T(8,128)S(1)} %early_mix.1.base_ref, bf16[32,1280]{1,0:T(8,128)(2,1)S(1)} %collective-permute-done.13.refs_0_, bf16[32,1280]{1,0:T(8,128)(2,1)S(1)} %collective-permute-done.14.refs_1_, ...), custom_call_target="tpu_custom_call" | custom-call | flops 655360 | bytes 655360 | tf_op jit(solution)/shard_map/late_mix/pallas_call | solution.py:251
  39.3 4.2 %collective-permute-start.16 = (bf16[2,32,1280]{2,1,0:T(8,128)(2,1)S(1)}, bf16[2,32,1280]{2,1,0:T(8,128)(2,1)S(1)}, u32[]{:S(2)}, u32[]{:S(2)}) collective-permute-start(bf16[2,32,1280]{2,1,0:T(8,128)(2,1)S(1)} %late_mix.1.s0_ref), channel_id=1, source_target_pairs={{0,128},{128,0},{1,129},{129,1},{2,130},{130,2},{3,131},{131,3},{4... | collective-permute-start | bytes 491528 | tf_op jit(solution)/shard_map/ppermute | solution.py:269
  43.4 1.0 %collective-permute-done.16.s1_ref = bf16[2,32,1280]{2,1,0:T(8,128)(2,1)S(1)} collective-permute-done((bf16[2,32,1280]{2,1,0:T(8,128)(2,1)S(1)}, bf16[2,32,1280]{2,1,0:T(8,128)(2,1)S(1)}, u32[]{:S(2)}, u32[]{:S(2)}) %collective-permute-start.16) | collective-permute-done | bytes 163872 | tf_op jit(solution)/shard_map/ppermute | solution.py:269
  44.5 5.5 %guided_columns.1 = bf16[1120,768]{1,0:T(8,128)(2,1)} custom-call(bf16[768,1152]{1,0:T(8,128)(2,1)S(1)} %bitcast.6, bf16[768,1152]{1,0:T(8,128)(2,1)S(1)} %collective-permute-done.3.q1_ref, bf16[2,32,1280]{2,1,0:T(8,128)(2,1)S(1)} %late_mix.1.s0_ref, bf16[2,32,1280]{2,1,0:T(8,128)(2,1)S(1)} %collective-permute-done.16.s1_ref, bf16[1120,1152]{1,0:T(8,128)(2,1)S(1)} %fetch.1.w_ref), custom_call_target="tpu_custom_call" | custom-call | flops 2887778304 | bytes 7839744 | tf_op jit(solution)/shard_map/guided_columns/pallas_call | solution.py:170
  (23 shorter events, 0.5 us)
Async XLA Ops:
  0.0 16.2 %collective-permute-start.3 = (bf16[768,1152]{1,0:T(8,128)(2,1)}, bf16[768,1152]{1,0:T(8,128)(2,1)S(1)}, u32[]{:S(2)}, u32[]{:S(2)}) collective-permute-start(bf16[768,1152]{1,0:T(8,128)(2,1)} %bitcast.5), channel_id=1, source_target_pairs={{0,128},{128,0},{1,129},{129,1},{2,130},{130,2},{3,131},{131,3},{4... | collective-permute-start | bytes 5308424 | tf_op jit(solution)/shard_map/ppermute | solution.py:269
  3.2 5.9 %copy-start = (s32[2]{0:T(128)S(1)}, s32[2]{0:T(128)}, u32[]{:S(2)}) copy-start(s32[2]{0:T(128)} %first_ref.3) | copy-start | bytes 28
  5.8 9.6 %collective-permute-start.2 = (bf16[32,1280]{1,0:T(8,128)(2,1)S(1)}, bf16[32,1280]{1,0:T(8,128)(2,1)S(1)}, u32[]{:S(2)}, u32[]{:S(2)}) collective-permute-start(bf16[32,1280]{1,0:T(8,128)(2,1)S(1)} %get-tuple-element.15), channel_id=1, source_target_pairs={{0,3},{1,2},{2,1},{3,0},{4,7},{5,6},{6,5},{7,4},{8,11},{9,10},{10,... | collective-permute-start | bytes 245768 | tf_op jit(solution)/shard_map/ppermute | solution.py:269
  6.6 8.8 %collective-permute-start.1 = (bf16[32,1280]{1,0:T(8,128)(2,1)S(1)}, bf16[32,1280]{1,0:T(8,128)(2,1)S(1)}, u32[]{:S(2)}, u32[]{:S(2)}) collective-permute-start(bf16[32,1280]{1,0:T(8,128)(2,1)S(1)} %get-tuple-element.15), channel_id=1, source_target_pairs={{0,2},{1,3},{2,0},{3,1},{4,6},{5,7},{6,4},{7,5},{8,10},{9,11},{10,... | collective-permute-start | bytes 245768 | tf_op jit(solution)/shard_map/ppermute | solution.py:269
  7.1 8.3 %collective-permute-start = (bf16[32,1280]{1,0:T(8,128)(2,1)S(1)}, bf16[32,1280]{1,0:T(8,128)(2,1)S(1)}, u32[]{:S(2)}, u32[]{:S(2)}) collective-permute-start(bf16[32,1280]{1,0:T(8,128)(2,1)S(1)} %get-tuple-element.15), channel_id=1, source_target_pairs={{0,1},{1,0},{2,3},{3,2},{4,5},{5,4},{6,7},{7,6},{8,9},{9,8},{10,11... | collective-permute-start | bytes 245768 | tf_op jit(solution)/shard_map/ppermute | solution.py:269
  9.1 7.0 %collective-permute-start.4 = (s32[2]{0:T(128)S(1)}, s32[2]{0:T(128)S(1)}, u32[]{:S(2)}, u32[]{:S(2)}) collective-permute-start(s32[2]{0:T(128)S(1)} %copy-done), channel_id=1, source_target_pairs={{0,124},{4,0},{8,4},{12,8},{16,12},{20,16},{24,20},{28,24},{32,28}... | collective-permute-start | bytes 32 | tf_op jit(solution)/shard_map/ppermute | solution.py:274
  16.2 6.5 %collective-permute-start.7 = (bf16[32,1280]{1,0:T(8,128)(2,1)S(1)}, bf16[32,1280]{1,0:T(8,128)(2,1)S(1)}, u32[]{:S(2)}, u32[]{:S(2)}) collective-permute-start(bf16[32,1280]{1,0:T(8,128)(2,1)S(1)} %add_convert_fusion.2), channel_id=1, source_target_pairs={{0,12},{4,8},{8,4},{12,0},{16,28},{20,24},{24,20},{28,16},{1,13},{... | collective-permute-start | bytes 245768 | tf_op jit(solution)/shard_map/ppermute | solution.py:269
  16.4 6.6 %collective-permute-start.6 = (bf16[32,1280]{1,0:T(8,128)(2,1)S(1)}, bf16[32,1280]{1,0:T(8,128)(2,1)S(1)}, u32[]{:S(2)}, u32[]{:S(2)}) collective-permute-start(bf16[32,1280]{1,0:T(8,128)(2,1)S(1)} %add_convert_fusion.2), channel_id=1, source_target_pairs={{0,8},{4,12},{8,0},{12,4},{16,24},{20,28},{24,16},{28,20},{1,9},{5... | collective-permute-start | bytes 245768 | tf_op jit(solution)/shard_map/ppermute | solution.py:269
  16.4 6.6 %collective-permute-start.5 = (bf16[32,1280]{1,0:T(8,128)(2,1)S(1)}, bf16[32,1280]{1,0:T(8,128)(2,1)S(1)}, u32[]{:S(2)}, u32[]{:S(2)}) collective-permute-start(bf16[32,1280]{1,0:T(8,128)(2,1)S(1)} %add_convert_fusion.2), channel_id=1, source_target_pairs={{0,4},{4,0},{8,12},{12,8},{16,20},{20,16},{24,28},{28,24},{1,5},{5... | collective-permute-start | bytes 245768 | tf_op jit(solution)/shard_map/ppermute | solution.py:269
  19.7 7.7 %collective-permute-start.11 = (bf16[32,1280]{1,0:T(8,128)(2,1)S(1)}, bf16[32,1280]{1,0:T(8,128)(2,1)S(1)}, u32[]{:S(2)}, u32[]{:S(2)}) collective-permute-start(bf16[32,1280]{1,0:T(8,128)(2,1)S(1)} %get-tuple-element.18), channel_id=1, source_target_pairs={{0,3},{1,2},{2,1},{3,0},{4,7},{5,6},{6,5},{7,4},{8,11},{9,10},{10,... | collective-permute-start | bytes 245768 | tf_op jit(solution)/shard_map/ppermute | solution.py:269
  22.2 5.2 %collective-permute-start.10 = (bf16[32,1280]{1,0:T(8,128)(2,1)S(1)}, bf16[32,1280]{1,0:T(8,128)(2,1)S(1)}, u32[]{:S(2)}, u32[]{:S(2)}) collective-permute-start(bf16[32,1280]{1,0:T(8,128)(2,1)S(1)} %get-tuple-element.18), channel_id=1, source_target_pairs={{0,2},{1,3},{2,0},{3,1},{4,6},{5,7},{6,4},{7,5},{8,10},{9,11},{10,... | collective-permute-start | bytes 245768 | tf_op jit(solution)/shard_map/ppermute | solution.py:269
  22.7 4.7 %collective-permute-start.9 = (bf16[32,1280]{1,0:T(8,128)(2,1)S(1)}, bf16[32,1280]{1,0:T(8,128)(2,1)S(1)}, u32[]{:S(2)}, u32[]{:S(2)}) collective-permute-start(bf16[32,1280]{1,0:T(8,128)(2,1)S(1)} %get-tuple-element.18), channel_id=1, source_target_pairs={{0,1},{1,0},{2,3},{3,2},{4,5},{5,4},{6,7},{7,6},{8,9},{9,8},{10,11... | collective-permute-start | bytes 245768 | tf_op jit(solution)/shard_map/ppermute | solution.py:269
  23.0 7.2 %collective-permute-start.8 = (bf16[32,1280]{1,0:T(8,128)(2,1)S(1)}, bf16[32,1280]{1,0:T(8,128)(2,1)S(1)}, u32[]{:S(2)}, u32[]{:S(2)}) collective-permute-start(bf16[32,1280]{1,0:T(8,128)(2,1)S(1)} %add_convert_fusion.1), channel_id=1, source_target_pairs={{0,28},{4,24},{8,20},{12,16},{16,12},{20,8},{24,4},{28,0},{1,29},{... | collective-permute-start | bytes 245768 | tf_op jit(solution)/shard_map/ppermute | solution.py:269
  28.2 8.0 %collective-permute-start.12 = (bf16[2,32,1280]{2,1,0:T(8,128)(2,1)S(1)}, bf16[2,32,1280]{2,1,0:T(8,128)(2,1)S(1)}, u32[]{:S(2)}, u32[]{:S(2)}) collective-permute-start(bf16[2,32,1280]{2,1,0:T(8,128)(2,1)S(1)} %window_mix.1), channel_id=1, source_target_pairs={{0,4},{4,8},{8,12},{12,16},{16,20},{20,24},{24,28},{28,32},{32,36}... | collective-permute-start | bytes 491528 | tf_op jit(solution)/shard_map/ppermute | solution.py:274
  30.2 6.9 %collective-permute-start.15 = (bf16[32,1280]{1,0:T(8,128)(2,1)S(1)}, bf16[32,1280]{1,0:T(8,128)(2,1)S(1)}, u32[]{:S(2)}, u32[]{:S(2)}) collective-permute-start(bf16[32,1280]{1,0:T(8,128)(2,1)S(1)} %add_convert_fusion), channel_id=1, source_target_pairs={{0,96},{32,64},{64,32},{96,0},{1,97},{33,65},{65,33},{97,1},{2,98}... | collective-permute-start | bytes 245768 | tf_op jit(solution)/shard_map/ppermute | solution.py:269
  33.0 5.7 %collective-permute-start.14 = (bf16[32,1280]{1,0:T(8,128)(2,1)S(1)}, bf16[32,1280]{1,0:T(8,128)(2,1)S(1)}, u32[]{:S(2)}, u32[]{:S(2)}) collective-permute-start(bf16[32,1280]{1,0:T(8,128)(2,1)S(1)} %add_convert_fusion), channel_id=1, source_target_pairs={{0,64},{32,96},{64,0},{96,32},{1,65},{33,97},{65,1},{97,33},{2,66}... | collective-permute-start | bytes 245768 | tf_op jit(solution)/shard_map/ppermute | solution.py:269
  33.0 5.7 %collective-permute-start.13 = (bf16[32,1280]{1,0:T(8,128)(2,1)S(1)}, bf16[32,1280]{1,0:T(8,128)(2,1)S(1)}, u32[]{:S(2)}, u32[]{:S(2)}) collective-permute-start(bf16[32,1280]{1,0:T(8,128)(2,1)S(1)} %add_convert_fusion), channel_id=1, source_target_pairs={{0,32},{32,0},{64,96},{96,64},{1,33},{33,1},{65,97},{97,65},{2,34}... | collective-permute-start | bytes 245768 | tf_op jit(solution)/shard_map/ppermute | solution.py:269
  35.4 9.1 %copy-start.1 = (bf16[1,768,1152]{2,1,0:T(8,128)(2,1)S(1)}, bf16[1,768,1152]{2,1,0:T(8,128)(2,1)}, u32[]{:S(2)}) copy-start(bf16[1,768,1152]{2,1,0:T(8,128)(2,1)} %param.5) | copy-start | bytes 5308420
  39.3 5.2 %collective-permute-start.16 = (bf16[2,32,1280]{2,1,0:T(8,128)(2,1)S(1)}, bf16[2,32,1280]{2,1,0:T(8,128)(2,1)S(1)}, u32[]{:S(2)}, u32[]{:S(2)}) collective-permute-start(bf16[2,32,1280]{2,1,0:T(8,128)(2,1)S(1)} %late_mix.1.s0_ref), channel_id=1, source_target_pairs={{0,128},{128,0},{1,129},{129,1},{2,130},{130,2},{3,131},{131,3},{4... | collective-permute-start | bytes 491528 | tf_op jit(solution)/shard_map/ppermute | solution.py:269

commit v5 on v4

--- a/solution.py
+++ b/solution.py
@@ -92,16 +92,7 @@
     )(in_hbm(keys), in_hbm(values))
 
 
-def output_kernel(
-    q0_ref, q1_ref, s0_ref, s1_ref, w_ref, out_hbm, x_buf, out_buf, out_sems
-):
-    width = out_hbm.shape[0]
-    part = width // 2
-
-    def out_copy(c):
-        rows = pl.ds(c * part, part)
-        return pltpu.make_async_copy(out_buf.at[rows], out_hbm.at[rows], out_sems.at[c])
-
+def attend(q_ref, s_ref, emit):
     head = lax.broadcasted_iota(jnp.int32, (LANES, HD), 0)
     lane = lax.broadcasted_iota(jnp.int32, (LANES, HD), 1)
     spread = (head == lane // DH).astype(jnp.bfloat16)
@@ -110,25 +101,51 @@
     own_head = (row_of == lane_of).astype(jnp.bfloat16)
     for f in range(FR):
         rows = slice(f * FT, (f + 1) * FT)
-        sums = [
-            jnp.dot(s_ref[f, :, HD:], spread, preferred_element_type=jnp.float32).astype(
-                jnp.bfloat16
-            )
-            for s_ref in (s0_ref, s1_ref)
-        ]
+        sums = jnp.dot(s_ref[f, :, HD:], spread, preferred_element_type=jnp.float32)
+        sums = sums.astype(jnp.bfloat16)
         for b in range(BLOCKS):
             columns = slice(b * LANES, (b + 1) * LANES)
-            parts = []
-            for i, (q_ref, s_ref) in enumerate(((q0_ref, s0_ref), (q1_ref, s1_ref))):
-                state = jnp.concatenate([s_ref[f, :, columns]] * HEADS_PER_BLOCK, axis=0)
-                total = jnp.concatenate([sums[i][:, columns]] * HEADS_PER_BLOCK, axis=0)
-                both = jnp.concatenate([state * own_head, total * own_head], axis=1)
-                feats = jnp.maximum(q_ref[rows, columns], 0)
-                parts.append(jnp.dot(feats, both, preferred_element_type=jnp.float32))
-            above = [part[:, :LANES] for part in parts]
-            below = [part[:, LANES:] + epsilon for part in parts]
-            mixed = (above[0] * below[1] + above[1] * below[0]) / (below[0] * below[1])
-            x_buf[rows, columns] = mixed.astype(jnp.bfloat16)
+            state = jnp.concatenate([s_ref[f, :, columns]] * HEADS_PER_BLOCK, axis=0)
+            total = jnp.concatenate([sums[:, columns]] * HEADS_PER_BLOCK, axis=0)
+            both = jnp.concatenate([state * own_head, total * own_head], axis=1)
+            feats = jnp.maximum(q_ref[rows, columns], 0)
+            part = jnp.dot(feats, both, preferred_element_type=jnp.float32)
+            emit(rows, columns, part[:, :LANES] / (part[:, LANES:] + epsilon))
+
+
+def own_kernel(q_ref, s_ref, own_ref):
+    def emit(rows, columns, attended):
+        own_ref[rows, columns] = attended
+
+    attend(q_ref, s_ref, emit)
+
+
+def own_branch(queries, states):
+    return pl.pallas_call(
+        own_kernel,
+        out_shape=jax.ShapeDtypeStruct((ROWS, HD), jnp.float32),
+        in_specs=[pl.BlockSpec(memory_space=pltpu.VMEM)] * 2,
+        out_specs=pl.BlockSpec(memory_space=pltpu.VMEM),
+        compiler_params=pltpu.CompilerParams(vmem_limit_bytes=VMEM_LIMIT),
+        cost_estimate=pl.CostEstimate(
+            flops=4 * ROWS * HD * LANES, bytes_accessed=6 * ROWS * HD, transcendentals=0
+        ),
+        name="own_branch",
+    )(queries, states)
+
+
+def output_kernel(own_ref, q_ref, s_ref, w_ref, out_hbm, x_buf, out_buf, out_sems):
+    width = out_hbm.shape[0]
+    part = width // 2
+
+    def out_copy(c):
+        rows = pl.ds(c * part, part)
+        return pltpu.make_async_copy(out_buf.at[rows], out_hbm.at[rows], out_sems.at[c])
+
+    def emit(rows, columns, attended):
+        x_buf[rows, columns] = (own_ref[rows, columns] + attended).astype(jnp.bfloat16)
+
+    attend(q_ref, s_ref, emit)
     for c in range(2):
         rows = slice(c * part, (c + 1) * part)
         out_buf[rows, :] = lax.dot_general(
@@ -163,14 +180,14 @@
     )(in_hbm(weight))
 
 
-def guided_columns(own_queries, other_queries, own_states, other_states, weight):
+def guided_columns(own, other_queries, other_states, weight):
     width = weight.shape[0]
     hbm = pl.BlockSpec(memory_space=pltpu.HBM)
     vmem = pl.BlockSpec(memory_space=pltpu.VMEM)
     return pl.pallas_call(
         output_kernel,
         out_shape=jax.ShapeDtypeStruct((width, ROWS), jnp.bfloat16),
-        in_specs=[vmem] * 5,
+        in_specs=[vmem] * 4,
         out_specs=hbm,
         scratch_shapes=[
             pltpu.VMEM((ROWS, HD), jnp.bfloat16),
@@ -184,7 +201,7 @@
             transcendentals=0,
         ),
         name="guided_columns",
-    )(own_queries, other_queries, own_states, other_states, weight)
+    )(own, other_queries, other_states, weight)
 
 
 def comes_before(axis, mask):
@@ -307,9 +324,8 @@
     base, half_weight = lax.optimization_barrier((base, half_weight))
     own_states = small_call(late_kernel, jnp.bfloat16, "late_mix", first_frame, base, *parts_y)
     other_states = exchanged(own_states, "cfg", 1)
-    return guided_columns(
-        own_queries, other_queries, own_states, other_states, half_weight
-    ).T
+    own = own_branch(own_queries, own_states)
+    return guided_columns(own, other_queries, other_states, half_weight).T
 
 
 def solution(mesh):

time: 50.2 us -> 49.6 us (0.988)
  waiting for transfers between devices: 5.91 us -> 4.88 us
    pallas_call x0 -> x1, Pallas kernels: none -> 1.33 us  [own_branch(): pl.pallas_call(own_kernel, out_shape=jax.ShapeDtypeStruct((ROWS, HD), jnp...]
    ppermute x15, waiting for transfers between devices: 4.4 us -> 3.37 us  [exchanged(): return lax.ppermute(value, axis, pairs)]
    pallas_call x1, Pallas kernels: 5.47 us -> 4.51 us  [guided_columns(): pl.pallas_call(output_kernel, out_shape=jax.ShapeDtypeStruct((width, ROWS...]
  transfers between devices with their start and end apart: 17 -> 17, of which waited for: 5 -> 4; matrix products, arithmetic and copies ran while one was open for 0% -> 0% of each run, Pallas kernels for 12% -> 15%
where the time goes in v5:
time: 49.6 us; the launch traced here: 49.4 us
  starting transfers between devices  31.7 us (64%)
  Pallas kernels  12.5 us (25%)
  waiting for transfers between devices  4.88 us (10%)
    ppermute x15, starting transfers between devices, exchanged(): return lax.ppermute(value, axis, pairs)  25.3 us
    ppermute x2, starting transfers between devices, shifted(): lax.ppermute(value, axis, [(i, (i + steps) % count) for i in range(count)])  6.38 us
    pallas_call x1, Pallas kernels, guided_columns(): pl.pallas_call(output_kernel, out_shape=jax.ShapeDtypeStruct((width, ROWS...  4.51 us
    ppermute x15, waiting for transfers between devices, exchanged(): return lax.ppermute(value, axis, pairs)  3.37 us
    pallas_call x1, Pallas kernels, frame_states(): pl.pallas_call(state_kernel, out_shape=(jax.ShapeDtypeStruct((FR, DH, PAC...  2.54 us
    pallas_call x3, Pallas kernels, small_call(): pl.pallas_call(kernel, out_shape=jax.ShapeDtypeStruct((FR, DH, PACKED), d...  2.39 us
    pallas_call x1, Pallas kernels, fetched(): pl.pallas_call(fetch_kernel, out_shape=jax.ShapeDtypeStruct((width, weigh...  1.74 us
    ppermute x2, waiting for transfers between devices, shifted(): lax.ppermute(value, axis, [(i, (i + steps) % count) for i in range(count)])  1.5 us
  transfers between devices with their start and end apart: 17, of which 4 were waited for; matrix products, arithmetic and copies ran while one was open for 0% of the time, Pallas kernels for 15%

profile of v5, /device:TPU:1, one launch (start us, length us, event | category | flops | bytes accessed | tf_op | source)
XLA Modules:
  0.0 49.4 jit_solution(3617926896431720470)
XLA Ops:
  0.0 3.2 %collective-permute-start.3 = (bf16[768,1152]{1,0:T(8,128)(2,1)}, bf16[768,1152]{1,0:T(8,128)(2,1)S(1)}, u32[]{:S(2)}, u32[]{:S(2)}) collective-permute-start(bf16[768,1152]{1,0:T(8,128)(2,1)} %bitcast.5), channel_id=1, source_target_pairs={{0,128},{128,0},{1,129},{129,1},{2,130},{130,2},{3,131},{131,3},{4... | collective-permute-start | bytes 5308424 | tf_op jit(solution)/shard_map/ppermute | solution.py:286
  3.2 2.5 %frame_states.1 = (f32[2,32,1280]{2,1,0:T(8,128)S(1)}, bf16[32,1280]{1,0:T(8,128)(2,1)S(1)}, bf16[32,1280]{1,0:T(8,128)(2,1)S(1)}) custom-call(bf16[768,1152]{1,0:T(8,128)(2,1)} %bitcast.8, bf16[768,1152]{1,0:T(8,128)(2,1)} %bitcast.9), custom_call_target="tpu_custom_call" | custom-call | flops 452984832 | bytes 3538944 | tf_op jit(solution)/shard_map/frame_states/pallas_call | solution.py:73
  5.8 0.8 %collective-permute-start.2 = (bf16[32,1280]{1,0:T(8,128)(2,1)S(1)}, bf16[32,1280]{1,0:T(8,128)(2,1)S(1)}, u32[]{:S(2)}, u32[]{:S(2)}) collective-permute-start(bf16[32,1280]{1,0:T(8,128)(2,1)S(1)} %get-tuple-element.15), channel_id=1, source_target_pairs={{0,3},{1,2},{2,1},{3,0},{4,7},{5,6},{6,5},{7,4},{8,11},{9,10},{10,... | collective-permute-start | bytes 245768 | tf_op jit(solution)/shard_map/ppermute | solution.py:286
  6.6 0.5 %collective-permute-start.1 = (bf16[32,1280]{1,0:T(8,128)(2,1)S(1)}, bf16[32,1280]{1,0:T(8,128)(2,1)S(1)}, u32[]{:S(2)}, u32[]{:S(2)}) collective-permute-start(bf16[32,1280]{1,0:T(8,128)(2,1)S(1)} %get-tuple-element.15), channel_id=1, source_target_pairs={{0,2},{1,3},{2,0},{3,1},{4,6},{5,7},{6,4},{7,5},{8,10},{9,11},{10,... | collective-permute-start | bytes 245768 | tf_op jit(solution)/shard_map/ppermute | solution.py:286
  7.1 2.0 %collective-permute-start = (bf16[32,1280]{1,0:T(8,128)(2,1)S(1)}, bf16[32,1280]{1,0:T(8,128)(2,1)S(1)}, u32[]{:S(2)}, u32[]{:S(2)}) collective-permute-start(bf16[32,1280]{1,0:T(8,128)(2,1)S(1)} %get-tuple-element.15), channel_id=1, source_target_pairs={{0,1},{1,0},{2,3},{3,2},{4,5},{5,4},{6,7},{7,6},{8,9},{9,8},{10,11... | collective-permute-start | bytes 245768 | tf_op jit(solution)/shard_map/ppermute | solution.py:286
  9.1 6.3 %collective-permute-start.4 = (s32[2]{0:T(128)S(1)}, s32[2]{0:T(128)S(1)}, u32[]{:S(2)}, u32[]{:S(2)}) collective-permute-start(s32[2]{0:T(128)S(1)} %copy-done.1), channel_id=1, source_target_pairs={{0,124},{4,0},{8,4},{12,8},{16,12},{20,16},{24,20},{28,24},{32,28}... | collective-permute-start | bytes 32 | tf_op jit(solution)/shard_map/ppermute | solution.py:291
  15.5 0.7 %collective-permute-done.4.first_ref = s32[2]{0:T(128)S(1)} collective-permute-done((s32[2]{0:T(128)S(1)}, s32[2]{0:T(128)S(1)}, u32[]{:S(2)}, u32[]{:S(2)}) %collective-permute-start.4) | collective-permute-done | bytes 40 | tf_op jit(solution)/shard_map/ppermute | solution.py:291
  16.4 3.3 %collective-permute-start.5 = (bf16[32,1280]{1,0:T(8,128)(2,1)S(1)}, bf16[32,1280]{1,0:T(8,128)(2,1)S(1)}, u32[]{:S(2)}, u32[]{:S(2)}) collective-permute-start(bf16[32,1280]{1,0:T(8,128)(2,1)S(1)} %add_convert_fusion.2), channel_id=1, source_target_pairs={{0,4},{4,0},{8,12},{12,8},{16,20},{20,16},{24,28},{28,24},{1,5},{5... | collective-permute-start | bytes 245768 | tf_op jit(solution)/shard_map/ppermute | solution.py:286
  19.7 2.5 %collective-permute-start.11 = (bf16[32,1280]{1,0:T(8,128)(2,1)S(1)}, bf16[32,1280]{1,0:T(8,128)(2,1)S(1)}, u32[]{:S(2)}, u32[]{:S(2)}) collective-permute-start(bf16[32,1280]{1,0:T(8,128)(2,1)S(1)} %get-tuple-element.17), channel_id=1, source_target_pairs={{0,3},{1,2},{2,1},{3,0},{4,7},{5,6},{6,5},{7,4},{8,11},{9,10},{10,... | collective-permute-start | bytes 245768 | tf_op jit(solution)/shard_map/ppermute | solution.py:286
  22.2 0.5 %collective-permute-start.10 = (bf16[32,1280]{1,0:T(8,128)(2,1)S(1)}, bf16[32,1280]{1,0:T(8,128)(2,1)S(1)}, u32[]{:S(2)}, u32[]{:S(2)}) collective-permute-start(bf16[32,1280]{1,0:T(8,128)(2,1)S(1)} %get-tuple-element.17), channel_id=1, source_target_pairs={{0,2},{1,3},{2,0},{3,1},{4,6},{5,7},{6,4},{7,5},{8,10},{9,11},{10,... | collective-permute-start | bytes 245768 | tf_op jit(solution)/shard_map/ppermute | solution.py:286
  22.7 0.3 collective-permute-start.9
  23.0 4.4 %collective-permute-start.8 = (bf16[32,1280]{1,0:T(8,128)(2,1)S(1)}, bf16[32,1280]{1,0:T(8,128)(2,1)S(1)}, u32[]{:S(2)}, u32[]{:S(2)}) collective-permute-start(bf16[32,1280]{1,0:T(8,128)(2,1)S(1)} %add_convert_fusion.1), channel_id=1, source_target_pairs={{0,28},{4,24},{8,20},{12,16},{16,12},{20,8},{24,4},{28,0},{1,29},{... | collective-permute-start | bytes 245768 | tf_op jit(solution)/shard_map/ppermute | solution.py:286
  27.4 0.8 %window_mix.1 = bf16[2,32,1280]{2,1,0:T(8,128)(2,1)S(1)} custom-call(s32[2]{0:T(128)S(1)} %collective-permute-done.4.first_ref, bf16[32,1280]{1,0:T(8,128)(2,1)S(1)} %collective-permute-done.total1.refs_4_, bf16[32,1280]{1,0:T(8,128)(2,1)S(1)} %collective-permute-done.1.total2.refs_5_, bf16[32,1280]{1,0:T(8,128)(2,1)S(1)} %collective-permute-done.2.total3.refs_6_, ...), custom_call_target="tpu_custom_call" | custom-call | flops 1146880 | bytes 1146880 | tf_op jit(solution)/shard_map/window_mix/pallas_call | solution.py:268
  28.3 1.9 %collective-permute-done.8.refs_3_ = bf16[32,1280]{1,0:T(8,128)(2,1)S(1)} collective-permute-done((bf16[32,1280]{1,0:T(8,128)(2,1)S(1)}, bf16[32,1280]{1,0:T(8,128)(2,1)S(1)}, u32[]{:S(2)}, u32[]{:S(2)}) %collective-permute-start.8) | collective-permute-done | bytes 81952 | tf_op jit(solution)/shard_map/ppermute | solution.py:286
  30.2 2.7 %collective-permute-start.15 = (bf16[32,1280]{1,0:T(8,128)(2,1)S(1)}, bf16[32,1280]{1,0:T(8,128)(2,1)S(1)}, u32[]{:S(2)}, u32[]{:S(2)}) collective-permute-start(bf16[32,1280]{1,0:T(8,128)(2,1)S(1)} %add_convert_fusion), channel_id=1, source_target_pairs={{0,96},{32,64},{64,32},{96,0},{1,97},{33,65},{65,33},{97,1},{2,98}... | collective-permute-start | bytes 245768 | tf_op jit(solution)/shard_map/ppermute | solution.py:286
  33.0 0.7 %collective-permute-start.13 = (bf16[32,1280]{1,0:T(8,128)(2,1)S(1)}, bf16[32,1280]{1,0:T(8,128)(2,1)S(1)}, u32[]{:S(2)}, u32[]{:S(2)}) collective-permute-start(bf16[32,1280]{1,0:T(8,128)(2,1)S(1)} %add_convert_fusion), channel_id=1, source_target_pairs={{0,32},{32,0},{64,96},{96,64},{1,33},{33,1},{65,97},{97,65},{2,34}... | collective-permute-start | bytes 245768 | tf_op jit(solution)/shard_map/ppermute | solution.py:286
  33.6 1.7 %fetch.1.w_ref = bf16[1120,1152]{1,0:T(8,128)(2,1)S(1)} custom-call(bf16[2240,1152]{1,0:T(8,128)(2,1)} %bitcast.7), custom_call_target="tpu_custom_call" | custom-call | bytes 5160960 | tf_op jit(solution)/shard_map/fetch/pallas_call | solution.py:169
  35.4 0.8 %collective-permute-done.12.refs_10_ = bf16[2,32,1280]{2,1,0:T(8,128)(2,1)S(1)} collective-permute-done((bf16[2,32,1280]{2,1,0:T(8,128)(2,1)S(1)}, bf16[2,32,1280]{2,1,0:T(8,128)(2,1)S(1)}, u32[]{:S(2)}, u32[]{:S(2)}) %collective-permute-start.12) | collective-permute-done | bytes 163872 | tf_op jit(solution)/shard_map/ppermute | solution.py:291
  36.2 0.9 %early_mix.1.base_ref = f32[2,32,1280]{2,1,0:T(8,128)S(1)} custom-call(s32[2]{0:T(128)S(1)} %copy-done.1, bf16[32,1280]{1,0:T(8,128)(2,1)S(1)} %collective-permute-done.5.refs_0_, bf16[32,1280]{1,0:T(8,128)(2,1)S(1)} %collective-permute-done.6.refs_1_, bf16[32,1280]{1,0:T(8,128)(2,1)S(1)} %collective-permute-done.7.refs_2_, ...), custom_call_target="tpu_custom_call" | custom-call | flops 1966080 | bytes 1966080 | tf_op jit(solution)/shard_map/early_mix/pallas_call | solution.py:268
  37.2 1.4 %collective-permute-done.14.refs_1_ = bf16[32,1280]{1,0:T(8,128)(2,1)S(1)} collective-permute-done((bf16[32,1280]{1,0:T(8,128)(2,1)S(1)}, bf16[32,1280]{1,0:T(8,128)(2,1)S(1)}, u32[]{:S(2)}, u32[]{:S(2)}) %collective-permute-start.14) | collective-permute-done | bytes 81952 | tf_op jit(solution)/shard_map/ppermute | solution.py:286
  38.6 0.6 %late_mix.1.s_ref = bf16[2,32,1280]{2,1,0:T(8,128)(2,1)S(1)} custom-call(s32[2]{0:T(128)S(1)} %copy-done.1, f32[2,32,1280]{2,1,0:T(8,128)S(1)} %early_mix.1.base_ref, bf16[32,1280]{1,0:T(8,128)(2,1)S(1)} %collective-permute-done.13.refs_0_, bf16[32,1280]{1,0:T(8,128)(2,1)S(1)} %collective-permute-done.14.refs_1_, ...), custom_call_target="tpu_custom_call" | custom-call | flops 655360 | bytes 655360 | tf_op jit(solution)/shard_map/late_mix/pallas_call | solution.py:268
  39.3 4.2 %collective-permute-start.16 = (bf16[2,32,1280]{2,1,0:T(8,128)(2,1)S(1)}, bf16[2,32,1280]{2,1,0:T(8,128)(2,1)S(1)}, u32[]{:S(2)}, u32[]{:S(2)}) collective-permute-start(bf16[2,32,1280]{2,1,0:T(8,128)(2,1)S(1)} %late_mix.1.s_ref), channel_id=1, source_target_pairs={{0,128},{128,0},{1,129},{129,1},{2,130},{130,2},{3,131},{131,3},{4... | collective-permute-start | bytes 491528 | tf_op jit(solution)/shard_map/ppermute | solution.py:286
  43.4 1.3 %own_branch.1.own_ref = f32[768,1152]{1,0:T(8,128)S(1)} custom-call(bf16[768,1152]{1,0:T(8,128)(2,1)S(1)} %bitcast.6, bf16[2,32,1280]{2,1,0:T(8,128)(2,1)S(1)} %late_mix.1.s_ref), custom_call_target="tpu_custom_call" | custom-call | flops 452984832 | bytes 5308416 | tf_op jit(solution)/shard_map/own_branch/pallas_call | solution.py:124
  44.8 4.5 %guided_columns.1 = bf16[1120,768]{1,0:T(8,128)(2,1)} custom-call(f32[768,1152]{1,0:T(8,128)S(1)} %own_branch.1.own_ref, bf16[768,1152]{1,0:T(8,128)(2,1)S(1)} %collective-permute-done.3.q_ref, bf16[2,32,1280]{2,1,0:T(8,128)(2,1)S(1)} %collective-permute-done.16.s_ref, bf16[1120,1152]{1,0:T(8,128)(2,1)S(1)} %fetch.1.w_ref), custom_call_target="tpu_custom_call" | custom-call | flops 2887778304 | bytes 7839744 | tf_op jit(solution)/shard_map/guided_columns/pallas_call | solution.py:187
  (24 shorter events, 0.5 us)
Async XLA Ops:
  0.0 16.2 %collective-permute-start.3 = (bf16[768,1152]{1,0:T(8,128)(2,1)}, bf16[768,1152]{1,0:T(8,128)(2,1)S(1)}, u32[]{:S(2)}, u32[]{:S(2)}) collective-permute-start(bf16[768,1152]{1,0:T(8,128)(2,1)} %bitcast.5), channel_id=1, source_target_pairs={{0,128},{128,0},{1,129},{129,1},{2,130},{130,2},{3,131},{131,3},{4... | collective-permute-start | bytes 5308424 | tf_op jit(solution)/shard_map/ppermute | solution.py:286
  3.2 5.9 %copy-start.1 = (s32[2]{0:T(128)S(1)}, s32[2]{0:T(128)}, u32[]{:S(2)}) copy-start(s32[2]{0:T(128)} %first_ref.3) | copy-start | bytes 28
  5.8 9.6 %collective-permute-start.2 = (bf16[32,1280]{1,0:T(8,128)(2,1)S(1)}, bf16[32,1280]{1,0:T(8,128)(2,1)S(1)}, u32[]{:S(2)}, u32[]{:S(2)}) collective-permute-start(bf16[32,1280]{1,0:T(8,128)(2,1)S(1)} %get-tuple-element.15), channel_id=1, source_target_pairs={{0,3},{1,2},{2,1},{3,0},{4,7},{5,6},{6,5},{7,4},{8,11},{9,10},{10,... | collective-permute-start | bytes 245768 | tf_op jit(solution)/shard_map/ppermute | solution.py:286
  6.6 8.8 %collective-permute-start.1 = (bf16[32,1280]{1,0:T(8,128)(2,1)S(1)}, bf16[32,1280]{1,0:T(8,128)(2,1)S(1)}, u32[]{:S(2)}, u32[]{:S(2)}) collective-permute-start(bf16[32,1280]{1,0:T(8,128)(2,1)S(1)} %get-tuple-element.15), channel_id=1, source_target_pairs={{0,2},{1,3},{2,0},{3,1},{4,6},{5,7},{6,4},{7,5},{8,10},{9,11},{10,... | collective-permute-start | bytes 245768 | tf_op jit(solution)/shard_map/ppermute | solution.py:286
  7.1 8.3 %collective-permute-start = (bf16[32,1280]{1,0:T(8,128)(2,1)S(1)}, bf16[32,1280]{1,0:T(8,128)(2,1)S(1)}, u32[]{:S(2)}, u32[]{:S(2)}) collective-permute-start(bf16[32,1280]{1,0:T(8,128)(2,1)S(1)} %get-tuple-element.15), channel_id=1, source_target_pairs={{0,1},{1,0},{2,3},{3,2},{4,5},{5,4},{6,7},{7,6},{8,9},{9,8},{10,11... | collective-permute-start | bytes 245768 | tf_op jit(solution)/shard_map/ppermute | solution.py:286
  9.1 7.0 %collective-permute-start.4 = (s32[2]{0:T(128)S(1)}, s32[2]{0:T(128)S(1)}, u32[]{:S(2)}, u32[]{:S(2)}) collective-permute-start(s32[2]{0:T(128)S(1)} %copy-done.1), channel_id=1, source_target_pairs={{0,124},{4,0},{8,4},{12,8},{16,12},{20,16},{24,20},{28,24},{32,28}... | collective-permute-start | bytes 32 | tf_op jit(solution)/shard_map/ppermute | solution.py:291
  16.2 6.5 %collective-permute-start.7 = (bf16[32,1280]{1,0:T(8,128)(2,1)S(1)}, bf16[32,1280]{1,0:T(8,128)(2,1)S(1)}, u32[]{:S(2)}, u32[]{:S(2)}) collective-permute-start(bf16[32,1280]{1,0:T(8,128)(2,1)S(1)} %add_convert_fusion.2), channel_id=1, source_target_pairs={{0,12},{4,8},{8,4},{12,0},{16,28},{20,24},{24,20},{28,16},{1,13},{... | collective-permute-start | bytes 245768 | tf_op jit(solution)/shard_map/ppermute | solution.py:286
  16.4 6.6 %collective-permute-start.6 = (bf16[32,1280]{1,0:T(8,128)(2,1)S(1)}, bf16[32,1280]{1,0:T(8,128)(2,1)S(1)}, u32[]{:S(2)}, u32[]{:S(2)}) collective-permute-start(bf16[32,1280]{1,0:T(8,128)(2,1)S(1)} %add_convert_fusion.2), channel_id=1, source_target_pairs={{0,8},{4,12},{8,0},{12,4},{16,24},{20,28},{24,16},{28,20},{1,9},{5... | collective-permute-start | bytes 245768 | tf_op jit(solution)/shard_map/ppermute | solution.py:286
  16.4 6.6 %collective-permute-start.5 = (bf16[32,1280]{1,0:T(8,128)(2,1)S(1)}, bf16[32,1280]{1,0:T(8,128)(2,1)S(1)}, u32[]{:S(2)}, u32[]{:S(2)}) collective-permute-start(bf16[32,1280]{1,0:T(8,128)(2,1)S(1)} %add_convert_fusion.2), channel_id=1, source_target_pairs={{0,4},{4,0},{8,12},{12,8},{16,20},{20,16},{24,28},{28,24},{1,5},{5... | collective-permute-start | bytes 245768 | tf_op jit(solution)/shard_map/ppermute | solution.py:286
  19.7 7.7 %collective-permute-start.11 = (bf16[32,1280]{1,0:T(8,128)(2,1)S(1)}, bf16[32,1280]{1,0:T(8,128)(2,1)S(1)}, u32[]{:S(2)}, u32[]{:S(2)}) collective-permute-start(bf16[32,1280]{1,0:T(8,128)(2,1)S(1)} %get-tuple-element.17), channel_id=1, source_target_pairs={{0,3},{1,2},{2,1},{3,0},{4,7},{5,6},{6,5},{7,4},{8,11},{9,10},{10,... | collective-permute-start | bytes 245768 | tf_op jit(solution)/shard_map/ppermute | solution.py:286
  22.2 5.2 %collective-permute-start.10 = (bf16[32,1280]{1,0:T(8,128)(2,1)S(1)}, bf16[32,1280]{1,0:T(8,128)(2,1)S(1)}, u32[]{:S(2)}, u32[]{:S(2)}) collective-permute-start(bf16[32,1280]{1,0:T(8,128)(2,1)S(1)} %get-tuple-element.17), channel_id=1, source_target_pairs={{0,2},{1,3},{2,0},{3,1},{4,6},{5,7},{6,4},{7,5},{8,10},{9,11},{10,... | collective-permute-start | bytes 245768 | tf_op jit(solution)/shard_map/ppermute | solution.py:286
  22.7 4.7 %collective-permute-start.9 = (bf16[32,1280]{1,0:T(8,128)(2,1)S(1)}, bf16[32,1280]{1,0:T(8,128)(2,1)S(1)}, u32[]{:S(2)}, u32[]{:S(2)}) collective-permute-start(bf16[32,1280]{1,0:T(8,128)(2,1)S(1)} %get-tuple-element.17), channel_id=1, source_target_pairs={{0,1},{1,0},{2,3},{3,2},{4,5},{5,4},{6,7},{7,6},{8,9},{9,8},{10,11... | collective-permute-start | bytes 245768 | tf_op jit(solution)/shard_map/ppermute | solution.py:286
  23.0 7.2 %collective-permute-start.8 = (bf16[32,1280]{1,0:T(8,128)(2,1)S(1)}, bf16[32,1280]{1,0:T(8,128)(2,1)S(1)}, u32[]{:S(2)}, u32[]{:S(2)}) collective-permute-start(bf16[32,1280]{1,0:T(8,128)(2,1)S(1)} %add_convert_fusion.1), channel_id=1, source_target_pairs={{0,28},{4,24},{8,20},{12,16},{16,12},{20,8},{24,4},{28,0},{1,29},{... | collective-permute-start | bytes 245768 | tf_op jit(solution)/shard_map/ppermute | solution.py:286
  28.2 8.0 %collective-permute-start.12 = (bf16[2,32,1280]{2,1,0:T(8,128)(2,1)S(1)}, bf16[2,32,1280]{2,1,0:T(8,128)(2,1)S(1)}, u32[]{:S(2)}, u32[]{:S(2)}) collective-permute-start(bf16[2,32,1280]{2,1,0:T(8,128)(2,1)S(1)} %window_mix.1), channel_id=1, source_target_pairs={{0,4},{4,8},{8,12},{12,16},{16,20},{20,24},{24,28},{28,32},{32,36}... | collective-permute-start | bytes 491528 | tf_op jit(solution)/shard_map/ppermute | solution.py:291
  30.2 6.9 %collective-permute-start.15 = (bf16[32,1280]{1,0:T(8,128)(2,1)S(1)}, bf16[32,1280]{1,0:T(8,128)(2,1)S(1)}, u32[]{:S(2)}, u32[]{:S(2)}) collective-permute-start(bf16[32,1280]{1,0:T(8,128)(2,1)S(1)} %add_convert_fusion), channel_id=1, source_target_pairs={{0,96},{32,64},{64,32},{96,0},{1,97},{33,65},{65,33},{97,1},{2,98}... | collective-permute-start | bytes 245768 | tf_op jit(solution)/shard_map/ppermute | solution.py:286
  33.0 5.7 %collective-permute-start.14 = (bf16[32,1280]{1,0:T(8,128)(2,1)S(1)}, bf16[32,1280]{1,0:T(8,128)(2,1)S(1)}, u32[]{:S(2)}, u32[]{:S(2)}) collective-permute-start(bf16[32,1280]{1,0:T(8,128)(2,1)S(1)} %add_convert_fusion), channel_id=1, source_target_pairs={{0,64},{32,96},{64,0},{96,32},{1,65},{33,97},{65,1},{97,33},{2,66}... | collective-permute-start | bytes 245768 | tf_op jit(solution)/shard_map/ppermute | solution.py:286
  33.0 5.7 %collective-permute-start.13 = (bf16[32,1280]{1,0:T(8,128)(2,1)S(1)}, bf16[32,1280]{1,0:T(8,128)(2,1)S(1)}, u32[]{:S(2)}, u32[]{:S(2)}) collective-permute-start(bf16[32,1280]{1,0:T(8,128)(2,1)S(1)} %add_convert_fusion), channel_id=1, source_target_pairs={{0,32},{32,0},{64,96},{96,64},{1,33},{33,1},{65,97},{97,65},{2,34}... | collective-permute-start | bytes 245768 | tf_op jit(solution)/shard_map/ppermute | solution.py:286
  35.4 8.0 %copy-start = (bf16[1,768,1152]{2,1,0:T(8,128)(2,1)S(1)}, bf16[1,768,1152]{2,1,0:T(8,128)(2,1)}, u32[]{:S(2)}) copy-start(bf16[1,768,1152]{2,1,0:T(8,128)(2,1)} %param.5) | copy-start | bytes 5308420
  39.3 5.5 %collective-permute-start.16 = (bf16[2,32,1280]{2,1,0:T(8,128)(2,1)S(1)}, bf16[2,32,1280]{2,1,0:T(8,128)(2,1)S(1)}, u32[]{:S(2)}, u32[]{:S(2)}) collective-permute-start(bf16[2,32,1280]{2,1,0:T(8,128)(2,1)S(1)} %late_mix.1.s_ref), channel_id=1, source_target_pairs={{0,128},{128,0},{1,129},{129,1},{2,130},{130,2},{3,131},{131,3},{4... | collective-permute-start | bytes 491528 | tf_op jit(solution)/shard_map/ppermute | solution.py:286
